TPU v7x, 128 devices: a whole 4x4x4 slice. The times are simulated.
128 devices in a mesh: solver: 4 (over z_lo, core), space: 32 (over z_hi, y, x).
Axes of the slice: x: 4, y: 4, z: 4 (z_hi: 2, z_lo: 2; z = z_hi * 2 + z_lo), core: 2. Of those that a mesh axis runs over, the one named last changes fastest.
Arguments:
- flow_state: float32 [5, 128, 128, 512], P(None, 'space', None, 'solver')
- acoustic_state: bfloat16 [4, 28672, 512], P(None, ('solver', 'space')), may hold values from -6 to 6
- deriv_x: bfloat16 [512, 512], replicated, may hold values from -0.25 to 0.25
- deriv_y: bfloat16 [512, 512], replicated, may hold values from -0.25 to 0.25
- deriv_z: bfloat16 [512, 512], replicated, may hold values from -0.25 to 0.25
- requests: int32 [128, 128, 4], P(('solver', 'space')), may hold values from 0 to 15, as said below
- elem_slot: int32 [28672], P(('solver', 'space')), may hold values from 0 to 511, as said below
- neighbours: int32 [6, 28672], P(None, ('solver', 'space')), may hold values from 0 to 28671, as said below
Outputs:
- flow_increment: float32 [5, 128, 128, 512], P(None, 'space', None, 'solver')
- acoustic_increment: float32 [4, 28672, 512], P(None, ('solver', 'space'))
Inputs may be any that keep to these rules, and one draw needn't show every extreme that they name: requests[r, o, c] names one of the 16 blocks of device o. `elem_slot`: the 224 elements of a device name distinct slots; from a quarter of the devices (the same for every requester) all 4 slots are named, from each other device the first 1; other slots are named by no element. `neighbours`: for faces 2 to 5 the neighbour lies on the element's own device; for face 0 on its own device or the one of next lower space index in the same solver group, cyclically; for face 1 on its own or the next higher.
All inputs are finite; a program needn't handle non-finite values.
Results may differ from a plain program's by a relative error of at most 0.0003.
The roundings to bfloat16 on the way count: a program that leaves them out, or rounds other values in their place, can miss the bound.
Values may be sent and summed in bfloat16 or wider, within the bound.
No kernel may reach another device: no remote copies, remote signals or barrier semaphores. Data moves between devices by JAX's collectives and lax.ppermute only.
A program may use at most 128 MiB of HBM per device.

v0:
```python
import jax
import jax.numpy as jnp
from jax import lax
from jax.experimental import pallas as pl
from jax.experimental.pallas import tpu as pltpu
from jax.sharding import PartitionSpec as P

F32 = jnp.float32
BF16 = jnp.bfloat16
I32 = jnp.int32

EL = 224
NODES = 512
FLOW_STEP = 0.2
SOUND_STEP = 0.2
VMEM_LIMIT = 40 * 1024 * 1024


def iota(shape, dim):
    return lax.broadcasted_iota(I32, shape, dim)


def full(*shape):
    return jax.ShapeDtypeStruct(shape, F32)


def half(*shape):
    return jax.ShapeDtypeStruct(shape, BF16)


def call(body, outs, name, args, scratch=(), aliases=None, in_specs=None, out_specs=None):
    vmem = pl.BlockSpec(memory_space=pltpu.VMEM)
    many = isinstance(outs, (list, tuple))
    return pl.pallas_call(
        body,
        out_shape=outs,
        in_specs=in_specs or [vmem] * len(args),
        out_specs=out_specs or ([vmem] * len(outs) if many else vmem),
        scratch_shapes=list(scratch),
        name=name,
        input_output_aliases=aliases or {},
        compiler_params=pltpu.CompilerParams(vmem_limit_bytes=VMEM_LIMIT),
    )(*args)


def primitives(rows):
    inv = 1.0 / rows[0]
    v1, v2, v3 = rows[1] * inv, rows[2] * inv, rows[3] * inv
    p = 0.4 * (rows[4] - 0.5 * (rows[1] * v1 + rows[2] * v2 + rows[3] * v3))
    return (v1, v2, v3), p


def flux(rows, v, p, k):
    along = v[k]
    out = [rows[1 + k]]
    for c in range(3):
        t = rows[1 + c] * along
        out.append(t + p if c == k else t)
    out.append((rows[4] + p) * along)
    return out


def roll_y(f, step):
    return pltpu.roll(f, step % f.shape[0], 0)


def roll_z(f, step):
    return pltpu.roll(f, step % f.shape[1], 1)


def put_lane(acc, lane, f, source, target):
    return jnp.where(lane == target, roll_z(f, target - source), acc)


def diff_y(f):
    return roll_y(f, -1) - roll_y(f, 1)


def diff_z(f, lane, below, above, slot):
    up = jnp.where(lane == 127, roll_z(above, 127 - slot), roll_z(f, -1))
    down = jnp.where(lane == 0, roll_z(below, -slot), roll_z(f, 1))
    return up - down


def pack_z(planes, lo_ref, hi_ref):
    lane = iota((128, 128), 1)
    lo = jnp.zeros((128, 128), F32)
    hi = jnp.zeros((128, 128), F32)
    for x in range(4):
        for f, field in enumerate(planes(x)):
            slot = f * 4 + x
            lo = put_lane(lo, lane, field, 0, slot)
            hi = put_lane(hi, lane, field, 127, slot)
    lo_ref[...] = lo
    hi_ref[...] = hi


def pair_lanes(tiles, upper):
    lane = iota((EL, 128), 1)
    out = []
    for w in range(2):
        a, b = tiles[2 * w], tiles[2 * w + 1]
        if upper:
            out.append(jnp.where(lane < 64, pltpu.roll(a, 64, 1), b))
        else:
            out.append(jnp.where(lane < 64, a, pltpu.roll(b, 64, 1)))
    return out


def store_traces(first_tiles, last_tiles, lo_ref, hi_ref):
    for w, t in enumerate(pair_lanes(first_tiles, False)):
        lo_ref[w] = t.astype(BF16)
    for w, t in enumerate(pair_lanes(last_tiles, True)):
        hi_ref[w] = t.astype(BF16)


def edges_body(u, q, xlo, xhi, zlo, zhi, qlo, qhi):
    xlo[...] = u[:, 0]
    xhi[...] = u[:, 3]

    def planes(x):
        rows = [u[f, x] for f in range(5)]
        v, p = primitives(rows)
        return flux(rows, v, p, 2) + [v[0], v[1]]

    pack_z(planes, zlo, zhi)
    store_traces(
        [q[v, :, 0:128].astype(F32) for v in range(4)],
        [q[v, :, 384:512].astype(F32) for v in range(4)],
        qlo,
        qhi,
    )


def lamb_body(u, xbelow, xabove, zbelow, zabove, table, vel, pooled):
    lane = iota((128, 128), 1)
    for x in range(-1, 5):
        if x == -1:
            r, m = xbelow[0], [xbelow[c] for c in (1, 2, 3)]
        elif x == 4:
            r, m = xabove[0], [xabove[c] for c in (1, 2, 3)]
        else:
            r, m = u[0, x], [u[c, x] for c in (1, 2, 3)]
        inv = 1.0 / r
        for c in range(3):
            vel[c, x + 1] = m[c] * inv
    below, above = zbelow[...], zabove[...]
    for pair in range(2):
        total = None
        for x in (2 * pair, 2 * pair + 1):
            v1, v2, v3 = vel[0, x + 1], vel[1, x + 1], vel[2, x + 1]
            w1 = diff_y(v3) - diff_z(v2, lane, below, above, 24 + x)
            w2 = diff_z(v1, lane, below, above, 20 + x) - (vel[2, x + 2] - vel[2, x])
            w3 = (vel[1, x + 2] - vel[1, x]) - diff_y(v1)
            lamb = [w2 * v3 - w3 * v2, w3 * v1 - w1 * v3, w1 * v2 - w2 * v1]
            total = lamb if total is None else [a + b for a, b in zip(total, lamb)]
        for c in range(3):
            pooled[c * 2 + pair] = total[c]
    even, odd = [], []
    for c in range(6):
        t = pooled.at[c]
        even.append(t[pl.ds(0, 32, stride=4), :] + t[pl.ds(1, 32, stride=4), :])
        odd.append(t[pl.ds(2, 32, stride=4), :] + t[pl.ds(3, 32, stride=4), :])
    rows = jnp.concatenate([jnp.concatenate(even, 0), jnp.concatenate(odd, 0)], 1)
    z, n = iota((256, 128), 0), iota((256, 128), 1)
    pool = jnp.where((z // 128) * 64 + (z % 128) // 2 == n, 0.0625, 0.0).astype(F32)
    coarse = jnp.dot(rows, pool, preferred_element_type=F32, precision=lax.Precision.HIGHEST)
    flat = pooled.at[0]
    hold = pooled.at[1]
    flat[...] = coarse[0:128]
    hold[0:64] = coarse[128:192]
    table[...] = jnp.zeros_like(table)
    for t in range(6):
        for par in range(2):
            c, inner = t // 2, (t % 2) * 2 + par
            src = flat if c < 2 else hold
            base = (c % 2) * 64
            piece = src[pl.ds(base + inner, 16, stride=4), :]
            table[par * 16 : par * 16 + 16, t * 128 : (t + 1) * 128] = piece.astype(BF16)


def tendency_plane(x, rows_of, along_a, below, above, lane):
    rows = rows_of(x)
    v, p = primitives(rows)
    fb = flux(rows, v, p, 1)
    fc = flux(rows, v, p, 2)
    out = []
    for f in range(5):
        total = along_a(x, f) + diff_y(fb[f])
        out.append(total + diff_z(fc[f], lane, below, above, f * 4 + x))
    return rows, out


def fill_flux_a(u, xbelow, xabove, fa):
    for x in range(-1, 5):
        if x == -1:
            rows = [xbelow[f] for f in range(5)]
        elif x == 4:
            rows = [xabove[f] for f in range(5)]
        else:
            rows = [u[f, x] for f in range(5)]
        v, p = primitives(rows)
        for f, t in enumerate(flux(rows, v, p, 0)):
            fa[f, x + 1] = t


def stage_one_body(u, xbelow, xabove, zbelow, zabove, first, xlo, xhi, zlo, zhi, fa):
    lane = iota((128, 128), 1)
    fill_flux_a(u, xbelow, xabove, fa)
    below, above = zbelow[...], zabove[...]
    for x in range(4):
        rows, out = tendency_plane(
            x,
            lambda x: [u[f, x] for f in range(5)],
            lambda x, f: fa[f, x + 2] - fa[f, x],
            below,
            above,
            lane,
        )
        for f in range(5):
            first[f, x] = rows[f] - (FLOW_STEP * 0.5) * out[f]
    xlo[...] = first[:, 0]
    xhi[...] = first[:, 3]

    def planes(x):
        rows = [first[f, x] for f in range(5)]
        v, p = primitives(rows)
        return flux(rows, v, p, 2)

    pack_z(planes, zlo, zhi)


def stage_two_body(u, first, xbelow, xabove, zbelow, zabove, inc, fa):
    lane = iota((128, 128), 1)
    fill_flux_a(first, xbelow, xabove, fa)
    below, above = zbelow[...], zabove[...]
    for x in range(4):
        rows, out = tendency_plane(
            x,
            lambda x: [first[f, x] for f in range(5)],
            lambda x, f: fa[f, x + 2] - fa[f, x],
            below,
            above,
            lane,
        )
        for f in range(5):
            inc[f, x] = 0.5 * ((rows[f] - u[f, x]) - (FLOW_STEP * 0.5) * out[f])


def send_body(req, table, send):
    wanted = req[...].reshape(128, 128).astype(F32).astype(BF16)
    row, col = iota((1024, 128), 0), iota((1024, 128), 1)
    spread = jnp.where(row // 8 == col, 1.0, 0.0).astype(BF16)
    rep = jnp.dot(spread, wanted, preferred_element_type=F32)
    own = jnp.where(row % 4 == col, rep, 0.0).astype(BF16)
    value = jnp.dot(own, jnp.ones((128, 128), BF16), preferred_element_type=F32)
    target = value + ((row % 8) // 4 * 16).astype(F32)
    pick = jnp.where(col.astype(F32) == target, 1.0, 0.0).astype(BF16)
    rows = jnp.dot(pick, table[...], preferred_element_type=F32)
    for u in range(3):
        a = rows[:, 256 * u : 256 * u + 128].reshape(128, 8, 128)
        b = rows[:, 256 * u + 128 : 256 * u + 256].reshape(128, 8, 128)
        send[:, 16 * u : 16 * u + 16, :] = jnp.concatenate([a, b], 1).astype(BF16)


def gather_sources(got, pick):
    tiles = []
    for u in range(3):
        t = got[:, 16 * u : 16 * u + 16, :].astype(F32)
        tiles.append(t[:, 0:8, :].reshape(1024, 128).astype(BF16))
        tiles.append(t[:, 8:16, :].reshape(1024, 128).astype(BF16))
    rhs = jnp.concatenate(tiles, 1)
    by_parity = [jnp.dot(pick[par], rhs, preferred_element_type=F32) for par in range(2)]
    out = []
    for c in range(3):
        row = []
        for j in range(4):
            t = 2 * c + j // 2
            row.append(by_parity[j % 2][:, t * 128 : (t + 1) * 128])
        out.append(jnp.concatenate(row, 1))
    return out


def prepare_body(idx, gcat, gx0, gx1, pick, esrc, edst):
    def onehot(col, width):
        return jnp.where(iota((EL, width), 1) == idx[:, col : col + 1], 1.0, 0.0).astype(BF16)

    gx0[...] = onehot(0, 2 * EL)
    gx1[...] = onehot(1, 2 * EL)
    wide = iota((EL, 4 * EL), 1)
    acc = jnp.zeros((EL, 4 * EL), jnp.bool_)
    for f in range(4):
        acc = acc | (wide == idx[:, 2 + f : 3 + f])
    gcat[...] = jnp.where(acc, 1.0, 0.0).astype(BF16)
    pick[0] = onehot(6, 1024)
    pick[1] = onehot(7, 1024)

    def node(c, flip):
        face, a, b = c // 64, c % 64 // 8, c % 8
        low = face % 2 == (1 if flip else 0)
        spot = jnp.where(low, 0, 7)
        return jnp.where(face < 2, a * 64 + spot * 8 + b, a * 64 + b * 8 + spot)

    esrc[...] = jnp.where(
        iota((512, 256), 0) == node(iota((512, 256), 1), True), 1.0, 0.0
    ).astype(BF16)
    edst[...] = jnp.where(
        iota((256, 512), 1) == node(iota((256, 512), 0), False), 1.0, 0.0
    ).astype(BF16)


def face_count():
    n = iota((1, NODES), 1)
    count = jnp.zeros((1, NODES), I32)
    for part in (n // 64, n // 8 % 8, n % 8):
        count = count + jnp.where((part == 0) | (part == 7), 1, 0)
    return count.astype(F32)


def times(a, b):
    return lax.dot_general(a, b, (((1,), (1,)), ((), ())), preferred_element_type=F32)


def local_terms(q, dx, dy, dz, gcat, esrc, edst):
    traces = jnp.dot(jnp.concatenate(q, 0), esrc[...], preferred_element_type=F32).astype(BF16)
    wide = jnp.concatenate([traces[v * EL : (v + 1) * EL] for v in range(4)], 1)
    lane = iota((1, 1024), 1) % 256 // 64
    rhs = jnp.concatenate(
        [wide * jnp.where(lane == f, 1.0, 0.0).astype(BF16) for f in range(4)], 0
    )
    got = jnp.dot(gcat[...], rhs, preferred_element_type=F32).astype(BF16)
    count = face_count()
    out = []
    for v in range(4):
        pen = jnp.dot(got[:, v * 256 : (v + 1) * 256], edst[...], preferred_element_type=F32)
        pen = pen - count * q[v].astype(F32)
        if v == 0:
            vol = times(q[1], dx[...]) + times(q[2], dy[...]) + times(q[3], dz[...])
        else:
            vol = times(q[0], (dx, dy, dz)[v - 1][...])
        out.append(pen - vol)
    return out


def cross_terms(gx0, gx1, own_lo, own_hi, below_hi, above_lo):
    lane = iota((EL, 128), 1)
    first, last = [], []
    low = jnp.concatenate(
        [jnp.concatenate([own_hi[w], below_hi[w]], 0) for w in range(2)], 1
    )
    high = jnp.concatenate(
        [jnp.concatenate([own_lo[w], above_lo[w]], 0) for w in range(2)], 1
    )
    low = jnp.dot(gx0[...], low, preferred_element_type=F32)
    high = jnp.dot(gx1[...], high, preferred_element_type=F32)
    for v in range(4):
        w = v // 2
        a = low[:, w * 128 : (w + 1) * 128]
        b = high[:, w * 128 : (w + 1) * 128]
        if v % 2 == 0:
            b = pltpu.roll(b, 64, 1)
        else:
            a = pltpu.roll(a, 64, 1)
        first.append(jnp.where(lane < 64, a, 0.0))
        last.append(jnp.where(lane < 64, 0.0, b))
    return first, last


def sound_zero_body(q, dx, dy, dz, gcat, esrc, edst, gx0, gx1, olo, ohi, bhi, alo, part):
    rounded = [q[v] for v in range(4)]
    terms = local_terms(rounded, dx, dy, dz, gcat, esrc, edst)
    first, last = cross_terms(gx0, gx1, olo, ohi, bhi, alo)
    for v in range(4):
        full_term = jnp.concatenate(
            [
                terms[v][:, 0:128] + first[v],
                terms[v][:, 128:384],
                terms[v][:, 384:512] + last[v],
            ],
            1,
        )
        part[v] = q[v].astype(F32) + SOUND_STEP * full_term


def sources_body(got, pick, part, q1, src, lo, hi):
    s = gather_sources(got, pick)
    q1[0] = part[0]
    for c in range(3):
        src[c] = s[c].astype(BF16)
        q1[1 + c] = part[1 + c] + SOUND_STEP * s[c]
    store_traces(
        [q1[v, :, 0:128] for v in range(4)],
        [q1[v, :, 384:512] for v in range(4)],
        lo,
        hi,
    )


def sound_one_body(q0, q1, src, dx, dy, dz, gcat, esrc, edst, part):
    terms = local_terms([q1[v].astype(BF16) for v in range(4)], dx, dy, dz, gcat, esrc, edst)
    for v in range(4):
        t = terms[v] if v == 0 else terms[v] + src[v - 1].astype(F32)
        part[v] = 0.75 * q0[v].astype(F32) + 0.25 * (q1[v] + SOUND_STEP * t)


def cross_body(scale, gx0, gx1, olo, ohi, bhi, alo, part, out, lo, hi):
    first, last = cross_terms(gx0, gx1, olo, ohi, bhi, alo)
    tiles = [[], []]
    for v in range(4):
        a = part[v, :, 0:128] + scale * first[v]
        b = part[v, :, 384:512] + scale * last[v]
        out[v] = part[v]
        out[v, :, 0:128] = a
        out[v, :, 384:512] = b
        tiles[0].append(a)
        tiles[1].append(b)
    store_traces(tiles[0], tiles[1], lo, hi)


def sound_two_body(q0, q2, src, dx, dy, dz, gcat, esrc, edst, part):
    terms = local_terms([q2[v].astype(BF16) for v in range(4)], dx, dy, dz, gcat, esrc, edst)
    for v in range(4):
        t = terms[v] if v == 0 else terms[v] + src[v - 1].astype(F32)
        start = q0[v].astype(F32)
        part[v] = start * (1.0 / 3.0) + (2.0 / 3.0) * (q2[v] + SOUND_STEP * t) - start


def final_body(scale, gx0, gx1, olo, ohi, bhi, alo, part, out):
    first, last = cross_terms(gx0, gx1, olo, ohi, bhi, alo)
    for v in range(4):
        out[v] = part[v]
        out[v, :, 0:128] = part[v, :, 0:128] + scale * first[v]
        out[v, :, 384:512] = part[v, :, 384:512] + scale * last[v]


def neighbour_pair(low_going, high_going, axis):
    count = lax.axis_size(axis)
    up = [(i, (i + 1) % count) for i in range(count)]
    down = [(b, a) for a, b in up]
    return lax.ppermute(high_going, axis, up), lax.ppermute(low_going, axis, down)


def local(flow_state, acoustic_state, dx, dy, dz, requests, elem_slot, neighbours):
    both = ("solver", "space")
    me = lax.axis_index("solver") * lax.axis_size("space") + lax.axis_index("space")

    wanted = jnp.pad(requests.reshape(128, 1, 4), ((0, 0), (0, 0), (0, 124)))
    wanted = lax.all_to_all(wanted, both, split_axis=0, concat_axis=0, tiled=True)

    xlo, xhi, zlo, zhi, qlo, qhi = call(
        edges_body,
        [full(5, 128, 128)] * 2 + [full(128, 128)] * 2 + [half(2, EL, 128)] * 2,
        "edges",
        (flow_state, acoustic_state),
    )
    xbelow, xabove = neighbour_pair(xlo, xhi, "space")
    zbelow, zabove = neighbour_pair(zlo, zhi, "solver")
    bhi, alo = neighbour_pair(qlo, qhi, "space")

    row = neighbours % EL
    away = (neighbours // EL != me).astype(I32) * EL
    spot = elem_slot // 4 * 8 + elem_slot % 4
    cols = [row[0] + away[0], row[1] + away[1]]
    cols += [row[2 + f] + f * EL for f in range(4)]
    cols += [spot, spot + 4]
    idx = jnp.stack(cols, axis=1)
    gcat, gx0, gx1, pick, esrc, edst = call(
        prepare_body,
        [half(EL, 4 * EL), half(EL, 2 * EL), half(EL, 2 * EL), half(2, EL, 1024), half(512, 256), half(256, 512)],
        "prepare",
        (idx,),
    )

    table = call(
        lamb_body,
        half(128, 768),
        "lamb",
        (flow_state, xbelow, xabove, zbelow, zabove),
        scratch=[pltpu.VMEM((3, 6, 128, 128), F32), pltpu.VMEM((6, 128, 128), F32)],
    )
    send = call(send_body, half(128, 48, 128), "send", (wanted, table))
    got = lax.all_to_all(send, both, split_axis=0, concat_axis=0, tiled=True)

    first, xlo, xhi, zlo, zhi = call(
        stage_one_body,
        [full(5, 4, 128, 128)] + [full(5, 128, 128)] * 2 + [full(128, 128)] * 2,
        "flow_one",
        (flow_state, xbelow, xabove, zbelow, zabove),
        scratch=[pltpu.VMEM((5, 6, 128, 128), F32)],
    )
    xbelow, xabove = neighbour_pair(xlo, xhi, "space")
    zbelow, zabove = neighbour_pair(zlo, zhi, "solver")

    mats = (dx, dy, dz, gcat, esrc, edst)
    part = call(
        sound_zero_body,
        full(4, EL, NODES),
        "sound_zero",
        (acoustic_state,) + mats + (gx0, gx1, qlo, qhi, bhi, alo),
    )
    flow_increment = call(
        stage_two_body,
        full(5, 4, 128, 128),
        "flow_two",
        (flow_state, first, xbelow, xabove, zbelow, zabove),
        scratch=[pltpu.VMEM((5, 6, 128, 128), F32)],
    )

    traces = [half(2, EL, 128)] * 2
    q1, src, qlo, qhi = call(
        sources_body,
        [full(4, EL, NODES), half(3, EL, NODES)] + traces,
        "sources",
        (got, pick, part),
    )
    bhi, alo = neighbour_pair(qlo, qhi, "space")
    part = call(sound_one_body, full(4, EL, NODES), "sound_one", (acoustic_state, q1, src) + mats)
    q2, qlo2, qhi2 = call(
        lambda *r: cross_body(0.25 * SOUND_STEP, *r),
        [full(4, EL, NODES)] + traces,
        "cross_one",
        (gx0, gx1, qlo, qhi, bhi, alo, part),
    )
    bhi, alo = neighbour_pair(qlo2, qhi2, "space")
    part = call(sound_two_body, full(4, EL, NODES), "sound_two", (acoustic_state, q2, src) + mats)
    out = call(
        lambda *r: final_body(2.0 / 3.0 * SOUND_STEP, *r),
        full(4, EL, NODES),
        "cross_two",
        (gx0, gx1, qlo2, qhi2, bhi, alo, part),
    )
    return flow_increment, out


def solution(mesh):
    both = ("solver", "space")
    grid = P(None, "space", None, "solver")
    sound = P(None, both, None)
    in_specs = (grid, sound, P(), P(), P(), P(both, None, None), P(both), P(None, both))
    return jax.shard_map(
        local, mesh=mesh, in_specs=in_specs, out_specs=(grid, sound), check_vma=False
    )
```

profile of v0, /device:TPU:1, one launch (start us, length us, event | category | flops | bytes accessed | tf_op | source)
XLA Modules:
  0.0 111.4 jit_solution(16858651249433611892)
XLA Ops:
  3.1 1.8 %edges.1 = (f32[5,128,128]{2,1,0:T(8,128)S(1)}, f32[5,128,128]{2,1,0:T(8,128)S(1)}, f32[128,128]{1,0:T(8,128)S(1)}, f32[128,128]{1,0:T(8,128)S(1)}, bf16[2,224,1...) custom-call(f32[5,4,128,128]{3,2,1,0:T(8,128)S(1)} %copy-done, bf16[4,224,512]{2,1,0:T(8,128)(2,1)S(1)} %copy-done.2), custom_call_target="tpu_custom_call" | custom-call | tf_op jit(solution)/shard_map/edges/pallas_call | solution.py:34
  4.9 2.0 %collective-permute-start = (f32[5,128,128]{2,1,0:T(8,128)S(1)}, f32[5,128,128]{2,1,0:T(8,128)S(1)}, u32[]{:S(2)}, u32[]{:S(2)}) collective-permute-start(f32[5,128,128]{2,1,0:T(8,128)S(1)} %get-tuple-element.26), channel_id=1, source_target_pairs={{0,1},{1,2},{2,3},{3,4},{4,5},{5,6},{6,7},{7,8},{8,9},{9,10},{10,1... | collective-permute-start | bytes 983048 | tf_op jit(solution)/shard_map/ppermute | solution.py:440
  6.9 7.0 %collective-permute-start.1 = (f32[5,128,128]{2,1,0:T(8,128)S(1)}, f32[5,128,128]{2,1,0:T(8,128)S(1)}, u32[]{:S(2)}, u32[]{:S(2)}) collective-permute-start(f32[5,128,128]{2,1,0:T(8,128)S(1)} %get-tuple-element.27), channel_id=1, source_target_pairs={{1,0},{2,1},{3,2},{4,3},{5,4},{6,5},{7,6},{8,7},{9,8},{10,9},{11,1... | collective-permute-start | bytes 983048 | tf_op jit(solution)/shard_map/ppermute | solution.py:440
  14.0 1.7 %collective-permute-start.2 = (f32[128,128]{1,0:T(8,128)S(1)}, f32[128,128]{1,0:T(8,128)S(1)}, u32[]{:S(2)}, u32[]{:S(2)}) collective-permute-start(f32[128,128]{1,0:T(8,128)S(1)} %get-tuple-element.28), channel_id=1, source_target_pairs={{0,32},{32,64},{64,96},{96,0},{1,33},{33,65},{65,97},{97,1},{2,34}... | collective-permute-start | bytes 196616 | tf_op jit(solution)/shard_map/ppermute | solution.py:440
  16.5 5.1 %all-to-all-start = ((s32[128,1,128]{2,1,0:T(1,128)}), s32[128,1,128]{2,1,0:T(1,128)S(1)}, u32[]{:S(2)}, u32[]{:S(2)}) async-start(s32[128,1,128]{2,1,0:T(1,128)} %pad.4), calls=%async_computation | async-start | bytes 131072 | tf_op jit(solution)/shard_map/all_to_all | solution.py:448
  22.4 1.5 %collective-permute-done.3.zabove = f32[128,128]{1,0:T(8,128)S(1)} collective-permute-done((f32[128,128]{1,0:T(8,128)S(1)}, f32[128,128]{1,0:T(8,128)S(1)}, u32[]{:S(2)}, u32[]{:S(2)}) %collective-permute-start.3) | collective-permute-done | bytes 65568 | tf_op jit(solution)/shard_map/ppermute | solution.py:440
  24.9 6.3 %all-to-all-done.req = s32[128,1,128]{2,1,0:T(1,128)S(1)} async-done(((s32[128,1,128]{2,1,0:T(1,128)}), s32[128,1,128]{2,1,0:T(1,128)S(1)}, u32[]{:S(2)}, u32[]{:S(2)}) %all-to-all-start) | async-done | bytes 65568 | tf_op jit(solution)/shard_map/all_to_all | solution.py:448
  31.2 2.2 %send.1 = bf16[128,48,128]{2,1,0:T(8,128)(2,1)} custom-call(s32[128,1,128]{2,1,0:T(1,128)S(1)} %all-to-all-done.req, bf16[128,768]{1,0:T(8,128)(2,1)S(1)} %lamb.1.table), custom_call_target="tpu_custom_call" | custom-call | tf_op jit(solution)/shard_map/send/pallas_call | solution.py:34
  33.4 5.3 %all-to-all-start.1 = ((bf16[128,48,128]{2,1,0:T(8,128)(2,1)}), bf16[128,48,128]{2,1,0:T(8,128)(2,1)}, u32[]{:S(2)}, u32[]{:S(2)}) async-start(bf16[128,48,128]{2,1,0:T(8,128)(2,1)} %send.1), calls=%async_computation.1 | async-start | bytes 3145728 | tf_op jit(solution)/shard_map/all_to_all | solution.py:482
  38.8 1.5 %collective-permute-start.8 = (bf16[2,224,128]{2,1,0:T(8,128)(2,1)}, bf16[2,224,128]{2,1,0:T(8,128)(2,1)}, u32[]{:S(2)}, u32[]{:S(2)}) collective-permute-start(bf16[2,224,128]{2,1,0:T(8,128)(2,1)} %get-tuple-element.42.ohi), channel_id=1, source_target_pairs={{0,1},{1,2},{2,3},{3,4},{4,5},{5,6},{6,7},{7,8},{8,9},{9,10},{10,1... | collective-permute-start | bytes 344072 | tf_op jit(solution)/shard_map/ppermute | solution.py:440
  40.2 6.6 %collective-permute-start.9 = (bf16[2,224,128]{2,1,0:T(8,128)(2,1)}, bf16[2,224,128]{2,1,0:T(8,128)(2,1)}, u32[]{:S(2)}, u32[]{:S(2)}) collective-permute-start(bf16[2,224,128]{2,1,0:T(8,128)(2,1)} %get-tuple-element.41.olo), channel_id=1, source_target_pairs={{1,0},{2,1},{3,2},{4,3},{5,4},{6,5},{7,6},{8,7},{9,8},{10,9},{11,1... | collective-permute-start | bytes 344072 | tf_op jit(solution)/shard_map/ppermute | solution.py:440
  48.8 2.9 %flow_one.1 = (f32[5,4,128,128]{3,2,1,0:T(8,128)S(1)}, f32[5,128,128]{2,1,0:T(8,128)}, f32[5,128,128]{2,1,0:T(8,128)}, f32[128,128]{1,0:T(8,128)S(1)}, f32[128,128]{1,0:T(8,128)S(1)}) custom-call(f32[5,4,128,128]{3,2,1,0:T(8,128)S(1)} %copy-done.1, f32[5,128,128]{2,1,0:T(8,128)S(1)} %copy-done.21, f32[5,128,128]{2,1,0:T(8,128)S(1)} %copy-done.23, ...), custom_call_target="tpu_custom_call" | custom-call | tf_op jit(solution)/shard_map/flow_one/pallas_call | solution.py:34
  54.0 7.2 %collective-permute-start.5 = (f32[5,128,128]{2,1,0:T(8,128)}, f32[5,128,128]{2,1,0:T(8,128)}, u32[]{:S(2)}, u32[]{:S(2)}) collective-permute-start(f32[5,128,128]{2,1,0:T(8,128)} %get-tuple-element.32), channel_id=1, source_target_pairs={{1,0},{2,1},{3,2},{4,3},{5,4},{6,5},{7,6},{8,7},{9,8},{10,9},{11,1... | collective-permute-start | bytes 983048 | tf_op jit(solution)/shard_map/ppermute | solution.py:440
  66.8 3.6 %sound_zero.1.part = f32[4,224,512]{2,1,0:T(8,128)S(1)} custom-call(bf16[4,224,512]{2,1,0:T(8,128)(2,1)S(1)} %copy-done.3, bf16[512,512]{1,0:T(8,128)(2,1)S(1)} %copy-done.6, bf16[512,512]{1,0:T(8,128)(2,1)S(1)} %copy-done.7, bf16[512,512]{1,0:T(8,128)(2,1)S(1)} %copy-done.8, bf16[224,896]{1,0:T(8,128)(2,1)S(1)} %get-tuple-element.38.gcat, ...), custom_call_target="tpu_custom_call" | custom-call | tf_op jit(solution)/shard_map/sound_zero/pallas_call | solution.py:34
  74.5 1.5 %copy-done.5 = f32[4,224,512]{2,1,0:T(8,128)S(1)} copy-done((f32[4,224,512]{2,1,0:T(8,128)S(1)}, f32[4,224,512]{2,1,0:T(8,128)}, u32[]{:S(2)}) %copy-start.5) | copy-done | bytes 1835032
  77.2 2.5 %sources.1 = (f32[4,224,512]{2,1,0:T(8,128)S(1)}, bf16[3,224,512]{2,1,0:T(8,128)(2,1)S(1)}, bf16[2,224,128]{2,1,0:T(8,128)(2,1)S(1)}, bf16[2,224,128]{2,1,0:T(8,128)(2,1)S(1)}) custom-call(bf16[128,48,128]{2,1,0:T(8,128)(2,1)} %all-to-all-done.1.got, bf16[2,224,1024]{2,1,0:T(8,128)(2,1)S(1)} %copy-done.25, f32[4,224,512]{2,1,0:T(8,128)S(1)} %copy-done.5), custom_call_target="tpu_custom_call" | custom-call | tf_op jit(solution)/shard_map/sources/pallas_call | solution.py:34
  79.8 7.2 %collective-permute-start.11 = (bf16[2,224,128]{2,1,0:T(8,128)(2,1)S(1)}, bf16[2,224,128]{2,1,0:T(8,128)(2,1)S(1)}, u32[]{:S(2)}, u32[]{:S(2)}) collective-permute-start(bf16[2,224,128]{2,1,0:T(8,128)(2,1)S(1)} %get-tuple-element.43.r_2_), channel_id=1, source_target_pairs={{1,0},{2,1},{3,2},{4,3},{5,4},{6,5},{7,6},{8,7},{9,8},{10,9},{11,1... | collective-permute-start | bytes 344072 | tf_op jit(solution)/shard_map/ppermute | solution.py:440
  87.0 2.3 %collective-permute-start.6 = (f32[128,128]{1,0:T(8,128)S(1)}, f32[128,128]{1,0:T(8,128)S(1)}, u32[]{:S(2)}, u32[]{:S(2)}) collective-permute-start(f32[128,128]{1,0:T(8,128)S(1)} %copy-done.30), channel_id=1, source_target_pairs={{0,32},{32,64},{64,96},{96,0},{1,33},{33,65},{65,97},{97,1},{2,34}... | collective-permute-start | bytes 196616 | tf_op jit(solution)/shard_map/ppermute | solution.py:440
  89.4 2.5 %sound_one.1.r_6_ = f32[4,224,512]{2,1,0:T(8,128)S(1)} custom-call(bf16[4,224,512]{2,1,0:T(8,128)(2,1)S(1)} %copy-done.3, f32[4,224,512]{2,1,0:T(8,128)S(1)} %get-tuple-element.45.q1, bf16[3,224,512]{2,1,0:T(8,128)(2,1)S(1)} %get-tuple-element.46.src, bf16[512,512]{1,0:T(8,128)(2,1)S(1)} %copy-done.6, bf16[512,512]{1,0:T(8,128)(2,1)S(1)} %copy-done.7, ...), custom_call_target="tpu_custom_call" | custom-call | tf_op jit(solution)/shard_map/sound_one/pallas_call | solution.py:34
  92.5 7.2 %collective-permute-start.13 = (bf16[2,224,128]{2,1,0:T(8,128)(2,1)S(1)}, bf16[2,224,128]{2,1,0:T(8,128)(2,1)S(1)}, u32[]{:S(2)}, u32[]{:S(2)}) collective-permute-start(bf16[2,224,128]{2,1,0:T(8,128)(2,1)S(1)} %get-tuple-element.47.r_2_), channel_id=1, source_target_pairs={{1,0},{2,1},{3,2},{4,3},{5,4},{6,5},{7,6},{8,7},{9,8},{10,9},{11,1... | collective-permute-start | bytes 344072 | tf_op jit(solution)/shard_map/ppermute | solution.py:440
  100.1 3.3 %collective-permute-done.7.zabove = f32[128,128]{1,0:T(8,128)S(1)} collective-permute-done((f32[128,128]{1,0:T(8,128)S(1)}, f32[128,128]{1,0:T(8,128)S(1)}, u32[]{:S(2)}, u32[]{:S(2)}) %collective-permute-start.7) | collective-permute-done | bytes 65568 | tf_op jit(solution)/shard_map/ppermute | solution.py:440
  103.4 3.7 %flow_two.1 = f32[5,4,128,128]{3,2,1,0:T(8,128)} custom-call(f32[5,4,128,128]{3,2,1,0:T(8,128)S(1)} %copy-done.1, f32[5,4,128,128]{3,2,1,0:T(8,128)S(1)} %copy-done.19, f32[5,128,128]{2,1,0:T(8,128)} %collective-permute-done.4.xbelow, f32[5,128,128]{2,1,0:T(8,128)} %collective-permute-done.5.xabove, f32[128,128]{1,0:T(8,128)S(1)} %collective-permute-done.6.zbelow, ...), custom_call_target="tpu_custom_call" | custom-call | tf_op jit(solution)/shard_map/flow_two/pallas_call | solution.py:34
  107.2 2.6 %sound_two.1.r_6_ = f32[4,224,512]{2,1,0:T(8,128)S(1)} custom-call(bf16[4,224,512]{2,1,0:T(8,128)(2,1)S(1)} %copy-done.3, f32[4,224,512]{2,1,0:T(8,128)S(1)} %get-tuple-element.49.q2, bf16[3,224,512]{2,1,0:T(8,128)(2,1)S(1)} %get-tuple-element.46.src, bf16[512,512]{1,0:T(8,128)(2,1)S(1)} %copy-done.6, bf16[512,512]{1,0:T(8,128)(2,1)S(1)} %copy-done.7, ...), custom_call_target="tpu_custom_call" | custom-call | tf_op jit(solution)/shard_map/sound_two/pallas_call | solution.py:34
  109.8 1.7 %cross_two.1 = f32[4,224,512]{2,1,0:T(8,128)} custom-call(bf16[224,448]{1,0:T(8,128)(2,1)S(1)} %copy-done.15, bf16[224,448]{1,0:T(8,128)(2,1)S(1)} %copy-done.17, bf16[2,224,128]{2,1,0:T(8,128)(2,1)S(1)} %get-tuple-element.47.r_2_, bf16[2,224,128]{2,1,0:T(8,128)(2,1)S(1)} %get-tuple-element.48.r_3_, bf16[2,224,128]{2,1,0:T(8,128)(2,1)S(1)} %collective-permute-done.12.r_4_, ...), custom_call_target="tpu_custom_call" | custom-call | tf_op jit(solution)/shard_map/cross_two/pallas_call | solution.py:34
  (95 shorter events, 21.3 us)
Async XLA Ops:
  3.1 12.6 %copy-start.32 = (s32[1,128,4]{1,2,0:T(4,128)S(1)}, s32[1,128,4]{1,2,0:T(4,128)}, u32[]{:S(2)}) copy-start(s32[1,128,4]{1,2,0:T(4,128)} %param.13) | copy-start | bytes 6148
  3.1 20.7 %copy-start.1 = (f32[5,4,128,128]{3,2,1,0:T(8,128)S(1)}, f32[5,4,128,128]{3,2,1,0:T(8,128)}, u32[]{:S(2)}) copy-start(f32[5,4,128,128]{3,2,1,0:T(8,128)} %u.7) | copy-start | bytes 3932164
  4.9 19.0 %collective-permute-start = (f32[5,128,128]{2,1,0:T(8,128)S(1)}, f32[5,128,128]{2,1,0:T(8,128)S(1)}, u32[]{:S(2)}, u32[]{:S(2)}) collective-permute-start(f32[5,128,128]{2,1,0:T(8,128)S(1)} %get-tuple-element.26), channel_id=1, source_target_pairs={{0,1},{1,2},{2,3},{3,4},{4,5},{5,6},{6,7},{7,8},{8,9},{9,10},{10,1... | collective-permute-start | bytes 983048 | tf_op jit(solution)/shard_map/ppermute | solution.py:440
  6.9 16.9 %collective-permute-start.1 = (f32[5,128,128]{2,1,0:T(8,128)S(1)}, f32[5,128,128]{2,1,0:T(8,128)S(1)}, u32[]{:S(2)}, u32[]{:S(2)}) collective-permute-start(f32[5,128,128]{2,1,0:T(8,128)S(1)} %get-tuple-element.27), channel_id=1, source_target_pairs={{1,0},{2,1},{3,2},{4,3},{5,4},{6,5},{7,6},{8,7},{9,8},{10,9},{11,1... | collective-permute-start | bytes 983048 | tf_op jit(solution)/shard_map/ppermute | solution.py:440
  14.0 8.4 %collective-permute-start.2 = (f32[128,128]{1,0:T(8,128)S(1)}, f32[128,128]{1,0:T(8,128)S(1)}, u32[]{:S(2)}, u32[]{:S(2)}) collective-permute-start(f32[128,128]{1,0:T(8,128)S(1)} %get-tuple-element.28), channel_id=1, source_target_pairs={{0,32},{32,64},{64,96},{96,0},{1,33},{33,65},{65,97},{97,1},{2,34}... | collective-permute-start | bytes 196616 | tf_op jit(solution)/shard_map/ppermute | solution.py:440
  15.7 8.2 %collective-permute-start.3 = (f32[128,128]{1,0:T(8,128)S(1)}, f32[128,128]{1,0:T(8,128)S(1)}, u32[]{:S(2)}, u32[]{:S(2)}) collective-permute-start(f32[128,128]{1,0:T(8,128)S(1)} %get-tuple-element.29), channel_id=1, source_target_pairs={{32,0},{64,32},{96,64},{0,96},{33,1},{65,33},{97,65},{1,97},{34,2}... | collective-permute-start | bytes 196616 | tf_op jit(solution)/shard_map/ppermute | solution.py:440
  16.5 14.7 %all-to-all-start = ((s32[128,1,128]{2,1,0:T(1,128)}), s32[128,1,128]{2,1,0:T(1,128)S(1)}, u32[]{:S(2)}, u32[]{:S(2)}) async-start(s32[128,1,128]{2,1,0:T(1,128)} %pad.4), calls=%async_computation | async-start | bytes 131072 | tf_op jit(solution)/shard_map/all_to_all | solution.py:448
  33.4 13.4 %copy-start.31 = (s32[6,224]{1,0:T(8,128)S(1)}, s32[6,224]{1,0:T(8,128)}, u32[]{:S(2)}) copy-start(s32[6,224]{1,0:T(8,128)} %param.15) | copy-start | bytes 16132
  33.4 27.8 %copy-start.33 = (s32[224]{0:T(256)S(1)}, s32[224]{0:T(256)}, u32[]{:S(2)}) copy-start(s32[224]{0:T(256)} %param.14) | copy-start | bytes 2692
  33.4 41.1 %all-to-all-start.1 = ((bf16[128,48,128]{2,1,0:T(8,128)(2,1)}), bf16[128,48,128]{2,1,0:T(8,128)(2,1)}, u32[]{:S(2)}, u32[]{:S(2)}) async-start(bf16[128,48,128]{2,1,0:T(8,128)(2,1)} %send.1), calls=%async_computation.1 | async-start | bytes 3145728 | tf_op jit(solution)/shard_map/all_to_all | solution.py:482
  38.7 27.0 %copy-start.3 = (bf16[4,224,512]{2,1,0:T(8,128)(2,1)S(1)}, bf16[4,224,512]{2,1,0:T(8,128)(2,1)}, u32[]{:S(2)}) copy-start(bf16[4,224,512]{2,1,0:T(8,128)(2,1)} %q0.3) | copy-start | bytes 2752516
  38.7 27.0 %copy-start.6 = (bf16[512,512]{1,0:T(8,128)(2,1)S(1)}, bf16[512,512]{1,0:T(8,128)(2,1)}, u32[]{:S(2)}) copy-start(bf16[512,512]{1,0:T(8,128)(2,1)} %dx.5) | copy-start | bytes 1572868
  38.7 27.0 %copy-start.7 = (bf16[512,512]{1,0:T(8,128)(2,1)S(1)}, bf16[512,512]{1,0:T(8,128)(2,1)}, u32[]{:S(2)}) copy-start(bf16[512,512]{1,0:T(8,128)(2,1)} %dy.5) | copy-start | bytes 1572868
  38.8 27.0 %collective-permute-start.8 = (bf16[2,224,128]{2,1,0:T(8,128)(2,1)}, bf16[2,224,128]{2,1,0:T(8,128)(2,1)}, u32[]{:S(2)}, u32[]{:S(2)}) collective-permute-start(bf16[2,224,128]{2,1,0:T(8,128)(2,1)} %get-tuple-element.42.ohi), channel_id=1, source_target_pairs={{0,1},{1,2},{2,3},{3,4},{4,5},{5,6},{6,7},{7,8},{8,9},{9,10},{10,1... | collective-permute-start | bytes 344072 | tf_op jit(solution)/shard_map/ppermute | solution.py:440
  40.2 25.5 %collective-permute-start.9 = (bf16[2,224,128]{2,1,0:T(8,128)(2,1)}, bf16[2,224,128]{2,1,0:T(8,128)(2,1)}, u32[]{:S(2)}, u32[]{:S(2)}) collective-permute-start(bf16[2,224,128]{2,1,0:T(8,128)(2,1)} %get-tuple-element.41.olo), channel_id=1, source_target_pairs={{1,0},{2,1},{3,2},{4,3},{5,4},{6,5},{7,6},{8,7},{9,8},{10,9},{11,1... | collective-permute-start | bytes 344072 | tf_op jit(solution)/shard_map/ppermute | solution.py:440
  54.0 49.5 %collective-permute-start.4 = (f32[5,128,128]{2,1,0:T(8,128)}, f32[5,128,128]{2,1,0:T(8,128)}, u32[]{:S(2)}, u32[]{:S(2)}) collective-permute-start(f32[5,128,128]{2,1,0:T(8,128)} %get-tuple-element.31), channel_id=1, source_target_pairs={{0,1},{1,2},{2,3},{3,4},{4,5},{5,6},{6,7},{7,8},{8,9},{9,10},{10,1... | collective-permute-start | bytes 983048 | tf_op jit(solution)/shard_map/ppermute | solution.py:440
  54.0 49.5 %collective-permute-start.5 = (f32[5,128,128]{2,1,0:T(8,128)}, f32[5,128,128]{2,1,0:T(8,128)}, u32[]{:S(2)}, u32[]{:S(2)}) collective-permute-start(f32[5,128,128]{2,1,0:T(8,128)} %get-tuple-element.32), channel_id=1, source_target_pairs={{1,0},{2,1},{3,2},{4,3},{5,4},{6,5},{7,6},{8,7},{9,8},{10,9},{11,1... | collective-permute-start | bytes 983048 | tf_op jit(solution)/shard_map/ppermute | solution.py:440
  77.2 12.1 %copy-start.13 = (bf16[256,512]{1,0:T(8,128)(2,1)S(1)}, bf16[256,512]{1,0:T(8,128)(2,1)}, u32[]{:S(2)}) copy-start(bf16[256,512]{1,0:T(8,128)(2,1)} %copy-done.12) | copy-start | bytes 786436
  79.7 12.1 %collective-permute-start.10 = (bf16[2,224,128]{2,1,0:T(8,128)(2,1)S(1)}, bf16[2,224,128]{2,1,0:T(8,128)(2,1)S(1)}, u32[]{:S(2)}, u32[]{:S(2)}) collective-permute-start(bf16[2,224,128]{2,1,0:T(8,128)(2,1)S(1)} %get-tuple-element.44.r_3_), channel_id=1, source_target_pairs={{0,1},{1,2},{2,3},{3,4},{4,5},{5,6},{6,7},{7,8},{8,9},{9,10},{10,1... | collective-permute-start | bytes 344072 | tf_op jit(solution)/shard_map/ppermute | solution.py:440
  79.8 12.1 %collective-permute-start.11 = (bf16[2,224,128]{2,1,0:T(8,128)(2,1)S(1)}, bf16[2,224,128]{2,1,0:T(8,128)(2,1)S(1)}, u32[]{:S(2)}, u32[]{:S(2)}) collective-permute-start(bf16[2,224,128]{2,1,0:T(8,128)(2,1)S(1)} %get-tuple-element.43.r_2_), channel_id=1, source_target_pairs={{1,0},{2,1},{3,2},{4,3},{5,4},{6,5},{7,6},{8,7},{9,8},{10,9},{11,1... | collective-permute-start | bytes 344072 | tf_op jit(solution)/shard_map/ppermute | solution.py:440
  87.0 12.7 %collective-permute-start.6 = (f32[128,128]{1,0:T(8,128)S(1)}, f32[128,128]{1,0:T(8,128)S(1)}, u32[]{:S(2)}, u32[]{:S(2)}) collective-permute-start(f32[128,128]{1,0:T(8,128)S(1)} %copy-done.30), channel_id=1, source_target_pairs={{0,32},{32,64},{64,96},{96,0},{1,33},{33,65},{65,97},{97,1},{2,34}... | collective-permute-start | bytes 196616 | tf_op jit(solution)/shard_map/ppermute | solution.py:440
  92.4 17.3 %collective-permute-start.12 = (bf16[2,224,128]{2,1,0:T(8,128)(2,1)S(1)}, bf16[2,224,128]{2,1,0:T(8,128)(2,1)S(1)}, u32[]{:S(2)}, u32[]{:S(2)}) collective-permute-start(bf16[2,224,128]{2,1,0:T(8,128)(2,1)S(1)} %get-tuple-element.48.r_3_), channel_id=1, source_target_pairs={{0,1},{1,2},{2,3},{3,4},{4,5},{5,6},{6,7},{7,8},{8,9},{9,10},{10,1... | collective-permute-start | bytes 344072 | tf_op jit(solution)/shard_map/ppermute | solution.py:440
  92.5 17.2 %collective-permute-start.13 = (bf16[2,224,128]{2,1,0:T(8,128)(2,1)S(1)}, bf16[2,224,128]{2,1,0:T(8,128)(2,1)S(1)}, u32[]{:S(2)}, u32[]{:S(2)}) collective-permute-start(bf16[2,224,128]{2,1,0:T(8,128)(2,1)S(1)} %get-tuple-element.47.r_2_), channel_id=1, source_target_pairs={{1,0},{2,1},{3,2},{4,3},{5,4},{6,5},{7,6},{8,7},{9,8},{10,9},{11,1... | collective-permute-start | bytes 344072 | tf_op jit(solution)/shard_map/ppermute | solution.py:440
  99.7 3.7 %collective-permute-start.7 = (f32[128,128]{1,0:T(8,128)S(1)}, f32[128,128]{1,0:T(8,128)S(1)}, u32[]{:S(2)}, u32[]{:S(2)}) collective-permute-start(f32[128,128]{1,0:T(8,128)S(1)} %copy-done.28), channel_id=1, source_target_pairs={{32,0},{64,32},{96,64},{0,96},{33,1},{65,33},{97,65},{1,97},{34,2}... | collective-permute-start | bytes 196616 | tf_op jit(solution)/shard_map/ppermute | solution.py:440
  (26 other events, 94.0 us)
where the time goes:
time: 112 us; the launch traced here: 111 us
  starting transfers between devices  53.7 us (48%)
  Pallas kernels  26.1 us (23%)
  local copies, waits for them, and re-layouts  18 us (16%)
  waiting for transfers between devices  12.7 us (11%)
    ppermute x7, starting transfers between devices, neighbour_pair(): lax.ppermute(low_going, axis, down)  35.5 us
    pallas_call x12, Pallas kernels, call(): pl.pallas_call(body, out_shape=outs, in_specs=in_specs or [vmem] * len(ar...  26.1 us
    unnamed x69, local copies, waits for them, and re-layouts  16.5 us
    ppermute x7, starting transfers between devices, neighbour_pair(): lax.ppermute(high_going, axis, up)  7.7 us
    all_to_all x1, waiting for transfers between devices, local(): lax.all_to_all(wanted, both, split_axis=0, concat_axis=0, tiled=True)  6.27 us
    all_to_all x1, starting transfers between devices, local(): got = lax.all_to_all(send, both, split_axis=0, concat_axis=0, tiled=True)  5.34 us
    all_to_all x1, starting transfers between devices, local(): lax.all_to_all(wanted, both, split_axis=0, concat_axis=0, tiled=True)  5.12 us
    ppermute x7, waiting for transfers between devices, neighbour_pair(): lax.ppermute(low_going, axis, down)  4.81 us
  transfers between devices with their start and end apart: 16, of which 5 were waited for; matrix products, arithmetic and copies ran while one was open for 1% of the time, Pallas kernels for 18%

commit v1 on v0

v1 whole, which is shorter than its diff:
```python
import jax
import jax.numpy as jnp
from jax import lax
from jax.experimental import pallas as pl
from jax.experimental.pallas import tpu as pltpu
from jax.sharding import PartitionSpec as P

F32 = jnp.float32
BF16 = jnp.bfloat16
I32 = jnp.int32

EL = 224
NODES = 512
FLOW_STEP = 0.2
SOUND_STEP = 0.2
VMEM_LIMIT = 20 * 1024 * 1024


def iota(shape, dim):
    return lax.broadcasted_iota(I32, shape, dim)


def full(*shape):
    return jax.ShapeDtypeStruct(shape, F32)


def half(*shape):
    return jax.ShapeDtypeStruct(shape, BF16)


def call(body, outs, name, args, scratch=(), aliases=None, far=(), far_out=()):
    space = [pl.BlockSpec(memory_space=pltpu.VMEM), pl.BlockSpec(memory_space=pltpu.HBM)]
    many = isinstance(outs, (list, tuple))
    outs = list(outs) if many else [outs]
    out_specs = [space[i in far_out] for i in range(len(outs))]
    outs = [pltpu.HBM(t.shape, t.dtype) if i in far_out else t for i, t in enumerate(outs)]
    args = [
        pltpu.with_memory_space_constraint(t, pltpu.HBM) if i in far else t
        for i, t in enumerate(args)
    ]
    return pl.pallas_call(
        body,
        out_shape=outs if many else outs[0],
        in_specs=[space[i in far] for i in range(len(args))],
        out_specs=out_specs if many else out_specs[0],
        scratch_shapes=list(scratch),
        name=name,
        input_output_aliases=aliases or {},
        compiler_params=pltpu.CompilerParams(vmem_limit_bytes=VMEM_LIMIT),
    )(*args)


def begin(sems, first, *pairs):
    out = []
    for i, (source, target) in enumerate(pairs):
        copy = pltpu.make_async_copy(source, target, sems.at[first + i])
        copy.start()
        out.append(copy)
    return out


def finish(copies):
    for copy in copies:
        copy.wait()


def dma(n):
    return pltpu.SemaphoreType.DMA((n,))


def primitives(rows):
    inv = 1.0 / rows[0]
    v1, v2, v3 = rows[1] * inv, rows[2] * inv, rows[3] * inv
    p = 0.4 * (rows[4] - 0.5 * (rows[1] * v1 + rows[2] * v2 + rows[3] * v3))
    return (v1, v2, v3), p


def flux(rows, v, p, k):
    along = v[k]
    out = [rows[1 + k]]
    for c in range(3):
        t = rows[1 + c] * along
        out.append(t + p if c == k else t)
    out.append((rows[4] + p) * along)
    return out


def roll_y(f, step):
    return pltpu.roll(f, step % f.shape[0], 0)


def roll_z(f, step):
    return pltpu.roll(f, step % f.shape[1], 1)


def put_lane(acc, lane, f, source, target):
    return jnp.where(lane == target, roll_z(f, target - source), acc)


def diff_y(f):
    return roll_y(f, -1) - roll_y(f, 1)


def diff_z(f, lane, below, above, slot):
    up = jnp.where(lane == 127, roll_z(above, 127 - slot), roll_z(f, -1))
    down = jnp.where(lane == 0, roll_z(below, -slot), roll_z(f, 1))
    return up - down


def add_columns(x, fields, lane, lo, hi):
    for f, field in enumerate(fields):
        slot = f * 4 + x
        lo = put_lane(lo, lane, field, 0, slot)
        hi = put_lane(hi, lane, field, 127, slot)
    return lo, hi


def pair_lanes(tiles, upper):
    lane = iota((EL, 128), 1)
    out = []
    for w in range(2):
        a, b = tiles[2 * w], tiles[2 * w + 1]
        if upper:
            out.append(jnp.where(lane < 64, pltpu.roll(a, 64, 1), b))
        else:
            out.append(jnp.where(lane < 64, a, pltpu.roll(b, 64, 1)))
    return out


def store_traces(first_tiles, last_tiles, lo_ref, hi_ref):
    for w, t in enumerate(pair_lanes(first_tiles, False)):
        lo_ref[w] = t.astype(BF16)
    for w, t in enumerate(pair_lanes(last_tiles, True)):
        hi_ref[w] = t.astype(BF16)


def edges_body(u, req, xlo, xhi, zlo, zhi, want, mid, sems):
    copies = begin(
        sems,
        0,
        (u.at[:, 0], xlo),
        (u.at[:, 3], xhi),
        (u.at[:, 1], mid.at[0]),
        (u.at[:, 2], mid.at[1]),
    )
    eye = iota((128, 128), 0) == iota((128, 128), 1)
    value = req[...].astype(F32)
    spread = [jnp.where(eye, value[c : c + 1], 0.0).astype(BF16) for c in range(4)]
    place = jnp.where(iota((512, 128), 0) // 128 == iota((512, 128), 1), 1.0, 0.0).astype(BF16)
    turned = jnp.dot(jnp.concatenate(spread, 1), place, preferred_element_type=F32)
    want[...] = turned.reshape(128, 1, 128)
    lane = iota((128, 128), 1)
    lo = hi = jnp.zeros((128, 128), F32)
    for x, plane, copy in ((0, xlo, 0), (3, xhi, 1), (1, mid.at[0], 2), (2, mid.at[1], 3)):
        copies[copy].wait()
        rows = [plane[f] for f in range(5)]
        v, p = primitives(rows)
        lo, hi = add_columns(x, flux(rows, v, p, 2) + [v[0], v[1]], lane, lo, hi)
    zlo[...] = lo
    zhi[...] = hi


def lamb_body(u, xbelow, xabove, zbelow, zabove, table, vel, pooled):
    lane = iota((128, 128), 1)
    for x in range(-1, 5):
        if x == -1:
            r, m = xbelow[0], [xbelow[c] for c in (1, 2, 3)]
        elif x == 4:
            r, m = xabove[0], [xabove[c] for c in (1, 2, 3)]
        else:
            r, m = u[0, x], [u[c, x] for c in (1, 2, 3)]
        inv = 1.0 / r
        for c in range(3):
            vel[c, x + 1] = m[c] * inv
    below, above = zbelow[...], zabove[...]
    for pair in range(2):
        total = None
        for x in (2 * pair, 2 * pair + 1):
            v1, v2, v3 = vel[0, x + 1], vel[1, x + 1], vel[2, x + 1]
            w1 = diff_y(v3) - diff_z(v2, lane, below, above, 24 + x)
            w2 = diff_z(v1, lane, below, above, 20 + x) - (vel[2, x + 2] - vel[2, x])
            w3 = (vel[1, x + 2] - vel[1, x]) - diff_y(v1)
            lamb = [w2 * v3 - w3 * v2, w3 * v1 - w1 * v3, w1 * v2 - w2 * v1]
            total = lamb if total is None else [a + b for a, b in zip(total, lamb)]
        for c in range(3):
            pooled[c * 2 + pair] = total[c]
    even, odd = [], []
    for c in range(6):
        t = pooled.at[c]
        even.append(t[pl.ds(0, 32, stride=4), :] + t[pl.ds(1, 32, stride=4), :])
        odd.append(t[pl.ds(2, 32, stride=4), :] + t[pl.ds(3, 32, stride=4), :])
    rows = jnp.concatenate([jnp.concatenate(even, 0), jnp.concatenate(odd, 0)], 1)
    z, n = iota((256, 128), 0), iota((256, 128), 1)
    pool = jnp.where((z // 128) * 64 + (z % 128) // 2 == n, 0.0625, 0.0).astype(F32)
    coarse = jnp.dot(rows, pool, preferred_element_type=F32, precision=lax.Precision.HIGHEST)
    flat = pooled.at[0]
    hold = pooled.at[1]
    flat[...] = coarse[0:128]
    hold[0:64] = coarse[128:192]
    table[...] = jnp.zeros_like(table)
    for t in range(6):
        for par in range(2):
            c, inner = t // 2, (t % 2) * 2 + par
            src = flat if c < 2 else hold
            base = (c % 2) * 64
            piece = src[pl.ds(base + inner, 16, stride=4), :]
            table[par * 16 : par * 16 + 16, t * 128 : (t + 1) * 128] = piece.astype(BF16)


def tendency_plane(x, rows_of, along_a, below, above, lane):
    rows = rows_of(x)
    v, p = primitives(rows)
    fb = flux(rows, v, p, 1)
    fc = flux(rows, v, p, 2)
    out = []
    for f in range(5):
        total = along_a(x, f) + diff_y(fb[f])
        out.append(total + diff_z(fc[f], lane, below, above, f * 4 + x))
    return rows, out


def fill_flux_a(u, xbelow, xabove, fa, planes=range(-1, 5)):
    for x in planes:
        if x == -1:
            rows = [xbelow[f] for f in range(5)]
        elif x == 4:
            rows = [xabove[f] for f in range(5)]
        else:
            rows = [u[f, x] for f in range(5)]
        v, p = primitives(rows)
        for f, t in enumerate(flux(rows, v, p, 0)):
            fa[f, x + 1] = t


def stage_one_body(u, xbelow, xabove, zbelow, zabove, first, xlo, xhi, zlo, zhi, fa, hold, zpack, halo, zhalo, sems):
    lane = iota((128, 128), 1)
    fetch = begin(
        sems, 8, (xbelow, halo.at[0]), (xabove, halo.at[1]), (zbelow, zhalo.at[0]), (zabove, zhalo.at[1])
    )
    fill_flux_a(u, None, None, fa, range(4))
    finish(fetch)
    fill_flux_a(u, halo.at[0], halo.at[1], fa, (-1, 4))
    below, above = zhalo[0], zhalo[1]
    lo = hi = jnp.zeros((128, 128), F32)
    copies = []
    for i, x in enumerate((0, 3, 1, 2)):
        rows, out = tendency_plane(
            x,
            lambda x: [u[f, x] for f in range(5)],
            lambda x, f: fa[f, x + 2] - fa[f, x],
            below,
            above,
            lane,
        )
        now = [rows[f] - (FLOW_STEP * 0.5) * out[f] for f in range(5)]
        for f in range(5):
            hold[x, f] = now[f]
        copies += begin(sems, i, (hold.at[x], first.at[:, x]))
        if x in (0, 3):
            copies += begin(sems, 4 + i, (hold.at[x], xhi if x else xlo))
        v, p = primitives(now)
        lo, hi = add_columns(x, flux(now, v, p, 2), lane, lo, hi)
    zpack[0] = lo
    zpack[1] = hi
    copies += begin(sems, 6, (zpack.at[0], zlo), (zpack.at[1], zhi))
    finish(copies)


def stage_two_body(u, first, xbelow, xabove, zbelow, zabove, inc, fa, hold, sems):
    lane = iota((128, 128), 1)
    fill_flux_a(first, xbelow, xabove, fa)
    below, above = zbelow[...], zabove[...]
    copies = []
    for x in range(4):
        rows, out = tendency_plane(
            x,
            lambda x: [first[f, x] for f in range(5)],
            lambda x, f: fa[f, x + 2] - fa[f, x],
            below,
            above,
            lane,
        )
        for f in range(5):
            hold[x, f] = 0.5 * ((rows[f] - u[f, x]) - (FLOW_STEP * 0.5) * out[f])
        copies += begin(sems, x, (hold.at[x], inc.at[:, x]))
    finish(copies)


def send_body(req, table, send, hold, sems):
    wanted = req[...].reshape(128, 128).astype(BF16)
    row, col = iota((1024, 128), 0), iota((1024, 128), 1)
    spread = jnp.where(row // 8 == col, 1.0, 0.0).astype(BF16)
    rep = jnp.dot(spread, wanted, preferred_element_type=F32)
    own = jnp.where(row % 4 == col, rep, 0.0).astype(BF16)
    value = jnp.dot(own, jnp.ones((128, 128), BF16), preferred_element_type=F32)
    target = value + ((row % 8) // 4 * 16).astype(F32)
    pick = jnp.where(col.astype(F32) == target, 1.0, 0.0).astype(BF16)
    copies = []
    for u in range(3):
        rows = jnp.dot(pick, table[:, 256 * u : 256 * u + 256], preferred_element_type=F32)
        a = rows[:, 0:128].reshape(128, 8, 128)
        b = rows[:, 128:256].reshape(128, 8, 128)
        hold[u] = jnp.concatenate([a, b], 1).astype(BF16)
        copies += begin(sems, u, (hold.at[u], send.at[:, 16 * u : 16 * u + 16, :]))
    finish(copies)


def gather_source(got, pick):
    t = got[...].astype(F32)
    rhs = jnp.concatenate(
        [
            t[:, 0:8, :].reshape(1024, 128).astype(BF16),
            t[:, 8:16, :].reshape(1024, 128).astype(BF16),
        ],
        1,
    )
    even = jnp.dot(pick[0], rhs, preferred_element_type=F32)
    odd = jnp.dot(pick[1], rhs, preferred_element_type=F32)
    return jnp.concatenate([even[:, 0:128], odd[:, 0:128], even[:, 128:256], odd[:, 128:256]], 1)


def prepare_body(nb, slot, q, gcat, gx0, gx1, pick, esrc, edst, qlo, qhi, *scratch):
    gcat_v, gx0_v, gx1_v, pick_v, esrc_v, edst_v, ends, packs, sems = scratch
    fetch = begin(sems, 0, (q.at[:, :, 0:128], ends.at[0]), (q.at[:, :, 384:512], ends.at[1]))
    me = lax.axis_index("solver") * lax.axis_size("space") + lax.axis_index("space")
    owner, row = nb[...] // EL, nb[...] % EL
    away = jnp.where(owner == me, 0, EL)
    spot = slot[...] // 4 * 8 + slot[...] % 4
    cols = [row[f : f + 1] + away[f : f + 1] for f in range(2)]
    cols += [row[f : f + 1] for f in range(2, 6)] + [spot]
    eye = iota((EL, EL), 0) == iota((EL, EL), 1)
    spread = [jnp.where(eye, c.astype(F32), 0.0) for c in cols]
    coarse = [jnp.floor(t * (1.0 / 32.0)) for t in spread]
    fine = [t - 32.0 * c for t, c in zip(spread, coarse)]
    ones = jnp.ones((EL, 128), BF16)
    coarse = jnp.dot(jnp.concatenate(coarse, 0).astype(BF16), ones, preferred_element_type=F32)
    fine = jnp.dot(jnp.concatenate(fine, 0).astype(BF16), ones, preferred_element_type=F32)
    column = 32.0 * coarse + fine
    lane = iota((EL, 128), 1).astype(F32)

    def onehot(ref, col, width, shift=0.0):
        number = column[col * EL : (col + 1) * EL] + shift
        for t in range(0, width, 128):
            n = min(128, width - t)
            hit = jnp.where(lane + t == number, 1.0, 0.0).astype(BF16)
            ref[:, t : t + n] = hit[:, :n]

    onehot(gx0_v, 0, 2 * EL)
    onehot(gx1_v, 1, 2 * EL)
    copies = begin(sems, 2, (gx0_v, gx0), (gx1_v, gx1))
    for t in range(0, 4 * EL, 128):
        hit = jnp.zeros((EL, 128), jnp.bool_)
        for f in range(4):
            hit = hit | (lane + t == column[(2 + f) * EL : (3 + f) * EL] + f * EL)
        gcat_v[:, t : t + 128] = jnp.where(hit, 1.0, 0.0).astype(BF16)
    copies += begin(sems, 4, (gcat_v, gcat))
    onehot(pick_v.at[0], 6, 1024)
    onehot(pick_v.at[1], 6, 1024, 4.0)
    copies += begin(sems, 5, (pick_v, pick))
    finish(fetch)
    store_traces(
        [ends[0, v].astype(F32) for v in range(4)], [ends[1, v].astype(F32) for v in range(4)], packs.at[0], packs.at[1]
    )
    copies += begin(sems, 8, (packs.at[0], qlo), (packs.at[1], qhi))

    def node(c, flip):
        face, a, b = c // 64, c % 64 // 8, c % 8
        low = face % 2 == (1 if flip else 0)
        spot = jnp.where(low, 0, 7)
        return jnp.where(face < 2, a * 64 + spot * 8 + b, a * 64 + b * 8 + spot)

    esrc_v[...] = jnp.where(
        iota((512, 256), 0) == node(iota((512, 256), 1), True), 1.0, 0.0
    ).astype(BF16)
    edst_v[...] = jnp.where(
        iota((256, 512), 1) == node(iota((256, 512), 0), False), 1.0, 0.0
    ).astype(BF16)
    copies += begin(sems, 6, (esrc_v, esrc), (edst_v, edst))
    finish(copies)


def lamb_and_prepare_body(u, xb, xa, zb, za, nb, slot, q, table, *rest):
    vel, pooled = rest[8:10]
    lamb_body(u, xb, xa, zb, za, table, vel, pooled)
    prepare_body(nb, slot, q, *rest[:8], *rest[10:])


def face_count():
    n = iota((1, NODES), 1)
    count = jnp.zeros((1, NODES), I32)
    for part in (n // 64, n // 8 % 8, n % 8):
        count = count + jnp.where((part == 0) | (part == 7), 1, 0)
    return count.astype(F32)


def times(a, b):
    return lax.dot_general(a, b, (((1,), (1,)), ((), ())), preferred_element_type=F32)


def local_terms(q, dx, dy, dz, gcat, esrc, edst, ready=lambda *refs: None):
    traces = jnp.dot(jnp.concatenate(q, 0), esrc[...], preferred_element_type=F32).astype(BF16)
    wide = jnp.concatenate([traces[v * EL : (v + 1) * EL] for v in range(4)], 1)
    lane = iota((1, 1024), 1) % 256 // 64
    rhs = jnp.concatenate(
        [wide * jnp.where(lane == f, 1.0, 0.0).astype(BF16) for f in range(4)], 0
    )
    ready(gcat, edst)
    got = jnp.dot(gcat[...], rhs, preferred_element_type=F32).astype(BF16)
    count = face_count()
    out = []
    ready(dx, dy, dz)
    for v in range(4):
        pen = jnp.dot(got[:, v * 256 : (v + 1) * 256], edst[...], preferred_element_type=F32)
        pen = pen - count * q[v].astype(F32)
        if v == 0:
            vol = times(q[1], dx[...]) + times(q[2], dy[...]) + times(q[3], dz[...])
        else:
            vol = times(q[0], (dx, dy, dz)[v - 1][...])
        out.append(pen - vol)
    return out


def cross_terms(gx0, gx1, own_lo, own_hi, below_hi, above_lo):
    lane = iota((EL, 128), 1)
    first, last = [], []
    low = jnp.concatenate(
        [jnp.concatenate([own_hi[w], below_hi[w]], 0) for w in range(2)], 1
    )
    high = jnp.concatenate(
        [jnp.concatenate([own_lo[w], above_lo[w]], 0) for w in range(2)], 1
    )
    low = jnp.dot(gx0[...], low, preferred_element_type=F32)
    high = jnp.dot(gx1[...], high, preferred_element_type=F32)
    for v in range(4):
        w = v // 2
        a = low[:, w * 128 : (w + 1) * 128]
        b = high[:, w * 128 : (w + 1) * 128]
        if v % 2 == 0:
            b = pltpu.roll(b, 64, 1)
        else:
            a = pltpu.roll(a, 64, 1)
        first.append(jnp.where(lane < 64, a, 0.0))
        last.append(jnp.where(lane < 64, 0.0, b))
    return first, last


def sound_zero_body(*refs):
    given, (bhi, alo, part, *here), (hold, sems) = refs[:11], refs[11:25], refs[25:]
    coming = {id(to): copy for to, copy in zip(here, begin(sems, 4, *zip(given, here)))}
    ready = lambda *names: finish([coming[id(t)] for t in names])
    q, esrc, gcat, edst, dx, dy, dz, gx0, gx1, olo, ohi = here
    ready(q, esrc)
    rounded = [q[v] for v in range(4)]
    terms = local_terms(rounded, dx, dy, dz, gcat, esrc, edst, ready)
    ready(gx0, gx1, olo, ohi)
    first, last = cross_terms(gx0, gx1, olo, ohi, bhi, alo)
    copies = []
    for v in range(4):
        full_term = jnp.concatenate(
            [
                terms[v][:, 0:128] + first[v],
                terms[v][:, 128:384],
                terms[v][:, 384:512] + last[v],
            ],
            1,
        )
        hold[v] = q[v].astype(F32) + SOUND_STEP * full_term
        copies += begin(sems, v, (hold.at[v], part.at[v]))
    finish(copies)


def sources_body(got, pick, part, after, q1, src, lo, hi, pick_v, part_v, sems):
    copies = begin(
        sems,
        0,
        (pick, pick_v),
        (part.at[0], q1.at[0]),
        *[(part.at[v], part_v.at[v - 1]) for v in (1, 2, 3)],
    )
    copies[0].wait()
    for c in range(3):
        s = gather_source(got.at[:, 16 * c : 16 * c + 16, :], pick_v)
        src[c] = s.astype(BF16)
        copies[2 + c].wait()
        q1[1 + c] = part_v[c] + SOUND_STEP * s
    copies[1].wait()
    store_traces(
        [q1[v, :, 0:128] for v in range(4)],
        [q1[v, :, 384:512] for v in range(4)],
        lo,
        hi,
    )


def sound_one_body(q0, q1, src, dx, dy, dz, gcat, esrc, edst, part):
    terms = local_terms([q1[v].astype(BF16) for v in range(4)], dx, dy, dz, gcat, esrc, edst)
    for v in range(4):
        t = terms[v] if v == 0 else terms[v] + src[v - 1].astype(F32)
        part[v] = 0.75 * q0[v].astype(F32) + 0.25 * (q1[v] + SOUND_STEP * t)


def cross_body(scale, gx0, gx1, olo, ohi, bhi, alo, part, ends, lo, hi):
    first, last = cross_terms(gx0, gx1, olo, ohi, bhi, alo)
    tiles = [[], []]
    for v in range(4):
        a = part[v, :, 0:128] + scale * first[v]
        b = part[v, :, 384:512] + scale * last[v]
        ends[0, v] = a
        ends[1, v] = b
        tiles[0].append(a)
        tiles[1].append(b)
    store_traces(tiles[0], tiles[1], lo, hi)


def sound_two_body(q0, mid, ends, src, dx, dy, dz, gcat, esrc, edst, out, rest, hold, sems):
    q2 = [jnp.concatenate([ends[0, v], mid[v, :, 128:384], ends[1, v]], 1) for v in range(4)]
    terms = local_terms([t.astype(BF16) for t in q2], dx, dy, dz, gcat, esrc, edst)
    copies = []
    for v in range(4):
        t = terms[v] if v == 0 else terms[v] + src[v - 1].astype(F32)
        start = q0[v].astype(F32)
        t = start * (1.0 / 3.0) + (2.0 / 3.0) * (q2[v] + SOUND_STEP * t) - start
        hold[v] = t[:, 128:384]
        rest[0, v] = t[:, 0:128]
        rest[1, v] = t[:, 384:512]
        copies += begin(sems, v, (hold.at[v], out.at[v, :, 128:384]))
    finish(copies)


def final_body(scale, gx0, gx1, olo, ohi, bhi, alo, rest, given, out, hold, sems):
    first, last = cross_terms(gx0, gx1, olo, ohi, bhi, alo)
    copies = []
    for v in range(4):
        hold[0, v] = rest[0, v] + scale * first[v]
        hold[1, v] = rest[1, v] + scale * last[v]
        copies += begin(
            sems, 2 * v, (hold.at[0, v], out.at[v, :, 0:128]), (hold.at[1, v], out.at[v, :, 384:512])
        )
    finish(copies)


def neighbour_pair(low_going, high_going, axis):
    count = lax.axis_size(axis)
    up = [(i, (i + 1) % count) for i in range(count)]
    down = [(b, a) for a, b in up]
    return lax.ppermute(high_going, axis, up), lax.ppermute(low_going, axis, down)


def local(flow_state, acoustic_state, dx, dy, dz, requests, elem_slot, neighbours):
    both = ("solver", "space")
    grid = full(5, 4, 128, 128)
    plane, column = full(5, 128, 128), full(128, 128)
    state = full(4, EL, NODES)
    traces = [half(2, EL, 128)] * 2
    keep = lambda *shape: pltpu.VMEM(shape, F32)
    keep_half = lambda *shape: pltpu.VMEM(shape, BF16)

    xlo, xhi, zlo, zhi, wanted = call(
        edges_body,
        [plane, plane, column, column, full(128, 1, 128)],
        "edges",
        (flow_state, requests.reshape(128, 4).T),
        scratch=[keep(2, 5, 128, 128), dma(4)],
        far=(0,),
    )
    xbelow, xabove = neighbour_pair(xlo, xhi, "space")
    zbelow, zabove = neighbour_pair(zlo, zhi, "solver")
    wanted = lax.all_to_all(wanted, both, split_axis=0, concat_axis=0, tiled=True)

    shapes = [(EL, 4 * EL), (EL, 2 * EL), (EL, 2 * EL), (2, EL, 1024), (512, 256), (256, 512)]
    table, gcat, gx0, gx1, pick, esrc, edst, qlo, qhi = call(
        lamb_and_prepare_body,
        [half(128, 768)] + [half(*t) for t in shapes] + traces,
        "lamb",
        (flow_state, xbelow, xabove, zbelow, zabove, neighbours, elem_slot.reshape(1, EL), acoustic_state),
        scratch=[keep(3, 6, 128, 128), keep(6, 128, 128)]
        + [keep_half(*t) for t in shapes]
        + [keep_half(2, 4, EL, 128), keep_half(2, 2, EL, 128), dma(10)],
        far=(7,),
        far_out=range(1, 9),
    )
    bhi, alo = neighbour_pair(qlo, qhi, "space")
    first, xlo, xhi, zlo, zhi = call(
        stage_one_body,
        [grid, plane, plane, column, column],
        "flow_one",
        (flow_state, xbelow, xabove, zbelow, zabove),
        scratch=[keep(5, 6, 128, 128), keep(4, 5, 128, 128), keep(2, 128, 128), keep(2, 5, 128, 128), keep(2, 128, 128), dma(12)],
        far=(1, 2, 3, 4),
        far_out=range(5),
    )
    send = call(
        send_body,
        half(128, 48, 128),
        "send",
        (wanted, table),
        scratch=[keep_half(3, 128, 16, 128), dma(3)],
        far_out=(0,),
    )
    got = lax.all_to_all(send, both, split_axis=0, concat_axis=0, tiled=True)

    xbelow, xabove = neighbour_pair(xlo, xhi, "space")
    zbelow, zabove = neighbour_pair(zlo, zhi, "solver")
    mats = (dx, dy, dz, gcat, esrc, edst)
    given = (acoustic_state, esrc, gcat, edst, dx, dy, dz, gx0, gx1, qlo, qhi)
    part = call(
        sound_zero_body,
        state,
        "sound_zero",
        given + (bhi, alo),
        scratch=[keep_half(*t.shape) for t in given] + [keep(4, EL, NODES), dma(15)],
        far=range(11),
        far_out=(0,),
    )
    flow_increment = call(
        stage_two_body,
        grid,
        "flow_two",
        (flow_state, first, xbelow, xabove, zbelow, zabove),
        scratch=[keep(5, 6, 128, 128), keep(4, 5, 128, 128), dma(4)],
        far_out=(0,),
    )

    q1, src, qlo, qhi = call(
        sources_body,
        [state, half(3, EL, NODES)] + traces,
        "sources",
        (got, pick, part, flow_increment),
        scratch=[keep_half(2, EL, 1024), keep(3, EL, NODES), dma(5)],
        far=(1, 2, 3),
    )
    bhi, alo = neighbour_pair(qlo, qhi, "space")
    part = call(sound_one_body, state, "sound_one", (acoustic_state, q1, src) + mats)
    ends, qlo, qhi = call(
        lambda *r: cross_body(0.25 * SOUND_STEP, *r),
        [full(2, 4, EL, 128)] + traces,
        "cross_one",
        (gx0, gx1, qlo, qhi, bhi, alo, part),
    )
    bhi, alo = neighbour_pair(qlo, qhi, "space")
    out, rest = call(
        sound_two_body,
        [state, full(2, 4, EL, 128)],
        "sound_two",
        (acoustic_state, part, ends, src) + mats,
        scratch=[keep(4, EL, 256), dma(4)],
        far_out=(0,),
    )
    out = call(
        lambda *r: final_body(2.0 / 3.0 * SOUND_STEP, *r),
        state,
        "cross_two",
        (gx0, gx1, qlo, qhi, bhi, alo, rest, out),
        scratch=[keep(2, 4, EL, 128), dma(8)],
        far=(7,),
        far_out=(0,),
        aliases={7: 0},
    )
    return flow_increment, out


def solution(mesh):
    both = ("solver", "space")
    grid = P(None, "space", None, "solver")
    sound = P(None, both, None)
    in_specs = (grid, sound, P(), P(), P(), P(both, None, None), P(both), P(None, both))
    return jax.shard_map(
        local, mesh=mesh, in_specs=in_specs, out_specs=(grid, sound), check_vma=False
    )
```

time: 112 us -> 108 us (0.964)
  the two profiles are of different devices: /device:TPU:1 before, /device:TPU:0 now
where the time goes in v1:
time: 108 us; the launch traced here: 107 us
  starting transfers between devices  36.8 us (34%)
  waiting for transfers between devices  36.2 us (34%)
  Pallas kernels  31 us (29%)
  local copies, waits for them, and re-layouts  2.26 us (2%)
  between operations  1.17 us (1%)
    pallas_call x11, Pallas kernels, call(): pl.pallas_call(body, out_shape=outs if many else outs[0], in_specs=[space...  31 us
    ppermute x7, waiting for transfers between devices, neighbour_pair(): lax.ppermute(high_going, axis, up)  20.5 us
    ppermute x7, starting transfers between devices, neighbour_pair(): lax.ppermute(low_going, axis, down)  19.8 us
    ppermute x7, waiting for transfers between devices, neighbour_pair(): lax.ppermute(low_going, axis, down)  13.8 us
    all_to_all x1, starting transfers between devices, local(): got = lax.all_to_all(send, both, split_axis=0, concat_axis=0, tiled=True)  6.3 us
    ppermute x7, starting transfers between devices, neighbour_pair(): lax.ppermute(high_going, axis, up)  5.57 us
    all_to_all x1, starting transfers between devices, local(): lax.all_to_all(wanted, both, split_axis=0, concat_axis=0, tiled=True)  5.11 us
    unnamed x40, local copies, waits for them, and re-layouts  2.26 us
  transfers between devices with their start and end apart: 16, of which 7 were waited for; matrix products, arithmetic and copies ran while one was open for 0% of the time, Pallas kernels for 20%

profile of v1, /device:TPU:0, one launch (start us, length us, event | category | flops | bytes accessed | tf_op | source)
XLA Modules:
  0.0 107.4 jit_solution(8191678704225330936)
XLA Ops:
  1.4 2.6 %edges.1 = (f32[5,128,128]{2,1,0:T(8,128)S(1)}, f32[5,128,128]{2,1,0:T(8,128)S(1)}, f32[128,128]{1,0:T(8,128)S(1)}, f32[128,128]{1,0:T(8,128)S(1)}, f32[128,1,128]{2,1,0:T(1,128)}) custom-call(f32[5,4,128,128]{3,2,1,0:T(8,128)} %u.7, s32[4,128]{1,0:T(4,128)S(1)} %bitcast.4), custom_call_target="tpu_custom_call" | custom-call | tf_op jit(solution)/shard_map/edges/pallas_call | solution.py:41
  4.0 1.6 %collective-permute-start = (f32[5,128,128]{2,1,0:T(8,128)S(1)}, f32[5,128,128]{2,1,0:T(8,128)S(1)}, u32[]{:S(2)}, u32[]{:S(2)}) collective-permute-start(f32[5,128,128]{2,1,0:T(8,128)S(1)} %get-tuple-element.30), channel_id=1, source_target_pairs={{0,1},{1,2},{2,3},{3,4},{4,5},{5,6},{6,7},{7,8},{8,9},{9,10},{10,1... | collective-permute-start | bytes 983048 | tf_op jit(solution)/shard_map/ppermute | solution.py:546
  5.6 7.1 %collective-permute-start.1 = (f32[5,128,128]{2,1,0:T(8,128)S(1)}, f32[5,128,128]{2,1,0:T(8,128)S(1)}, u32[]{:S(2)}, u32[]{:S(2)}) collective-permute-start(f32[5,128,128]{2,1,0:T(8,128)S(1)} %get-tuple-element.31), channel_id=1, source_target_pairs={{1,0},{2,1},{3,2},{4,3},{5,4},{6,5},{7,6},{8,7},{9,8},{10,9},{11,1... | collective-permute-start | bytes 983048 | tf_op jit(solution)/shard_map/ppermute | solution.py:546
  12.8 1.7 %collective-permute-start.3 = (f32[128,128]{1,0:T(8,128)S(1)}, f32[128,128]{1,0:T(8,128)S(1)}, u32[]{:S(2)}, u32[]{:S(2)}) collective-permute-start(f32[128,128]{1,0:T(8,128)S(1)} %get-tuple-element.33), channel_id=1, source_target_pairs={{32,0},{64,32},{96,64},{0,96},{33,1},{65,33},{97,65},{1,97},{34,2}... | collective-permute-start | bytes 196616 | tf_op jit(solution)/shard_map/ppermute | solution.py:546
  14.5 5.1 %all-to-all-start = ((f32[128,1,128]{2,1,0:T(1,128)}), f32[128,1,128]{2,1,0:T(1,128)S(1)}, u32[]{:S(2)}, u32[]{:S(2)}) async-start(f32[128,1,128]{2,1,0:T(1,128)} %get-tuple-element.41), calls=%async_computation | async-start | bytes 131072 | tf_op jit(solution)/shard_map/all_to_all | solution.py:568
  19.6 2.4 %collective-permute-done.2.zbelow.zb = f32[128,128]{1,0:T(8,128)S(1)} collective-permute-done((f32[128,128]{1,0:T(8,128)S(1)}, f32[128,128]{1,0:T(8,128)S(1)}, u32[]{:S(2)}, u32[]{:S(2)}) %collective-permute-start.2) | collective-permute-done | bytes 65568 | tf_op jit(solution)/shard_map/ppermute | solution.py:546
  23.5 3.4 %lamb.1 = (bf16[128,768]{1,0:T(8,128)(2,1)S(1)}, bf16[224,896]{1,0:T(8,128)(2,1)}, bf16[224,448]{1,0:T(8,128)(2,1)}, bf16[224,448]{1,0:T(8,128)(2,1)}, bf16[2,22...) custom-call(f32[5,4,128,128]{3,2,1,0:T(8,128)S(1)} %copy-done, ...), custom_call_target="tpu_custom_call" | custom-call | tf_op jit(solution)/shard_map/lamb/pallas_call | solution.py:41
  26.9 1.9 %all-to-all-done.req = f32[128,1,128]{2,1,0:T(1,128)S(1)} async-done(((f32[128,1,128]{2,1,0:T(1,128)}), f32[128,1,128]{2,1,0:T(1,128)S(1)}, u32[]{:S(2)}, u32[]{:S(2)}) %all-to-all-start) | async-done | bytes 65568 | tf_op jit(solution)/shard_map/all_to_all | solution.py:568
  28.8 2.0 %send.1 = bf16[128,48,128]{2,1,0:T(8,128)(2,1)} custom-call(f32[128,1,128]{2,1,0:T(1,128)S(1)} %all-to-all-done.req, bf16[128,768]{1,0:T(8,128)(2,1)S(1)} %get-tuple-element.42.table), custom_call_target="tpu_custom_call" | custom-call | tf_op jit(solution)/shard_map/send/pallas_call | solution.py:41
  30.8 6.3 %all-to-all-start.1 = ((bf16[128,48,128]{2,1,0:T(8,128)(2,1)}), bf16[128,48,128]{2,1,0:T(8,128)(2,1)S(1)}, u32[]{:S(2)}, u32[]{:S(2)}) async-start(bf16[128,48,128]{2,1,0:T(8,128)(2,1)} %send.1), calls=%async_computation.1 | async-start | bytes 3145728 | tf_op jit(solution)/shard_map/all_to_all | solution.py:600
  37.1 4.1 %flow_one.1 = (f32[5,4,128,128]{3,2,1,0:T(8,128)}, f32[5,128,128]{2,1,0:T(8,128)}, f32[5,128,128]{2,1,0:T(8,128)}, f32[128,128]{1,0:T(8,128)}, f32[128,128]{1,0:T(8,128)}) custom-call(f32[5,4,128,128]{3,2,1,0:T(8,128)S(1)} %copy-done, f32[5,128,128]{2,1,0:T(8,128)} %copy-done.11, f32[5,128,128]{2,1,0:T(8,128)} %copy-done.12, f32[128,128]{1,0:T(8,128)} %copy-done.13, ...), custom_call_target="tpu_custom_call" | custom-call | tf_op jit(solution)/shard_map/flow_one/pallas_call | solution.py:41
  42.3 6.8 %collective-permute-start.5 = (f32[5,128,128]{2,1,0:T(8,128)}, f32[5,128,128]{2,1,0:T(8,128)S(1)}, u32[]{:S(2)}, u32[]{:S(2)}) collective-permute-start(f32[5,128,128]{2,1,0:T(8,128)} %get-tuple-element.36), channel_id=1, source_target_pairs={{1,0},{2,1},{3,2},{4,3},{5,4},{6,5},{7,6},{8,7},{9,8},{10,9},{11,1... | collective-permute-start | bytes 983048 | tf_op jit(solution)/shard_map/ppermute | solution.py:546
  49.1 1.6 %collective-permute-start.9 = (bf16[2,224,128]{2,1,0:T(8,128)(2,1)S(1)}, bf16[2,224,128]{2,1,0:T(8,128)(2,1)S(1)}, u32[]{:S(2)}, u32[]{:S(2)}) collective-permute-start(bf16[2,224,128]{2,1,0:T(8,128)(2,1)S(1)} %copy-done.18), channel_id=1, source_target_pairs={{1,0},{2,1},{3,2},{4,3},{5,4},{6,5},{7,6},{8,7},{9,8},{10,9},{11,1... | collective-permute-start | bytes 344072 | tf_op jit(solution)/shard_map/ppermute | solution.py:546
  51.1 13.7 %collective-permute-done.9.refs_12_ = bf16[2,224,128]{2,1,0:T(8,128)(2,1)S(1)} collective-permute-done((bf16[2,224,128]{2,1,0:T(8,128)(2,1)S(1)}, bf16[2,224,128]{2,1,0:T(8,128)(2,1)S(1)}, u32[]{:S(2)}, u32[]{:S(2)}) %collective-permute-start.9) | collective-permute-done | bytes 114720 | tf_op jit(solution)/shard_map/ppermute | solution.py:546
  65.6 5.6 %collective-permute-done.8.refs_11_ = bf16[2,224,128]{2,1,0:T(8,128)(2,1)S(1)} collective-permute-done((bf16[2,224,128]{2,1,0:T(8,128)(2,1)S(1)}, bf16[2,224,128]{2,1,0:T(8,128)(2,1)S(1)}, u32[]{:S(2)}, u32[]{:S(2)}) %collective-permute-start.8) | collective-permute-done | bytes 114720 | tf_op jit(solution)/shard_map/ppermute | solution.py:546
  71.2 6.0 %sound_zero.1.part = f32[4,224,512]{2,1,0:T(8,128)} custom-call(bf16[4,224,512]{2,1,0:T(8,128)(2,1)} %q0.3, bf16[512,256]{1,0:T(8,128)(2,1)} %get-tuple-element.44.refs_1_.esrc, bf16[224,896]{1,0:T(8,128)(2,1)} %get-tuple-element.45.refs_2_.gcat, bf16[256,512]{1,0:T(8,128)(2,1)} %get-tuple-element.46.refs_3_.edst, bf16[512,512]{1,0:T(8,128)(2,1)} %dx.3, ...), custom_call_target="tpu_custom_call" | custom-call | tf_op jit(solution)/shard_map/sound_zero/pallas_call | solution.py:41
  77.2 2.4 %flow_two.1.after = f32[5,4,128,128]{3,2,1,0:T(8,128)} custom-call(f32[5,4,128,128]{3,2,1,0:T(8,128)S(1)} %copy-done, f32[5,4,128,128]{3,2,1,0:T(8,128)S(1)} %copy-done.10, f32[5,128,128]{2,1,0:T(8,128)S(1)} %collective-permute-done.4.xbelow, f32[5,128,128]{2,1,0:T(8,128)S(1)} %collective-permute-done.5.xabove, ...), custom_call_target="tpu_custom_call" | custom-call | tf_op jit(solution)/shard_map/flow_two/pallas_call | solution.py:41
  79.7 2.9 %sources.1 = (f32[4,224,512]{2,1,0:T(8,128)S(1)}, bf16[3,224,512]{2,1,0:T(8,128)(2,1)S(1)}, bf16[2,224,128]{2,1,0:T(8,128)(2,1)S(1)}, bf16[2,224,128]{2,1,0:T(8,128)(2,1)S(1)}) custom-call(bf16[128,48,128]{2,1,0:T(8,128)(2,1)S(1)} %all-to-all-done.1.got, bf16[2,224,1024]{2,1,0:T(8,128)(2,1)} %get-tuple-element.43.pick, f32[4,224,512]{2,1,0:T(8,128)} %sound_zero.1.part, ...), custom_call_target="tpu_custom_call" | custom-call | tf_op jit(solution)/shard_map/sources/pallas_call | solution.py:41
  82.5 1.6 %collective-permute-start.11 = (bf16[2,224,128]{2,1,0:T(8,128)(2,1)S(1)}, bf16[2,224,128]{2,1,0:T(8,128)(2,1)S(1)}, u32[]{:S(2)}, u32[]{:S(2)}) collective-permute-start(bf16[2,224,128]{2,1,0:T(8,128)(2,1)S(1)} %get-tuple-element.49.r_2_), channel_id=1, source_target_pairs={{1,0},{2,1},{3,2},{4,3},{5,4},{6,5},{7,6},{8,7},{9,8},{10,9},{11,1... | collective-permute-start | bytes 344072 | tf_op jit(solution)/shard_map/ppermute | solution.py:546
  84.7 2.5 %sound_one.1.r_6_.mid = f32[4,224,512]{2,1,0:T(8,128)S(1)} custom-call(bf16[4,224,512]{2,1,0:T(8,128)(2,1)S(1)} %copy-done.1, f32[4,224,512]{2,1,0:T(8,128)S(1)} %get-tuple-element.51.q1, bf16[3,224,512]{2,1,0:T(8,128)(2,1)S(1)} %get-tuple-element.52.src, bf16[512,512]{1,0:T(8,128)(2,1)S(1)} %copy-done.2, bf16[512,512]{1,0:T(8,128)(2,1)S(1)} %copy-done.3, ...), custom_call_target="tpu_custom_call" | custom-call | tf_op jit(solution)/shard_map/sound_one/pallas_call | solution.py:41
  87.4 7.3 %collective-permute-done.10.r_4_ = bf16[2,224,128]{2,1,0:T(8,128)(2,1)S(1)} collective-permute-done((bf16[2,224,128]{2,1,0:T(8,128)(2,1)S(1)}, bf16[2,224,128]{2,1,0:T(8,128)(2,1)S(1)}, u32[]{:S(2)}, u32[]{:S(2)}) %collective-permute-start.10) | collective-permute-done | bytes 114720 | tf_op jit(solution)/shard_map/ppermute | solution.py:546
  95.3 2.0 %collective-permute-start.12 = (bf16[2,224,128]{2,1,0:T(8,128)(2,1)S(1)}, bf16[2,224,128]{2,1,0:T(8,128)(2,1)S(1)}, u32[]{:S(2)}, u32[]{:S(2)}) collective-permute-start(bf16[2,224,128]{2,1,0:T(8,128)(2,1)S(1)} %get-tuple-element.54.r_3_), channel_id=1, source_target_pairs={{0,1},{1,2},{2,3},{3,4},{4,5},{5,6},{6,7},{7,8},{8,9},{9,10},{10,1... | collective-permute-start | bytes 344072 | tf_op jit(solution)/shard_map/ppermute | solution.py:546
  97.3 3.4 %sound_two.1 = (f32[4,224,512]{2,1,0:T(8,128)}, f32[2,4,224,128]{3,2,1,0:T(8,128)S(1)}) custom-call(bf16[4,224,512]{2,1,0:T(8,128)(2,1)S(1)} %copy-done.1, f32[4,224,512]{2,1,0:T(8,128)S(1)} %sound_one.1.r_6_.mid, f32[2,4,224,128]{3,2,1,0:T(8,128)S(1)} %get-tuple-element.55.ends, bf16[3,224,512]{2,1,0:T(8,128)(2,1)S(1)} %get-tuple-element.52.src, ...), custom_call_target="tpu_custom_call" | custom-call | tf_op jit(solution)/shard_map/sound_two/pallas_call | solution.py:41
  100.7 5.2 %collective-permute-done.12.r_4_ = bf16[2,224,128]{2,1,0:T(8,128)(2,1)S(1)} collective-permute-done((bf16[2,224,128]{2,1,0:T(8,128)(2,1)S(1)}, bf16[2,224,128]{2,1,0:T(8,128)(2,1)S(1)}, u32[]{:S(2)}, u32[]{:S(2)}) %collective-permute-start.12) | collective-permute-done | bytes 114720 | tf_op jit(solution)/shard_map/ppermute | solution.py:546
  (59 shorter events, 7.2 us)
Async XLA Ops:
  0.6 21.4 %copy-start = (f32[5,4,128,128]{3,2,1,0:T(8,128)S(1)}, f32[5,4,128,128]{3,2,1,0:T(8,128)}, u32[]{:S(2)}) copy-start(f32[5,4,128,128]{3,2,1,0:T(8,128)} %u.7) | copy-start | bytes 3932164
  4.0 18.0 %collective-permute-start = (f32[5,128,128]{2,1,0:T(8,128)S(1)}, f32[5,128,128]{2,1,0:T(8,128)S(1)}, u32[]{:S(2)}, u32[]{:S(2)}) collective-permute-start(f32[5,128,128]{2,1,0:T(8,128)S(1)} %get-tuple-element.30), channel_id=1, source_target_pairs={{0,1},{1,2},{2,3},{3,4},{4,5},{5,6},{6,7},{7,8},{8,9},{9,10},{10,1... | collective-permute-start | bytes 983048 | tf_op jit(solution)/shard_map/ppermute | solution.py:546
  5.6 16.4 %collective-permute-start.1 = (f32[5,128,128]{2,1,0:T(8,128)S(1)}, f32[5,128,128]{2,1,0:T(8,128)S(1)}, u32[]{:S(2)}, u32[]{:S(2)}) collective-permute-start(f32[5,128,128]{2,1,0:T(8,128)S(1)} %get-tuple-element.31), channel_id=1, source_target_pairs={{1,0},{2,1},{3,2},{4,3},{5,4},{6,5},{7,6},{8,7},{9,8},{10,9},{11,1... | collective-permute-start | bytes 983048 | tf_op jit(solution)/shard_map/ppermute | solution.py:546
  12.8 9.3 %collective-permute-start.2 = (f32[128,128]{1,0:T(8,128)S(1)}, f32[128,128]{1,0:T(8,128)S(1)}, u32[]{:S(2)}, u32[]{:S(2)}) collective-permute-start(f32[128,128]{1,0:T(8,128)S(1)} %get-tuple-element.32), channel_id=1, source_target_pairs={{0,32},{32,64},{64,96},{96,0},{1,33},{33,65},{65,97},{97,1},{2,34}... | collective-permute-start | bytes 196616 | tf_op jit(solution)/shard_map/ppermute | solution.py:546
  12.8 9.3 %collective-permute-start.3 = (f32[128,128]{1,0:T(8,128)S(1)}, f32[128,128]{1,0:T(8,128)S(1)}, u32[]{:S(2)}, u32[]{:S(2)}) collective-permute-start(f32[128,128]{1,0:T(8,128)S(1)} %get-tuple-element.33), channel_id=1, source_target_pairs={{32,0},{64,32},{96,64},{0,96},{33,1},{65,33},{97,65},{1,97},{34,2}... | collective-permute-start | bytes 196616 | tf_op jit(solution)/shard_map/ppermute | solution.py:546
  14.5 14.3 %all-to-all-start = ((f32[128,1,128]{2,1,0:T(1,128)}), f32[128,1,128]{2,1,0:T(1,128)S(1)}, u32[]{:S(2)}, u32[]{:S(2)}) async-start(f32[128,1,128]{2,1,0:T(1,128)} %get-tuple-element.41), calls=%async_computation | async-start | bytes 131072 | tf_op jit(solution)/shard_map/all_to_all | solution.py:568
  22.0 8.8 %copy-start.13 = (f32[128,128]{1,0:T(8,128)}, f32[128,128]{1,0:T(8,128)S(1)}, u32[]{:S(2)}) copy-start(f32[128,128]{1,0:T(8,128)S(1)} %collective-permute-done.2.zbelow.zb) | copy-start | bytes 196612
  22.0 8.8 %copy-start.14 = (f32[128,128]{1,0:T(8,128)}, f32[128,128]{1,0:T(8,128)S(1)}, u32[]{:S(2)}) copy-start(f32[128,128]{1,0:T(8,128)S(1)} %collective-permute-done.3.zabove.za) | copy-start | bytes 196612
  22.0 8.8 %copy-start.11 = (f32[5,128,128]{2,1,0:T(8,128)}, f32[5,128,128]{2,1,0:T(8,128)S(1)}, u32[]{:S(2)}) copy-start(f32[5,128,128]{2,1,0:T(8,128)S(1)} %collective-permute-done.xbelow.xb) | copy-start | bytes 983044
  30.8 48.7 %all-to-all-start.1 = ((bf16[128,48,128]{2,1,0:T(8,128)(2,1)}), bf16[128,48,128]{2,1,0:T(8,128)(2,1)S(1)}, u32[]{:S(2)}, u32[]{:S(2)}) async-start(bf16[128,48,128]{2,1,0:T(8,128)(2,1)} %send.1), calls=%async_computation.1 | async-start | bytes 3145728 | tf_op jit(solution)/shard_map/all_to_all | solution.py:600
  37.1 11.9 %copy-start.18 = (bf16[2,224,128]{2,1,0:T(8,128)(2,1)S(1)}, bf16[2,224,128]{2,1,0:T(8,128)(2,1)}, u32[]{:S(2)}) copy-start(bf16[2,224,128]{2,1,0:T(8,128)(2,1)} %get-tuple-element.47.refs_9_) | copy-start | bytes 344068
  37.1 13.5 %copy-start.19 = (bf16[2,224,128]{2,1,0:T(8,128)(2,1)S(1)}, bf16[2,224,128]{2,1,0:T(8,128)(2,1)}, u32[]{:S(2)}) copy-start(bf16[2,224,128]{2,1,0:T(8,128)(2,1)} %get-tuple-element.48.refs_10_) | copy-start | bytes 344068
  41.2 35.9 %collective-permute-start.4 = (f32[5,128,128]{2,1,0:T(8,128)}, f32[5,128,128]{2,1,0:T(8,128)S(1)}, u32[]{:S(2)}, u32[]{:S(2)}) collective-permute-start(f32[5,128,128]{2,1,0:T(8,128)} %get-tuple-element.35), channel_id=1, source_target_pairs={{0,1},{1,2},{2,3},{3,4},{4,5},{5,6},{6,7},{7,8},{8,9},{9,10},{10,1... | collective-permute-start | bytes 983048 | tf_op jit(solution)/shard_map/ppermute | solution.py:546
  42.3 34.9 %collective-permute-start.5 = (f32[5,128,128]{2,1,0:T(8,128)}, f32[5,128,128]{2,1,0:T(8,128)S(1)}, u32[]{:S(2)}, u32[]{:S(2)}) collective-permute-start(f32[5,128,128]{2,1,0:T(8,128)} %get-tuple-element.36), channel_id=1, source_target_pairs={{1,0},{2,1},{3,2},{4,3},{5,4},{6,5},{7,6},{8,7},{9,8},{10,9},{11,1... | collective-permute-start | bytes 983048 | tf_op jit(solution)/shard_map/ppermute | solution.py:546
  49.1 15.7 %collective-permute-start.9 = (bf16[2,224,128]{2,1,0:T(8,128)(2,1)S(1)}, bf16[2,224,128]{2,1,0:T(8,128)(2,1)S(1)}, u32[]{:S(2)}, u32[]{:S(2)}) collective-permute-start(bf16[2,224,128]{2,1,0:T(8,128)(2,1)S(1)} %copy-done.18), channel_id=1, source_target_pairs={{1,0},{2,1},{3,2},{4,3},{5,4},{6,5},{7,6},{8,7},{9,8},{10,9},{11,1... | collective-permute-start | bytes 344072 | tf_op jit(solution)/shard_map/ppermute | solution.py:546
  50.7 20.5 %collective-permute-start.8 = (bf16[2,224,128]{2,1,0:T(8,128)(2,1)S(1)}, bf16[2,224,128]{2,1,0:T(8,128)(2,1)S(1)}, u32[]{:S(2)}, u32[]{:S(2)}) collective-permute-start(bf16[2,224,128]{2,1,0:T(8,128)(2,1)S(1)} %copy-done.19), channel_id=1, source_target_pairs={{0,1},{1,2},{2,3},{3,4},{4,5},{5,6},{6,7},{7,8},{8,9},{9,10},{10,1... | collective-permute-start | bytes 344072 | tf_op jit(solution)/shard_map/ppermute | solution.py:546
  51.1 26.1 %collective-permute-start.6 = (f32[128,128]{1,0:T(8,128)}, f32[128,128]{1,0:T(8,128)S(1)}, u32[]{:S(2)}, u32[]{:S(2)}) collective-permute-start(f32[128,128]{1,0:T(8,128)} %get-tuple-element.37), channel_id=1, source_target_pairs={{0,32},{32,64},{64,96},{96,0},{1,33},{33,65},{65,97},{97,1},{2,34}... | collective-permute-start | bytes 196616 | tf_op jit(solution)/shard_map/ppermute | solution.py:546
  64.8 12.4 %collective-permute-start.7 = (f32[128,128]{1,0:T(8,128)}, f32[128,128]{1,0:T(8,128)S(1)}, u32[]{:S(2)}, u32[]{:S(2)}) collective-permute-start(f32[128,128]{1,0:T(8,128)} %get-tuple-element.38), channel_id=1, source_target_pairs={{32,0},{64,32},{96,64},{0,96},{33,1},{65,33},{97,65},{1,97},{34,2}... | collective-permute-start | bytes 196616 | tf_op jit(solution)/shard_map/ppermute | solution.py:546
  82.5 4.9 %collective-permute-start.11 = (bf16[2,224,128]{2,1,0:T(8,128)(2,1)S(1)}, bf16[2,224,128]{2,1,0:T(8,128)(2,1)S(1)}, u32[]{:S(2)}, u32[]{:S(2)}) collective-permute-start(bf16[2,224,128]{2,1,0:T(8,128)(2,1)S(1)} %get-tuple-element.49.r_2_), channel_id=1, source_target_pairs={{1,0},{2,1},{3,2},{4,3},{5,4},{6,5},{7,6},{8,7},{9,8},{10,9},{11,1... | collective-permute-start | bytes 344072 | tf_op jit(solution)/shard_map/ppermute | solution.py:546
  84.2 10.5 %collective-permute-start.10 = (bf16[2,224,128]{2,1,0:T(8,128)(2,1)S(1)}, bf16[2,224,128]{2,1,0:T(8,128)(2,1)S(1)}, u32[]{:S(2)}, u32[]{:S(2)}) collective-permute-start(bf16[2,224,128]{2,1,0:T(8,128)(2,1)S(1)} %get-tuple-element.50.r_3_), channel_id=1, source_target_pairs={{0,1},{1,2},{2,3},{3,4},{4,5},{5,6},{6,7},{7,8},{8,9},{9,10},{10,1... | collective-permute-start | bytes 344072 | tf_op jit(solution)/shard_map/ppermute | solution.py:546
  84.7 10.0 %copy-start.8 = (bf16[224,448]{1,0:T(8,128)(2,1)S(1)}, bf16[224,448]{1,0:T(8,128)(2,1)}, u32[]{:S(2)}) copy-start(bf16[224,448]{1,0:T(8,128)(2,1)} %get-tuple-element.39.refs_7_.r_0_) | copy-start | bytes 602116
  84.7 10.0 %copy-start.9 = (bf16[224,448]{1,0:T(8,128)(2,1)S(1)}, bf16[224,448]{1,0:T(8,128)(2,1)}, u32[]{:S(2)}) copy-start(bf16[224,448]{1,0:T(8,128)(2,1)} %get-tuple-element.40.refs_8_.r_1_) | copy-start | bytes 602116
  95.2 5.5 %collective-permute-start.13 = (bf16[2,224,128]{2,1,0:T(8,128)(2,1)S(1)}, bf16[2,224,128]{2,1,0:T(8,128)(2,1)S(1)}, u32[]{:S(2)}, u32[]{:S(2)}) collective-permute-start(bf16[2,224,128]{2,1,0:T(8,128)(2,1)S(1)} %get-tuple-element.53.r_2_), channel_id=1, source_target_pairs={{1,0},{2,1},{3,2},{4,3},{5,4},{6,5},{7,6},{8,7},{9,8},{10,9},{11,1... | collective-permute-start | bytes 344072 | tf_op jit(solution)/shard_map/ppermute | solution.py:546
  95.3 10.6 %collective-permute-start.12 = (bf16[2,224,128]{2,1,0:T(8,128)(2,1)S(1)}, bf16[2,224,128]{2,1,0:T(8,128)(2,1)S(1)}, u32[]{:S(2)}, u32[]{:S(2)}) collective-permute-start(bf16[2,224,128]{2,1,0:T(8,128)(2,1)S(1)} %get-tuple-element.54.r_3_), channel_id=1, source_target_pairs={{0,1},{1,2},{2,3},{3,4},{4,5},{5,6},{6,7},{7,8},{8,9},{9,10},{10,1... | collective-permute-start | bytes 344072 | tf_op jit(solution)/shard_map/ppermute | solution.py:546
  (12 other events, 52.2 us)

commit v2 on v1

--- a/solution.py
+++ b/solution.py
@@ -64,6 +64,10 @@
         copy.wait()
 
 
+def is_even(axis):
+    return lax.rem(lax.axis_index(axis), 2) == 0
+
+
 def dma(n):
     return pltpu.SemaphoreType.DMA((n,))
 
@@ -127,52 +131,63 @@
     return out
 
 
-def store_traces(first_tiles, last_tiles, lo_ref, hi_ref):
-    for w, t in enumerate(pair_lanes(first_tiles, False)):
-        lo_ref[w] = t.astype(BF16)
-    for w, t in enumerate(pair_lanes(last_tiles, True)):
-        hi_ref[w] = t.astype(BF16)
-
-
-def edges_body(u, req, xlo, xhi, zlo, zhi, want, mid, sems):
+def store_traces(first_tiles, last_tiles, even_ref, odd_ref):
+    lower, upper = pair_lanes(first_tiles, False), pair_lanes(last_tiles, True)
+    even = is_even("space")
+    for w in range(2):
+        even_ref[w] = jnp.where(even, upper[w], lower[w]).astype(BF16)
+        odd_ref[w] = jnp.where(even, lower[w], upper[w]).astype(BF16)
+
+
+def edges_body(u, q, ue, uo, ze, zo, qe, qo, planes, ends, sems):
+    even = is_even("space")
     copies = begin(
         sems,
         0,
-        (u.at[:, 0], xlo),
-        (u.at[:, 3], xhi),
-        (u.at[:, 1], mid.at[0]),
-        (u.at[:, 2], mid.at[1]),
-    )
-    eye = iota((128, 128), 0) == iota((128, 128), 1)
-    value = req[...].astype(F32)
-    spread = [jnp.where(eye, value[c : c + 1], 0.0).astype(BF16) for c in range(4)]
-    place = jnp.where(iota((512, 128), 0) // 128 == iota((512, 128), 1), 1.0, 0.0).astype(BF16)
-    turned = jnp.dot(jnp.concatenate(spread, 1), place, preferred_element_type=F32)
-    want[...] = turned.reshape(128, 1, 128)
+        *[(u.at[:, x], planes.at[x]) for x in range(4)],
+        (q.at[:, :, 0:128], ends.at[0]),
+        (q.at[:, :, 384:512], ends.at[1]),
+        (u.at[:, jnp.where(even, 3, 0)], ue),
+        (u.at[:, jnp.where(even, 0, 3)], uo),
+    )
     lane = iota((128, 128), 1)
     lo = hi = jnp.zeros((128, 128), F32)
-    for x, plane, copy in ((0, xlo, 0), (3, xhi, 1), (1, mid.at[0], 2), (2, mid.at[1], 3)):
-        copies[copy].wait()
-        rows = [plane[f] for f in range(5)]
+    for x in range(4):
+        copies[x].wait()
+        rows = [planes[x, f] for f in range(5)]
         v, p = primitives(rows)
         lo, hi = add_columns(x, flux(rows, v, p, 2) + [v[0], v[1]], lane, lo, hi)
-    zlo[...] = lo
-    zhi[...] = hi
-
-
-def lamb_body(u, xbelow, xabove, zbelow, zabove, table, vel, pooled):
+    even = is_even("solver")
+    ze[...] = jnp.where(even, hi, lo)
+    zo[...] = jnp.where(even, lo, hi)
+    finish(copies[4:6])
+    store_traces(
+        [ends[0, v].astype(F32) for v in range(4)],
+        [ends[1, v].astype(F32) for v in range(4)],
+        qe,
+        qo,
+    )
+    finish(copies[6:])
+
+
+def lamb_body(u, xe, xo, ze, zo, table, vel, pooled):
     lane = iota((128, 128), 1)
-    for x in range(-1, 5):
-        if x == -1:
-            r, m = xbelow[0], [xbelow[c] for c in (1, 2, 3)]
-        elif x == 4:
-            r, m = xabove[0], [xabove[c] for c in (1, 2, 3)]
-        else:
-            r, m = u[0, x], [u[c, x] for c in (1, 2, 3)]
-        inv = 1.0 / r
+    for x in range(4):
+        inv = 1.0 / u[0, x]
         for c in range(3):
-            vel[c, x + 1] = m[c] * inv
-    below, above = zbelow[...], zabove[...]
+            vel[c, x + 1] = u[1 + c, x] * inv
+    even = is_even("space")
+    by_link = []
+    for link in (xe, xo):
+        inv = 1.0 / link[0]
+        by_link.append([link[1 + c] * inv for c in (1, 2)])
+    for c in (1, 2):
+        by_even, by_odd = by_link[0][c - 1], by_link[1][c - 1]
+        vel[c, 0] = jnp.where(even, by_odd, by_even)
+        vel[c, 5] = jnp.where(even, by_even, by_odd)
+    even = is_even("solver")
+    below = jnp.where(even, zo[...], ze[...])
+    above = jnp.where(even, ze[...], zo[...])
     for pair in range(2):
         total = None
         for x in (2 * pair, 2 * pair + 1):
@@ -219,27 +234,29 @@
     return rows, out
 
 
-def fill_flux_a(u, xbelow, xabove, fa, planes=range(-1, 5)):
-    for x in planes:
-        if x == -1:
-            rows = [xbelow[f] for f in range(5)]
-        elif x == 4:
-            rows = [xabove[f] for f in range(5)]
-        else:
-            rows = [u[f, x] for f in range(5)]
+def fill_flux_a(planes, fa):
+    for x, rows in planes:
         v, p = primitives(rows)
         for f, t in enumerate(flux(rows, v, p, 0)):
             fa[f, x + 1] = t
 
 
-def stage_one_body(u, xbelow, xabove, zbelow, zabove, first, xlo, xhi, zlo, zhi, fa, hold, zpack, halo, zhalo, sems):
+def inner_planes(u):
+    return [(x, [u[f, x] for f in range(5)]) for x in range(4)]
+
+
+def stage_one_body(u, ue, uo, ze, zo, first, ce, co, ye, yo, *scratch):
+    fa, hold, edge, zpack, halo, zhalo, sems = scratch
     lane = iota((128, 128), 1)
+    even, even_z = is_even("space"), is_even("solver")
+    e, o = jnp.where(even, 1, 0), jnp.where(even, 0, 1)
+    ez, oz = jnp.where(even_z, 1, 0), jnp.where(even_z, 0, 1)
     fetch = begin(
-        sems, 8, (xbelow, halo.at[0]), (xabove, halo.at[1]), (zbelow, zhalo.at[0]), (zabove, zhalo.at[1])
-    )
-    fill_flux_a(u, None, None, fa, range(4))
+        sems, 8, (ue, halo.at[e]), (uo, halo.at[o]), (ze, zhalo.at[ez]), (zo, zhalo.at[oz])
+    )
+    fill_flux_a(inner_planes(u), fa)
     finish(fetch)
-    fill_flux_a(u, halo.at[0], halo.at[1], fa, (-1, 4))
+    fill_flux_a([(x, [halo[i, f] for f in range(5)]) for i, x in enumerate((-1, 4))], fa)
     below, above = zhalo[0], zhalo[1]
     lo = hi = jnp.zeros((128, 128), F32)
     copies = []
@@ -257,19 +274,37 @@
             hold[x, f] = now[f]
         copies += begin(sems, i, (hold.at[x], first.at[:, x]))
         if x in (0, 3):
-            copies += begin(sems, 4 + i, (hold.at[x], xhi if x else xlo))
+            for f in range(5):
+                edge[i, f] = ((-FLOW_STEP * 0.5) * out[f]).astype(BF16)
         v, p = primitives(now)
         lo, hi = add_columns(x, flux(now, v, p, 2), lane, lo, hi)
     zpack[0] = lo
     zpack[1] = hi
-    copies += begin(sems, 6, (zpack.at[0], zlo), (zpack.at[1], zhi))
+    copies += begin(
+        sems, 4, (edge.at[e], ce), (edge.at[o], co), (zpack.at[ez], ye), (zpack.at[oz], yo)
+    )
     finish(copies)
 
 
-def stage_two_body(u, first, xbelow, xabove, zbelow, zabove, inc, fa, hold, sems):
+def stage_two_body(u, first, ue, uo, ce, co, ze, zo, after, inc, *scratch):
+    fa, hold, halo, sems = scratch
     lane = iota((128, 128), 1)
-    fill_flux_a(first, xbelow, xabove, fa)
-    below, above = zbelow[...], zabove[...]
+    even, even_z = is_even("space"), is_even("solver")
+    e, o = jnp.where(even, 1, 0), jnp.where(even, 0, 1)
+    fetch = begin(sems, 4, (ue, halo.at[e]), (uo, halo.at[o]))
+    fill_flux_a(inner_planes(first), fa)
+    finish(fetch)
+    outer = []
+    for i, x in enumerate((-1, 4)):
+        rows = []
+        for f in range(5):
+            by_even, by_odd = ce[f].astype(F32), co[f].astype(F32)
+            change = jnp.where(even, by_odd, by_even) if i == 0 else jnp.where(even, by_even, by_odd)
+            rows.append(halo[i, f] + change)
+        outer.append((x, rows))
+    fill_flux_a(outer, fa)
+    below = jnp.where(even_z, zo[...], ze[...])
+    above = jnp.where(even_z, ze[...], zo[...])
     copies = []
     for x in range(4):
         rows, out = tendency_plane(
@@ -287,7 +322,7 @@
 
 
 def send_body(req, table, send, hold, sems):
-    wanted = req[...].reshape(128, 128).astype(BF16)
+    wanted = req[...].reshape(128, 128).astype(F32).astype(BF16)
     row, col = iota((1024, 128), 0), iota((1024, 128), 1)
     spread = jnp.where(row // 8 == col, 1.0, 0.0).astype(BF16)
     rep = jnp.dot(spread, wanted, preferred_element_type=F32)
@@ -296,12 +331,14 @@
     target = value + ((row % 8) // 4 * 16).astype(F32)
     pick = jnp.where(col.astype(F32) == target, 1.0, 0.0).astype(BF16)
     copies = []
-    for u in range(3):
-        rows = jnp.dot(pick, table[:, 256 * u : 256 * u + 256], preferred_element_type=F32)
+    for part in range(3):
+        rows = jnp.dot(
+            pick, table[:, 256 * part : 256 * part + 256], preferred_element_type=F32
+        )
         a = rows[:, 0:128].reshape(128, 8, 128)
         b = rows[:, 128:256].reshape(128, 8, 128)
-        hold[u] = jnp.concatenate([a, b], 1).astype(BF16)
-        copies += begin(sems, u, (hold.at[u], send.at[:, 16 * u : 16 * u + 16, :]))
+        hold[part] = jnp.concatenate([a, b], 1).astype(BF16)
+        copies += begin(sems, part, (hold.at[part], send.at[:, 16 * part : 16 * part + 16, :]))
     finish(copies)
 
 
@@ -319,14 +356,17 @@
     return jnp.concatenate([even[:, 0:128], odd[:, 0:128], even[:, 128:256], odd[:, 128:256]], 1)
 
 
-def prepare_body(nb, slot, q, gcat, gx0, gx1, pick, esrc, edst, qlo, qhi, *scratch):
-    gcat_v, gx0_v, gx1_v, pick_v, esrc_v, edst_v, ends, packs, sems = scratch
-    fetch = begin(sems, 0, (q.at[:, :, 0:128], ends.at[0]), (q.at[:, :, 384:512], ends.at[1]))
+def prepare_body(nb_far, slot_far, after, gcat, ge, go, pick, esrc, edst, *scratch):
+    gcat_v, gx0_v, gx1_v, pick_v, esrc_v, edst_v, nb, slot, sems = scratch
+    fetch = begin(sems, 0, (nb_far, nb), (slot_far, slot))
     me = lax.axis_index("solver") * lax.axis_size("space") + lax.axis_index("space")
+    finish(fetch)
     owner, row = nb[...] // EL, nb[...] % EL
     away = jnp.where(owner == me, 0, EL)
     spot = slot[...] // 4 * 8 + slot[...] % 4
     cols = [row[f : f + 1] + away[f : f + 1] for f in range(2)]
+    even = is_even("space")
+    cols = [jnp.where(even, cols[1], cols[0]), jnp.where(even, cols[0], cols[1])]
     cols += [row[f : f + 1] for f in range(2, 6)] + [spot]
     eye = iota((EL, EL), 0) == iota((EL, EL), 1)
     spread = [jnp.where(eye, c.astype(F32), 0.0) for c in cols]
@@ -347,7 +387,7 @@
 
     onehot(gx0_v, 0, 2 * EL)
     onehot(gx1_v, 1, 2 * EL)
-    copies = begin(sems, 2, (gx0_v, gx0), (gx1_v, gx1))
+    copies = begin(sems, 2, (gx0_v, ge), (gx1_v, go))
     for t in range(0, 4 * EL, 128):
         hit = jnp.zeros((EL, 128), jnp.bool_)
         for f in range(4):
@@ -357,11 +397,6 @@
     onehot(pick_v.at[0], 6, 1024)
     onehot(pick_v.at[1], 6, 1024, 4.0)
     copies += begin(sems, 5, (pick_v, pick))
-    finish(fetch)
-    store_traces(
-        [ends[0, v].astype(F32) for v in range(4)], [ends[1, v].astype(F32) for v in range(4)], packs.at[0], packs.at[1]
-    )
-    copies += begin(sems, 8, (packs.at[0], qlo), (packs.at[1], qhi))
 
     def node(c, flip):
         face, a, b = c // 64, c % 64 // 8, c % 8
@@ -377,12 +412,6 @@
     ).astype(BF16)
     copies += begin(sems, 6, (esrc_v, esrc), (edst_v, edst))
     finish(copies)
-
-
-def lamb_and_prepare_body(u, xb, xa, zb, za, nb, slot, q, table, *rest):
-    vel, pooled = rest[8:10]
-    lamb_body(u, xb, xa, zb, za, table, vel, pooled)
-    prepare_body(nb, slot, q, *rest[:8], *rest[10:])
 
 
 def face_count():
@@ -420,17 +449,16 @@
     return out
 
 
-def cross_terms(gx0, gx1, own_lo, own_hi, below_hi, above_lo):
+def cross_terms(ge, go, own_e, own_o, got_e, got_o):
     lane = iota((EL, 128), 1)
     first, last = [], []
-    low = jnp.concatenate(
-        [jnp.concatenate([own_hi[w], below_hi[w]], 0) for w in range(2)], 1
-    )
-    high = jnp.concatenate(
-        [jnp.concatenate([own_lo[w], above_lo[w]], 0) for w in range(2)], 1
-    )
-    low = jnp.dot(gx0[...], low, preferred_element_type=F32)
-    high = jnp.dot(gx1[...], high, preferred_element_type=F32)
+    by_even = jnp.concatenate([jnp.concatenate([own_o[w], got_e[w]], 0) for w in range(2)], 1)
+    by_odd = jnp.concatenate([jnp.concatenate([own_e[w], got_o[w]], 0) for w in range(2)], 1)
+    by_even = jnp.dot(ge[...], by_even, preferred_element_type=F32)
+    by_odd = jnp.dot(go[...], by_odd, preferred_element_type=F32)
+    even = is_even("space")
+    low = jnp.where(even, by_odd, by_even)
+    high = jnp.where(even, by_even, by_odd)
     for v in range(4):
         w = v // 2
         a = low[:, w * 128 : (w + 1) * 128]
@@ -445,7 +473,7 @@
 
 
 def sound_zero_body(*refs):
-    given, (bhi, alo, part, *here), (hold, sems) = refs[:11], refs[11:25], refs[25:]
+    given, (bhi, alo, after, part, *here), (hold, sems) = refs[:11], refs[11:26], refs[26:]
     coming = {id(to): copy for to, copy in zip(here, begin(sems, 4, *zip(given, here)))}
     ready = lambda *names: finish([coming[id(t)] for t in names])
     q, esrc, gcat, edst, dx, dy, dz, gx0, gx1, olo, ohi = here
@@ -469,13 +497,15 @@
     finish(copies)
 
 
-def sources_body(got, pick, part, after, q1, src, lo, hi, pick_v, part_v, sems):
+def sources_body(got, pick, part, q1, src, lo, hi, token, pick_v, part_v, token_v, sems):
+    token_v[...] = jnp.zeros_like(token_v)
     copies = begin(
         sems,
         0,
         (pick, pick_v),
         (part.at[0], q1.at[0]),
         *[(part.at[v], part_v.at[v - 1]) for v in (1, 2, 3)],
+        (token_v, token),
     )
     copies[0].wait()
     for c in range(3):
@@ -484,6 +514,7 @@
         copies[2 + c].wait()
         q1[1 + c] = part_v[c] + SOUND_STEP * s
     copies[1].wait()
+    copies[5].wait()
     store_traces(
         [q1[v, :, 0:128] for v in range(4)],
         [q1[v, :, 384:512] for v in range(4)],
@@ -492,7 +523,7 @@
     )
 
 
-def sound_one_body(q0, q1, src, dx, dy, dz, gcat, esrc, edst, part):
+def sound_one_body(q0, q1, src, dx, dy, dz, gcat, esrc, edst, after, part):
     terms = local_terms([q1[v].astype(BF16) for v in range(4)], dx, dy, dz, gcat, esrc, edst)
     for v in range(4):
         t = terms[v] if v == 0 else terms[v] + src[v - 1].astype(F32)
@@ -539,11 +570,12 @@
     finish(copies)
 
 
-def neighbour_pair(low_going, high_going, axis):
+def swap(even, odd, axis):
     count = lax.axis_size(axis)
-    up = [(i, (i + 1) % count) for i in range(count)]
-    down = [(b, a) for a, b in up]
-    return lax.ppermute(high_going, axis, up), lax.ppermute(low_going, axis, down)
+    by_even = [(i, i + 1 - 2 * (i % 2)) for i in range(count)]
+    by_odd = [(i, (i - 1 + 2 * (i % 2)) % count) for i in range(count)]
+    other = lax.ppermute(odd, axis, by_odd)
+    return lax.ppermute(even, axis, by_even), other
 
 
 def local(flow_state, acoustic_state, dx, dy, dz, requests, elem_slot, neighbours):
@@ -555,40 +587,29 @@
     keep = lambda *shape: pltpu.VMEM(shape, F32)
     keep_half = lambda *shape: pltpu.VMEM(shape, BF16)
 
-    xlo, xhi, zlo, zhi, wanted = call(
+    wanted = jnp.pad(requests.reshape(128, 1, 4), ((0, 0), (0, 0), (0, 124)))
+    wanted = lax.all_to_all(wanted, both, split_axis=0, concat_axis=0, tiled=True)
+    packs = call(
         edges_body,
-        [plane, plane, column, column, full(128, 1, 128)],
+        [plane, plane, column, column] + traces,
         "edges",
-        (flow_state, requests.reshape(128, 4).T),
-        scratch=[keep(2, 5, 128, 128), dma(4)],
-        far=(0,),
-    )
-    xbelow, xabove = neighbour_pair(xlo, xhi, "space")
-    zbelow, zabove = neighbour_pair(zlo, zhi, "solver")
-    wanted = lax.all_to_all(wanted, both, split_axis=0, concat_axis=0, tiled=True)
-
-    shapes = [(EL, 4 * EL), (EL, 2 * EL), (EL, 2 * EL), (2, EL, 1024), (512, 256), (256, 512)]
-    table, gcat, gx0, gx1, pick, esrc, edst, qlo, qhi = call(
-        lamb_and_prepare_body,
-        [half(128, 768)] + [half(*t) for t in shapes] + traces,
+        (flow_state, acoustic_state),
+        scratch=[keep(4, 5, 128, 128), keep_half(2, 4, EL, 128), dma(8)],
+        far=(0, 1),
+    )
+    ue, uo, ze, zo, qe, qo = packs
+    ue, uo = swap(ue, uo, "space")
+    ze, zo = swap(ze, zo, "solver")
+    got_qe, got_qo = swap(qe, qo, "space")
+
+    table = call(
+        lamb_body,
+        half(128, 768),
         "lamb",
-        (flow_state, xbelow, xabove, zbelow, zabove, neighbours, elem_slot.reshape(1, EL), acoustic_state),
-        scratch=[keep(3, 6, 128, 128), keep(6, 128, 128)]
-        + [keep_half(*t) for t in shapes]
-        + [keep_half(2, 4, EL, 128), keep_half(2, 2, EL, 128), dma(10)],
-        far=(7,),
-        far_out=range(1, 9),
-    )
-    bhi, alo = neighbour_pair(qlo, qhi, "space")
-    first, xlo, xhi, zlo, zhi = call(
-        stage_one_body,
-        [grid, plane, plane, column, column],
-        "flow_one",
-        (flow_state, xbelow, xabove, zbelow, zabove),
-        scratch=[keep(5, 6, 128, 128), keep(4, 5, 128, 128), keep(2, 128, 128), keep(2, 5, 128, 128), keep(2, 128, 128), dma(12)],
-        far=(1, 2, 3, 4),
-        far_out=range(5),
-    )
+        (flow_state, ue, uo, ze, zo),
+        scratch=[keep(3, 6, 128, 128), keep(6, 128, 128)],
+    )
+    table, got_qe, got_qo = lax.optimization_barrier((table, got_qe, got_qo))
     send = call(
         send_body,
         half(128, 48, 128),
@@ -599,45 +620,81 @@
     )
     got = lax.all_to_all(send, both, split_axis=0, concat_axis=0, tiled=True)
 
-    xbelow, xabove = neighbour_pair(xlo, xhi, "space")
-    zbelow, zabove = neighbour_pair(zlo, zhi, "solver")
-    mats = (dx, dy, dz, gcat, esrc, edst)
-    given = (acoustic_state, esrc, gcat, edst, dx, dy, dz, gx0, gx1, qlo, qhi)
+    shapes = [(EL, 4 * EL), (EL, 2 * EL), (EL, 2 * EL), (2, EL, 1024), (512, 256), (256, 512)]
+    gcat, ge, go, pick, esrc, edst = call(
+        prepare_body,
+        [half(*t) for t in shapes],
+        "prepare",
+        (neighbours, elem_slot.reshape(1, EL), send),
+        scratch=[keep_half(*t) for t in shapes] + [pltpu.VMEM((6, EL), I32), pltpu.VMEM((1, EL), I32), dma(8)],
+        far=(0, 1, 2),
+        far_out=range(6),
+    )
+    first, ce, co, ye, yo = call(
+        stage_one_body,
+        [grid] + [half(5, 128, 128)] * 2 + [column, column],
+        "flow_one",
+        (flow_state, ue, uo, ze, zo),
+        scratch=[
+            keep(5, 6, 128, 128),
+            keep(4, 5, 128, 128),
+            keep_half(2, 5, 128, 128),
+            keep(2, 128, 128),
+            keep(2, 5, 128, 128),
+            keep(2, 128, 128),
+            dma(12),
+        ],
+        far=range(1, 5),
+        far_out=range(5),
+    )
+    ce, co = swap(ce, co, "space")
+    ye, yo = swap(ye, yo, "solver")
+
+    given = (acoustic_state, esrc, gcat, edst, dx, dy, dz, ge, go, qe, qo)
     part = call(
         sound_zero_body,
         state,
         "sound_zero",
-        given + (bhi, alo),
+        given + (got_qe, got_qo, first),
         scratch=[keep_half(*t.shape) for t in given] + [keep(4, EL, NODES), dma(15)],
-        far=range(11),
+        far=[*range(11), 13],
         far_out=(0,),
     )
+
+    q1, src, qe, qo, token = call(
+        sources_body,
+        [state, half(3, EL, NODES)] + traces + [full(8, 128)],
+        "sources",
+        (got, pick, part),
+        scratch=[keep_half(2, EL, 1024), keep(3, EL, NODES), keep(8, 128), dma(6)],
+        far=(1, 2),
+        far_out=(4,),
+    )
+    mats = (dx, dy, dz, gcat, esrc, edst)
+    got_qe, got_qo = swap(qe, qo, "space")
     flow_increment = call(
         stage_two_body,
         grid,
         "flow_two",
-        (flow_state, first, xbelow, xabove, zbelow, zabove),
-        scratch=[keep(5, 6, 128, 128), keep(4, 5, 128, 128), dma(4)],
+        (flow_state, first, ue, uo, ce, co, ye, yo, token),
+        scratch=[keep(5, 6, 128, 128), keep(4, 5, 128, 128), keep(2, 5, 128, 128), dma(6)],
+        far=(2, 3, 8),
         far_out=(0,),
     )
-
-    q1, src, qlo, qhi = call(
-        sources_body,
-        [state, half(3, EL, NODES)] + traces,
-        "sources",
-        (got, pick, part, flow_increment),
-        scratch=[keep_half(2, EL, 1024), keep(3, EL, NODES), dma(5)],
-        far=(1, 2, 3),
-    )
-    bhi, alo = neighbour_pair(qlo, qhi, "space")
-    part = call(sound_one_body, state, "sound_one", (acoustic_state, q1, src) + mats)
-    ends, qlo, qhi = call(
+    part = call(
+        sound_one_body,
+        state,
+        "sound_one",
+        (acoustic_state, q1, src) + mats + (flow_increment,),
+        far=(9,),
+    )
+    ends, qe, qo = call(
         lambda *r: cross_body(0.25 * SOUND_STEP, *r),
         [full(2, 4, EL, 128)] + traces,
         "cross_one",
-        (gx0, gx1, qlo, qhi, bhi, alo, part),
-    )
-    bhi, alo = neighbour_pair(qlo, qhi, "space")
+        (ge, go, qe, qo, got_qe, got_qo, part),
+    )
+    got_qe, got_qo = swap(qe, qo, "space")
     out, rest = call(
         sound_two_body,
         [state, full(2, 4, EL, 128)],
@@ -650,7 +707,7 @@
         lambda *r: final_body(2.0 / 3.0 * SOUND_STEP, *r),
         state,
         "cross_two",
-        (gx0, gx1, qlo, qhi, bhi, alo, rest, out),
+        (ge, go, qe, qo, got_qe, got_qo, rest, out),
         scratch=[keep(2, 4, EL, 128), dma(8)],
         far=(7,),
         far_out=(0,),

time: 108 us -> 98.4 us (0.911)
  waiting for transfers between devices: 36.2 us -> 20.4 us
  starting transfers between devices: 36.8 us -> 42.4 us
  Pallas kernels: 31 us -> 32.8 us
  local copies, waits for them, and re-layouts: 2.26 us -> 0.9 us
    ppermute x14, waiting for transfers between devices: 34.3 us -> 10.3 us  [the longest x7 10.2 us: swap(): other = lax.ppermute(odd, axis, by_odd)]
    all_to_all x1, waiting for transfers between devices: 1.92 us -> 7.82 us  [local(): lax.all_to_all(wanted, both, split_axis=0, concat_axis=0, tiled=True)]
    all_to_all x1, starting transfers between devices: 5.11 us -> 9.11 us  [local(): lax.all_to_all(wanted, both, split_axis=0, concat_axis=0, tiled=True)]
    ppermute x14, starting transfers between devices: 25.4 us -> 28.7 us  [the longest x7 25.3 us: swap(): other = lax.ppermute(odd, axis, by_odd)]
    all_to_all x1, waiting for transfers between devices: 0.01 us -> 2.37 us  [local(): got = lax.all_to_all(send, both, split_axis=0, concat_axis=0, tiled=True)]
    unnamed x40 -> x47, local copies, waits for them, and re-layouts: 2.26 us -> 0.22 us
    pallas_call x11 -> x12, Pallas kernels: 31 us -> 32.8 us  [call(): pl.pallas_call(body, out_shape=outs if many else outs[0], in_specs=[space...]
    all_to_all x1, starting transfers between devices: 6.3 us -> 4.66 us  [local(): got = lax.all_to_all(send, both, split_axis=0, concat_axis=0, tiled=True)]
  transfers between devices with their start and end apart: 16 -> 16, of which waited for: 7 -> 5; matrix products, arithmetic and copies ran while one was open for 0% -> 1% of each run, Pallas kernels for 20% -> 27%
where the time goes in v2:
time: 98.4 us; the launch traced here: 97.9 us
  starting transfers between devices  42.4 us (43%)
  Pallas kernels  32.8 us (33%)
  waiting for transfers between devices  20.4 us (21%)
  between operations  1.28 us (1%)
    pallas_call x12, Pallas kernels, call(): pl.pallas_call(body, out_shape=outs if many else outs[0], in_specs=[space...  32.8 us
    ppermute x7, starting transfers between devices, swap(): other = lax.ppermute(odd, axis, by_odd)  25.3 us
    ppermute x7, waiting for transfers between devices, swap(): other = lax.ppermute(odd, axis, by_odd)  10.2 us
    all_to_all x1, starting transfers between devices, local(): lax.all_to_all(wanted, both, split_axis=0, concat_axis=0, tiled=True)  9.11 us
    all_to_all x1, waiting for transfers between devices, local(): lax.all_to_all(wanted, both, split_axis=0, concat_axis=0, tiled=True)  7.82 us
    all_to_all x1, starting transfers between devices, local(): got = lax.all_to_all(send, both, split_axis=0, concat_axis=0, tiled=True)  4.66 us
    ppermute x7, starting transfers between devices, swap(): return (lax.ppermute(even, axis, by_even), other)  3.31 us
    all_to_all x1, waiting for transfers between devices, local(): got = lax.all_to_all(send, both, split_axis=0, concat_axis=0, tiled=True)  2.37 us
  transfers between devices with their start and end apart: 16, of which 5 were waited for; matrix products, arithmetic and copies ran while one was open for 1% of the time, Pallas kernels for 27%

profile of v2, /device:TPU:0, one launch (start us, length us, event | category | flops | bytes accessed | tf_op | source)
XLA Modules:
  0.0 97.9 jit_solution(5686736843988060886)
XLA Ops:
  0.6 2.5 %edges.1 = (f32[5,128,128]{2,1,0:T(8,128)S(1)}, f32[5,128,128]{2,1,0:T(8,128)S(1)}, f32[128,128]{1,0:T(8,128)S(1)}, f32[128,128]{1,0:T(8,128)S(1)}, bf16[2,224,1...) custom-call(f32[5,4,128,128]{3,2,1,0:T(8,128)} %u.7, bf16[4,224,512]{2,1,0:T(8,128)(2,1)} %q0.3), custom_call_target="tpu_custom_call" | custom-call | tf_op jit(solution)/shard_map/edges/pallas_call | solution.py:41
  3.2 1.7 %collective-permute-start = (f32[5,128,128]{2,1,0:T(8,128)S(1)}, f32[5,128,128]{2,1,0:T(8,128)S(1)}, u32[]{:S(2)}, u32[]{:S(2)}) collective-permute-start(f32[5,128,128]{2,1,0:T(8,128)S(1)} %get-tuple-element.32), channel_id=1, source_target_pairs={{0,1},{1,0},{2,3},{3,2},{4,5},{5,4},{6,7},{7,6},{8,9},{9,8},{10,11... | collective-permute-start | bytes 983048 | tf_op jit(solution)/shard_map/ppermute | solution.py:578
  4.8 7.9 %collective-permute-start.1 = (f32[5,128,128]{2,1,0:T(8,128)S(1)}, f32[5,128,128]{2,1,0:T(8,128)S(1)}, u32[]{:S(2)}, u32[]{:S(2)}) collective-permute-start(f32[5,128,128]{2,1,0:T(8,128)S(1)} %get-tuple-element.33), channel_id=1, source_target_pairs={{0,31},{1,2},{2,1},{3,4},{4,3},{5,6},{6,5},{7,8},{8,7},{9,10},{10,... | collective-permute-start | bytes 983048 | tf_op jit(solution)/shard_map/ppermute | solution.py:577
  12.7 1.2 %collective-permute-start.9 = (bf16[2,224,128]{2,1,0:T(8,128)(2,1)S(1)}, bf16[2,224,128]{2,1,0:T(8,128)(2,1)S(1)}, u32[]{:S(2)}, u32[]{:S(2)}) collective-permute-start(bf16[2,224,128]{2,1,0:T(8,128)(2,1)S(1)} %get-tuple-element.42.refs_10_), channel_id=1, source_target_pairs={{0,31},{1,2},{2,1},{3,4},{4,3},{5,6},{6,5},{7,8},{8,7},{9,10},{10,... | collective-permute-start | bytes 344072 | tf_op jit(solution)/shard_map/ppermute | solution.py:577
  15.5 9.1 %all-to-all-start = ((s32[128,1,128]{2,1,0:T(1,128)}), s32[128,1,128]{2,1,0:T(1,128)S(1)}, u32[]{:S(2)}, u32[]{:S(2)}) async-start(s32[128,1,128]{2,1,0:T(1,128)} %pad.4), calls=%async_computation | async-start | bytes 131072 | tf_op jit(solution)/shard_map/all_to_all | solution.py:591
  25.0 1.0 %lamb.1.table = bf16[128,768]{1,0:T(8,128)(2,1)S(1)} custom-call(f32[5,4,128,128]{3,2,1,0:T(8,128)S(1)} %copy-done, f32[5,128,128]{2,1,0:T(8,128)S(1)} %collective-permute-done.ue.xe, f32[5,128,128]{2,1,0:T(8,128)S(1)} %collective-permute-done.1.uo.xo, f32[128,128]{1,0:T(8,128)S(1)} %collective-permute-done.2.ze, f32[128,128]{1,0:T(8,128)S(1)} %collective-permute-done.3.zo), custom_call_target="tpu_custom_call" | custom-call | tf_op jit(solution)/shard_map/lamb/pallas_call | solution.py:41
  26.0 7.8 %all-to-all-done.req = s32[128,1,128]{2,1,0:T(1,128)S(1)} async-done(((s32[128,1,128]{2,1,0:T(1,128)}), s32[128,1,128]{2,1,0:T(1,128)S(1)}, u32[]{:S(2)}, u32[]{:S(2)}) %all-to-all-start) | async-done | bytes 65568 | tf_op jit(solution)/shard_map/all_to_all | solution.py:591
  33.8 2.0 %send.1.after = bf16[128,48,128]{2,1,0:T(8,128)(2,1)} custom-call(s32[128,1,128]{2,1,0:T(1,128)S(1)} %all-to-all-done.req, bf16[128,768]{1,0:T(8,128)(2,1)S(1)} %lamb.1.table), custom_call_target="tpu_custom_call" | custom-call | tf_op jit(solution)/shard_map/send/pallas_call | solution.py:41
  35.9 4.7 %all-to-all-start.1 = ((bf16[128,48,128]{2,1,0:T(8,128)(2,1)}), bf16[128,48,128]{2,1,0:T(8,128)(2,1)S(1)}, u32[]{:S(2)}, u32[]{:S(2)}) async-start(bf16[128,48,128]{2,1,0:T(8,128)(2,1)} %send.1.after), calls=%async_computation.1 | async-start | bytes 3145728 | tf_op jit(solution)/shard_map/all_to_all | solution.py:621
  40.6 4.1 %flow_one.1 = (f32[5,4,128,128]{3,2,1,0:T(8,128)}, bf16[5,128,128]{2,1,0:T(8,128)(2,1)}, bf16[5,128,128]{2,1,0:T(8,128)(2,1)}, f32[128,128]{1,0:T(8,128)}, f32[128,128]{1,0:T(8,128)}) custom-call(f32[5,4,128,128]{3,2,1,0:T(8,128)S(1)} %copy-done, f32[5,128,128]{2,1,0:T(8,128)} %copy-done.7, f32[5,128,128]{2,1,0:T(8,128)} %copy-done.8, ...), custom_call_target="tpu_custom_call" | custom-call | tf_op jit(solution)/shard_map/flow_one/pallas_call | solution.py:41
  44.7 0.9 collective-permute-start.4
  45.6 7.3 %collective-permute-start.5 = (bf16[5,128,128]{2,1,0:T(8,128)(2,1)}, bf16[5,128,128]{2,1,0:T(8,128)(2,1)S(1)}, u32[]{:S(2)}, u32[]{:S(2)}) collective-permute-start(bf16[5,128,128]{2,1,0:T(8,128)(2,1)} %get-tuple-element.38), channel_id=1, source_target_pairs={{0,31},{1,2},{2,1},{3,4},{4,3},{5,6},{6,5},{7,8},{8,7},{9,10},{10,... | collective-permute-start | bytes 491528 | tf_op jit(solution)/shard_map/ppermute | solution.py:577
  53.0 3.2 %prepare.1 = (bf16[224,896]{1,0:T(8,128)(2,1)}, bf16[224,448]{1,0:T(8,128)(2,1)}, bf16[224,448]{1,0:T(8,128)(2,1)}, bf16[2,224,1024]{2,1,0:T(8,128)(2,1)}, bf16[...) custom-call(s32[6,224]{1,0:T(8,128)} %nb_far.1, s32[1,224]{1,0:T(1,128)} %bitcast.3, bf16[128,48,128]{2,1,0:T(8,128)(2,1)} %send.1.after), custom_call_target="tpu_custom_call" | custom-call | tf_op jit(solution)/shard_map/prepare/pallas_call | solution.py:41
  56.2 5.9 %sound_zero.1.part = f32[4,224,512]{2,1,0:T(8,128)} custom-call(bf16[4,224,512]{2,1,0:T(8,128)(2,1)} %q0.3, bf16[512,256]{1,0:T(8,128)(2,1)} %get-tuple-element.45.refs_1_.esrc, bf16[224,896]{1,0:T(8,128)(2,1)} %get-tuple-element.46.refs_2_.gcat, bf16[256,512]{1,0:T(8,128)(2,1)} %get-tuple-element.47.refs_3_.edst, bf16[512,512]{1,0:T(8,128)(2,1)} %dx.3, ...), custom_call_target="tpu_custom_call" | custom-call | tf_op jit(solution)/shard_map/sound_zero/pallas_call | solution.py:41
  62.1 2.4 %all-to-all-done.1.got = bf16[128,48,128]{2,1,0:T(8,128)(2,1)S(1)} async-done(((bf16[128,48,128]{2,1,0:T(8,128)(2,1)}), bf16[128,48,128]{2,1,0:T(8,128)(2,1)S(1)}, u32[]{:S(2)}, u32[]{:S(2)}) %all-to-all-start.1) | async-done | bytes 1572896 | tf_op jit(solution)/shard_map/all_to_all | solution.py:621
  64.5 2.8 %sources.1 = (f32[4,224,512]{2,1,0:T(8,128)S(1)}, bf16[3,224,512]{2,1,0:T(8,128)(2,1)S(1)}, bf16[2,224,128]{2,1,0:T(8,128)(2,1)S(1)}, bf16[2,224,128]{2,1,0:T(8,128)(2,1)S(1)}, f32[8,128]{1,0:T(8,128)}) custom-call(bf16[128,48,128]{2,1,0:T(8,128)(2,1)S(1)} %all-to-all-done.1.got, bf16[2,224,1024]{2,1,0:T(8,128)(2,1)} %get-tuple-element.44.pick, ...), custom_call_target="tpu_custom_call" | custom-call | tf_op jit(solution)/shard_map/sources/pallas_call | solution.py:41
  68.0 3.9 %collective-permute-start.11 = (bf16[2,224,128]{2,1,0:T(8,128)(2,1)S(1)}, bf16[2,224,128]{2,1,0:T(8,128)(2,1)S(1)}, u32[]{:S(2)}, u32[]{:S(2)}) collective-permute-start(bf16[2,224,128]{2,1,0:T(8,128)(2,1)S(1)} %get-tuple-element.54.r_3_), channel_id=1, source_target_pairs={{0,31},{1,2},{2,1},{3,4},{4,3},{5,6},{6,5},{7,8},{8,7},{9,10},{10,... | collective-permute-start | bytes 344072 | tf_op jit(solution)/shard_map/ppermute | solution.py:577
  71.9 6.3 %collective-permute-done.7.zo = f32[128,128]{1,0:T(8,128)S(1)} collective-permute-done((f32[128,128]{1,0:T(8,128)S(1)}, f32[128,128]{1,0:T(8,128)S(1)}, u32[]{:S(2)}, u32[]{:S(2)}) %collective-permute-start.7) | collective-permute-done | bytes 65568 | tf_op jit(solution)/shard_map/ppermute | solution.py:577
  78.3 3.6 %flow_two.1.after = f32[5,4,128,128]{3,2,1,0:T(8,128)} custom-call(f32[5,4,128,128]{3,2,1,0:T(8,128)S(1)} %copy-done, f32[5,4,128,128]{3,2,1,0:T(8,128)S(1)} %copy-done.2, f32[5,128,128]{2,1,0:T(8,128)} %copy-done.7, f32[5,128,128]{2,1,0:T(8,128)} %copy-done.8, bf16[5,128,128]{2,1,0:T(8,128)(2,1)S(1)} %collective-permute-done.4.ce, ...), custom_call_target="tpu_custom_call" | custom-call | tf_op jit(solution)/shard_map/flow_two/pallas_call | solution.py:41
  82.0 2.5 %sound_one.1.r_6_.mid = f32[4,224,512]{2,1,0:T(8,128)S(1)} custom-call(bf16[4,224,512]{2,1,0:T(8,128)(2,1)S(1)} %copy-done.1, f32[4,224,512]{2,1,0:T(8,128)S(1)} %get-tuple-element.55.q1, bf16[3,224,512]{2,1,0:T(8,128)(2,1)S(1)} %get-tuple-element.56.src, bf16[512,512]{1,0:T(8,128)(2,1)S(1)} %copy-done.3, bf16[512,512]{1,0:T(8,128)(2,1)S(1)} %copy-done.4, ...), custom_call_target="tpu_custom_call" | custom-call | tf_op jit(solution)/shard_map/sound_one/pallas_call | solution.py:41
  85.1 4.3 %collective-permute-start.13 = (bf16[2,224,128]{2,1,0:T(8,128)(2,1)S(1)}, bf16[2,224,128]{2,1,0:T(8,128)(2,1)S(1)}, u32[]{:S(2)}, u32[]{:S(2)}) collective-permute-start(bf16[2,224,128]{2,1,0:T(8,128)(2,1)S(1)} %get-tuple-element.58.r_3_), channel_id=1, source_target_pairs={{0,31},{1,2},{2,1},{3,4},{4,3},{5,6},{6,5},{7,8},{8,7},{9,10},{10,... | collective-permute-start | bytes 344072 | tf_op jit(solution)/shard_map/ppermute | solution.py:577
  89.4 3.4 %sound_two.1 = (f32[4,224,512]{2,1,0:T(8,128)}, f32[2,4,224,128]{3,2,1,0:T(8,128)S(1)}) custom-call(bf16[4,224,512]{2,1,0:T(8,128)(2,1)S(1)} %copy-done.1, f32[4,224,512]{2,1,0:T(8,128)S(1)} %sound_one.1.r_6_.mid, f32[2,4,224,128]{3,2,1,0:T(8,128)S(1)} %get-tuple-element.59.ends, bf16[3,224,512]{2,1,0:T(8,128)(2,1)S(1)} %get-tuple-element.56.src, ...), custom_call_target="tpu_custom_call" | custom-call | tf_op jit(solution)/shard_map/sound_two/pallas_call | solution.py:41
  92.7 3.6 %collective-permute-done.13.r_5_ = bf16[2,224,128]{2,1,0:T(8,128)(2,1)S(1)} collective-permute-done((bf16[2,224,128]{2,1,0:T(8,128)(2,1)S(1)}, bf16[2,224,128]{2,1,0:T(8,128)(2,1)S(1)}, u32[]{:S(2)}, u32[]{:S(2)}) %collective-permute-start.13) | collective-permute-done | bytes 114720 | tf_op jit(solution)/shard_map/ppermute | solution.py:577
  96.3 1.4 %cross_two.1 = f32[4,224,512]{2,1,0:T(8,128)} custom-call(bf16[224,448]{1,0:T(8,128)(2,1)S(1)} %copy-done.11, bf16[224,448]{1,0:T(8,128)(2,1)S(1)} %copy-done.12, bf16[2,224,128]{2,1,0:T(8,128)(2,1)S(1)} %get-tuple-element.57.r_2_, bf16[2,224,128]{2,1,0:T(8,128)(2,1)S(1)} %get-tuple-element.58.r_3_, ...), custom_call_target="tpu_custom_call", output_to_operand_aliasing={{}: (7, {})} | custom-call | tf_op jit(solution)/shard_map/cross_two/pallas_call | solution.py:41
  (68 shorter events, 3.3 us)
Async XLA Ops:
  0.6 24.3 %copy-start = (f32[5,4,128,128]{3,2,1,0:T(8,128)S(1)}, f32[5,4,128,128]{3,2,1,0:T(8,128)}, u32[]{:S(2)}) copy-start(f32[5,4,128,128]{3,2,1,0:T(8,128)} %u.7) | copy-start | bytes 3932164
  0.6 14.1 %copy-start.21 = (s32[1,128,4]{1,2,0:T(4,128)S(1)}, s32[1,128,4]{1,2,0:T(4,128)}, u32[]{:S(2)}) copy-start(s32[1,128,4]{1,2,0:T(4,128)} %param.13) | copy-start | bytes 6148
  3.2 32.7 %copy-start.15 = (bf16[2,224,128]{2,1,0:T(8,128)(2,1)}, bf16[2,224,128]{2,1,0:T(8,128)(2,1)S(1)}, u32[]{:S(2)}) copy-start(bf16[2,224,128]{2,1,0:T(8,128)(2,1)S(1)} %get-tuple-element.41.refs_9_) | copy-start | bytes 344068
  3.2 32.7 %copy-start.16 = (bf16[2,224,128]{2,1,0:T(8,128)(2,1)}, bf16[2,224,128]{2,1,0:T(8,128)(2,1)S(1)}, u32[]{:S(2)}) copy-start(bf16[2,224,128]{2,1,0:T(8,128)(2,1)S(1)} %get-tuple-element.42.refs_10_) | copy-start | bytes 344068
  3.2 21.7 %collective-permute-start = (f32[5,128,128]{2,1,0:T(8,128)S(1)}, f32[5,128,128]{2,1,0:T(8,128)S(1)}, u32[]{:S(2)}, u32[]{:S(2)}) collective-permute-start(f32[5,128,128]{2,1,0:T(8,128)S(1)} %get-tuple-element.32), channel_id=1, source_target_pairs={{0,1},{1,0},{2,3},{3,2},{4,5},{5,4},{6,7},{7,6},{8,9},{9,8},{10,11... | collective-permute-start | bytes 983048 | tf_op jit(solution)/shard_map/ppermute | solution.py:578
  4.8 20.1 %collective-permute-start.1 = (f32[5,128,128]{2,1,0:T(8,128)S(1)}, f32[5,128,128]{2,1,0:T(8,128)S(1)}, u32[]{:S(2)}, u32[]{:S(2)}) collective-permute-start(f32[5,128,128]{2,1,0:T(8,128)S(1)} %get-tuple-element.33), channel_id=1, source_target_pairs={{0,31},{1,2},{2,1},{3,4},{4,3},{5,6},{6,5},{7,8},{8,7},{9,10},{10,... | collective-permute-start | bytes 983048 | tf_op jit(solution)/shard_map/ppermute | solution.py:577
  12.7 1.3 %collective-permute-start.2 = (f32[128,128]{1,0:T(8,128)S(1)}, f32[128,128]{1,0:T(8,128)S(1)}, u32[]{:S(2)}, u32[]{:S(2)}) collective-permute-start(f32[128,128]{1,0:T(8,128)S(1)} %get-tuple-element.34), channel_id=1, source_target_pairs={{0,32},{32,0},{64,96},{96,64},{1,33},{33,1},{65,97},{97,65},{2,34}... | collective-permute-start | bytes 196616 | tf_op jit(solution)/shard_map/ppermute | solution.py:578
  12.7 13.3 %collective-permute-start.8 = (bf16[2,224,128]{2,1,0:T(8,128)(2,1)S(1)}, bf16[2,224,128]{2,1,0:T(8,128)(2,1)S(1)}, u32[]{:S(2)}, u32[]{:S(2)}) collective-permute-start(bf16[2,224,128]{2,1,0:T(8,128)(2,1)S(1)} %get-tuple-element.41.refs_9_), channel_id=1, source_target_pairs={{0,1},{1,0},{2,3},{3,2},{4,5},{5,4},{6,7},{7,6},{8,9},{9,8},{10,11... | collective-permute-start | bytes 344072 | tf_op jit(solution)/shard_map/ppermute | solution.py:578
  12.7 13.3 %collective-permute-start.9 = (bf16[2,224,128]{2,1,0:T(8,128)(2,1)S(1)}, bf16[2,224,128]{2,1,0:T(8,128)(2,1)S(1)}, u32[]{:S(2)}, u32[]{:S(2)}) collective-permute-start(bf16[2,224,128]{2,1,0:T(8,128)(2,1)S(1)} %get-tuple-element.42.refs_10_), channel_id=1, source_target_pairs={{0,31},{1,2},{2,1},{3,4},{4,3},{5,6},{6,5},{7,8},{8,7},{9,10},{10,... | collective-permute-start | bytes 344072 | tf_op jit(solution)/shard_map/ppermute | solution.py:577
  13.9 21.9 %copy-start.13 = (f32[128,128]{1,0:T(8,128)}, f32[128,128]{1,0:T(8,128)S(1)}, u32[]{:S(2)}) copy-start(f32[128,128]{1,0:T(8,128)S(1)} %collective-permute-done.2.ze) | copy-start | bytes 196612
  13.9 11.0 %collective-permute-start.3 = (f32[128,128]{1,0:T(8,128)S(1)}, f32[128,128]{1,0:T(8,128)S(1)}, u32[]{:S(2)}, u32[]{:S(2)}) collective-permute-start(f32[128,128]{1,0:T(8,128)S(1)} %get-tuple-element.35), channel_id=1, source_target_pairs={{0,96},{32,64},{64,32},{96,0},{1,97},{33,65},{65,33},{97,1},{2,98}... | collective-permute-start | bytes 196616 | tf_op jit(solution)/shard_map/ppermute | solution.py:577
  15.5 18.3 %all-to-all-start = ((s32[128,1,128]{2,1,0:T(1,128)}), s32[128,1,128]{2,1,0:T(1,128)S(1)}, u32[]{:S(2)}, u32[]{:S(2)}) async-start(s32[128,1,128]{2,1,0:T(1,128)} %pad.4), calls=%async_computation | async-start | bytes 131072 | tf_op jit(solution)/shard_map/all_to_all | solution.py:591
  35.9 28.6 %all-to-all-start.1 = ((bf16[128,48,128]{2,1,0:T(8,128)(2,1)}), bf16[128,48,128]{2,1,0:T(8,128)(2,1)S(1)}, u32[]{:S(2)}, u32[]{:S(2)}) async-start(bf16[128,48,128]{2,1,0:T(8,128)(2,1)} %send.1.after), calls=%async_computation.1 | async-start | bytes 3145728 | tf_op jit(solution)/shard_map/all_to_all | solution.py:621
  40.6 15.6 %copy-start.18 = (bf16[2,224,128]{2,1,0:T(8,128)(2,1)S(1)}, bf16[2,224,128]{2,1,0:T(8,128)(2,1)}, u32[]{:S(2)}) copy-start(bf16[2,224,128]{2,1,0:T(8,128)(2,1)} %copy-done.17) | copy-start | bytes 344068
  40.6 15.6 %copy-start.20 = (bf16[2,224,128]{2,1,0:T(8,128)(2,1)S(1)}, bf16[2,224,128]{2,1,0:T(8,128)(2,1)}, u32[]{:S(2)}) copy-start(bf16[2,224,128]{2,1,0:T(8,128)(2,1)} %copy-done.19) | copy-start | bytes 344068
  44.7 33.5 %collective-permute-start.4 = (bf16[5,128,128]{2,1,0:T(8,128)(2,1)}, bf16[5,128,128]{2,1,0:T(8,128)(2,1)S(1)}, u32[]{:S(2)}, u32[]{:S(2)}) collective-permute-start(bf16[5,128,128]{2,1,0:T(8,128)(2,1)} %get-tuple-element.37), channel_id=1, source_target_pairs={{0,1},{1,0},{2,3},{3,2},{4,5},{5,4},{6,7},{7,6},{8,9},{9,8},{10,11... | collective-permute-start | bytes 491528 | tf_op jit(solution)/shard_map/ppermute | solution.py:578
  45.6 32.6 %collective-permute-start.5 = (bf16[5,128,128]{2,1,0:T(8,128)(2,1)}, bf16[5,128,128]{2,1,0:T(8,128)(2,1)S(1)}, u32[]{:S(2)}, u32[]{:S(2)}) collective-permute-start(bf16[5,128,128]{2,1,0:T(8,128)(2,1)} %get-tuple-element.38), channel_id=1, source_target_pairs={{0,31},{1,2},{2,1},{3,4},{4,3},{5,6},{6,5},{7,8},{8,7},{9,10},{10,... | collective-permute-start | bytes 491528 | tf_op jit(solution)/shard_map/ppermute | solution.py:577
  53.0 18.9 %collective-permute-start.6 = (f32[128,128]{1,0:T(8,128)}, f32[128,128]{1,0:T(8,128)S(1)}, u32[]{:S(2)}, u32[]{:S(2)}) collective-permute-start(f32[128,128]{1,0:T(8,128)} %get-tuple-element.39), channel_id=1, source_target_pairs={{0,32},{32,0},{64,96},{96,64},{1,33},{33,1},{65,97},{97,65},{2,34}... | collective-permute-start | bytes 196616 | tf_op jit(solution)/shard_map/ppermute | solution.py:578
  64.5 13.8 %copy-start.2 = (f32[5,4,128,128]{3,2,1,0:T(8,128)S(1)}, f32[5,4,128,128]{3,2,1,0:T(8,128)}, u32[]{:S(2)}) copy-start(f32[5,4,128,128]{3,2,1,0:T(8,128)} %get-tuple-element.36.refs_13_.first) | copy-start | bytes 3932164
  67.3 17.2 %collective-permute-start.10 = (bf16[2,224,128]{2,1,0:T(8,128)(2,1)S(1)}, bf16[2,224,128]{2,1,0:T(8,128)(2,1)S(1)}, u32[]{:S(2)}, u32[]{:S(2)}) collective-permute-start(bf16[2,224,128]{2,1,0:T(8,128)(2,1)S(1)} %get-tuple-element.53.r_2_), channel_id=1, source_target_pairs={{0,1},{1,0},{2,3},{3,2},{4,5},{5,4},{6,7},{7,6},{8,9},{9,8},{10,11... | collective-permute-start | bytes 344072 | tf_op jit(solution)/shard_map/ppermute | solution.py:578
  68.0 16.5 %collective-permute-start.11 = (bf16[2,224,128]{2,1,0:T(8,128)(2,1)S(1)}, bf16[2,224,128]{2,1,0:T(8,128)(2,1)S(1)}, u32[]{:S(2)}, u32[]{:S(2)}) collective-permute-start(bf16[2,224,128]{2,1,0:T(8,128)(2,1)S(1)} %get-tuple-element.54.r_3_), channel_id=1, source_target_pairs={{0,31},{1,2},{2,1},{3,4},{4,3},{5,6},{6,5},{7,8},{8,7},{9,10},{10,... | collective-permute-start | bytes 344072 | tf_op jit(solution)/shard_map/ppermute | solution.py:577
  71.9 6.3 %collective-permute-start.7 = (f32[128,128]{1,0:T(8,128)S(1)}, f32[128,128]{1,0:T(8,128)S(1)}, u32[]{:S(2)}, u32[]{:S(2)}) collective-permute-start(f32[128,128]{1,0:T(8,128)S(1)} %copy-done.22), channel_id=1, source_target_pairs={{0,96},{32,64},{64,32},{96,0},{1,97},{33,65},{65,33},{97,1},{2,98}... | collective-permute-start | bytes 196616 | tf_op jit(solution)/shard_map/ppermute | solution.py:577
  85.0 7.7 %collective-permute-start.12 = (bf16[2,224,128]{2,1,0:T(8,128)(2,1)S(1)}, bf16[2,224,128]{2,1,0:T(8,128)(2,1)S(1)}, u32[]{:S(2)}, u32[]{:S(2)}) collective-permute-start(bf16[2,224,128]{2,1,0:T(8,128)(2,1)S(1)} %get-tuple-element.57.r_2_), channel_id=1, source_target_pairs={{0,1},{1,0},{2,3},{3,2},{4,5},{5,4},{6,7},{7,6},{8,9},{9,8},{10,11... | collective-permute-start | bytes 344072 | tf_op jit(solution)/shard_map/ppermute | solution.py:578
  85.1 11.2 %collective-permute-start.13 = (bf16[2,224,128]{2,1,0:T(8,128)(2,1)S(1)}, bf16[2,224,128]{2,1,0:T(8,128)(2,1)S(1)}, u32[]{:S(2)}, u32[]{:S(2)}) collective-permute-start(bf16[2,224,128]{2,1,0:T(8,128)(2,1)S(1)} %get-tuple-element.58.r_3_), channel_id=1, source_target_pairs={{0,31},{1,2},{2,1},{3,4},{4,3},{5,6},{6,5},{7,8},{8,7},{9,10},{10,... | collective-permute-start | bytes 344072 | tf_op jit(solution)/shard_map/ppermute | solution.py:577
  (15 other events, 90.5 us)

commit v3 on v2

--- a/solution.py
+++ b/solution.py
@@ -473,7 +473,7 @@
 
 
 def sound_zero_body(*refs):
-    given, (bhi, alo, after, part, *here), (hold, sems) = refs[:11], refs[11:26], refs[26:]
+    given, (bhi, alo, _, _, part, *here), (hold, sems) = refs[:11], refs[11:27], refs[27:]
     coming = {id(to): copy for to, copy in zip(here, begin(sems, 4, *zip(given, here)))}
     ready = lambda *names: finish([coming[id(t)] for t in names])
     q, esrc, gcat, edst, dx, dy, dz, gx0, gx1, olo, ohi = here
@@ -497,7 +497,7 @@
     finish(copies)
 
 
-def sources_body(got, pick, part, q1, src, lo, hi, token, pick_v, part_v, token_v, sems):
+def sources_body(got, pick, part, _, q1, src, lo, hi, token, pick_v, part_v, token_v, sems):
     token_v[...] = jnp.zeros_like(token_v)
     copies = begin(
         sems,
@@ -647,15 +647,15 @@
         far=range(1, 5),
         far_out=range(5),
     )
+    ye, yo = swap(ye, yo, "solver")
     ce, co = swap(ce, co, "space")
-    ye, yo = swap(ye, yo, "solver")
 
     given = (acoustic_state, esrc, gcat, edst, dx, dy, dz, ge, go, qe, qo)
     part = call(
         sound_zero_body,
         state,
         "sound_zero",
-        given + (got_qe, got_qo, first),
+        given + (got_qe, got_qo, first, ye),
         scratch=[keep_half(*t.shape) for t in given] + [keep(4, EL, NODES), dma(15)],
         far=[*range(11), 13],
         far_out=(0,),
@@ -665,7 +665,7 @@
         sources_body,
         [state, half(3, EL, NODES)] + traces + [full(8, 128)],
         "sources",
-        (got, pick, part),
+        (got, pick, part, yo),
         scratch=[keep_half(2, EL, 1024), keep(3, EL, NODES), keep(8, 128), dma(6)],
         far=(1, 2),
         far_out=(4,),

time: 98.4 us -> 94 us (0.955)
  waiting for transfers between devices: 20.4 us -> 11.7 us
  starting transfers between devices: 42.4 us -> 46.7 us
    ppermute x7, waiting for transfers between devices: 10.2 us -> 3.06 us  [swap(): other = lax.ppermute(odd, axis, by_odd)]
    ppermute x7, starting transfers between devices: 25.3 us -> 29 us  [swap(): other = lax.ppermute(odd, axis, by_odd)]
    all_to_all x1, waiting for transfers between devices: 2.37 us -> 0.8 us  [local(): got = lax.all_to_all(send, both, split_axis=0, concat_axis=0, tiled=True)]
  transfers between devices with their start and end apart: 16 -> 16, of which waited for: 5 -> 4; matrix products, arithmetic and copies ran while one was open for 1% -> 1% of each run, Pallas kernels for 27% -> 28%
where the time goes in v3:
time: 94 us; the launch traced here: 93.7 us
  starting transfers between devices  46.7 us (50%)
  Pallas kernels  33 us (35%)
  waiting for transfers between devices  11.7 us (12%)
  between operations  1.3 us (1%)
    pallas_call x12, Pallas kernels, call(): pl.pallas_call(body, out_shape=outs if many else outs[0], in_specs=[space...  33 us
    ppermute x7, starting transfers between devices, swap(): other = lax.ppermute(odd, axis, by_odd)  29 us
    all_to_all x1, starting transfers between devices, local(): lax.all_to_all(wanted, both, split_axis=0, concat_axis=0, tiled=True)  9.11 us
    all_to_all x1, waiting for transfers between devices, local(): lax.all_to_all(wanted, both, split_axis=0, concat_axis=0, tiled=True)  7.82 us
    all_to_all x1, starting transfers between devices, local(): got = lax.all_to_all(send, both, split_axis=0, concat_axis=0, tiled=True)  4.66 us
    ppermute x7, starting transfers between devices, swap(): return (lax.ppermute(even, axis, by_even), other)  3.96 us
    ppermute x7, waiting for transfers between devices, swap(): other = lax.ppermute(odd, axis, by_odd)  3.06 us
  transfers between devices with their start and end apart: 16, of which 4 were waited for; matrix products, arithmetic and copies ran while one was open for 1% of the time, Pallas kernels for 28%

profile of v3, /device:TPU:0, one launch (start us, length us, event | category | flops | bytes accessed | tf_op | source)
XLA Modules:
  0.0 93.7 jit_solution(6249562706131624154)
XLA Ops:
  0.6 2.5 %edges.1 = (f32[5,128,128]{2,1,0:T(8,128)S(1)}, f32[5,128,128]{2,1,0:T(8,128)S(1)}, f32[128,128]{1,0:T(8,128)S(1)}, f32[128,128]{1,0:T(8,128)S(1)}, bf16[2,224,1...) custom-call(f32[5,4,128,128]{3,2,1,0:T(8,128)} %u.7, bf16[4,224,512]{2,1,0:T(8,128)(2,1)} %q0.3), custom_call_target="tpu_custom_call" | custom-call | tf_op jit(solution)/shard_map/edges/pallas_call | solution.py:41
  3.2 1.7 %collective-permute-start = (f32[5,128,128]{2,1,0:T(8,128)S(1)}, f32[5,128,128]{2,1,0:T(8,128)S(1)}, u32[]{:S(2)}, u32[]{:S(2)}) collective-permute-start(f32[5,128,128]{2,1,0:T(8,128)S(1)} %get-tuple-element.32), channel_id=1, source_target_pairs={{0,1},{1,0},{2,3},{3,2},{4,5},{5,4},{6,7},{7,6},{8,9},{9,8},{10,11... | collective-permute-start | bytes 983048 | tf_op jit(solution)/shard_map/ppermute | solution.py:578
  4.8 7.9 %collective-permute-start.1 = (f32[5,128,128]{2,1,0:T(8,128)S(1)}, f32[5,128,128]{2,1,0:T(8,128)S(1)}, u32[]{:S(2)}, u32[]{:S(2)}) collective-permute-start(f32[5,128,128]{2,1,0:T(8,128)S(1)} %get-tuple-element.33), channel_id=1, source_target_pairs={{0,31},{1,2},{2,1},{3,4},{4,3},{5,6},{6,5},{7,8},{8,7},{9,10},{10,... | collective-permute-start | bytes 983048 | tf_op jit(solution)/shard_map/ppermute | solution.py:577
  12.7 1.2 %collective-permute-start.9 = (bf16[2,224,128]{2,1,0:T(8,128)(2,1)S(1)}, bf16[2,224,128]{2,1,0:T(8,128)(2,1)S(1)}, u32[]{:S(2)}, u32[]{:S(2)}) collective-permute-start(bf16[2,224,128]{2,1,0:T(8,128)(2,1)S(1)} %get-tuple-element.42.refs_10_), channel_id=1, source_target_pairs={{0,31},{1,2},{2,1},{3,4},{4,3},{5,6},{6,5},{7,8},{8,7},{9,10},{10,... | collective-permute-start | bytes 344072 | tf_op jit(solution)/shard_map/ppermute | solution.py:577
  15.5 9.1 %all-to-all-start = ((s32[128,1,128]{2,1,0:T(1,128)}), s32[128,1,128]{2,1,0:T(1,128)S(1)}, u32[]{:S(2)}, u32[]{:S(2)}) async-start(s32[128,1,128]{2,1,0:T(1,128)} %pad.4), calls=%async_computation | async-start | bytes 131072 | tf_op jit(solution)/shard_map/all_to_all | solution.py:591
  25.0 1.0 %lamb.1.table = bf16[128,768]{1,0:T(8,128)(2,1)S(1)} custom-call(f32[5,4,128,128]{3,2,1,0:T(8,128)S(1)} %copy-done, f32[5,128,128]{2,1,0:T(8,128)S(1)} %collective-permute-done.ue.xe, f32[5,128,128]{2,1,0:T(8,128)S(1)} %collective-permute-done.1.uo.xo, f32[128,128]{1,0:T(8,128)S(1)} %collective-permute-done.2.ze, f32[128,128]{1,0:T(8,128)S(1)} %collective-permute-done.3.zo), custom_call_target="tpu_custom_call" | custom-call | tf_op jit(solution)/shard_map/lamb/pallas_call | solution.py:41
  26.0 7.8 %all-to-all-done.req = s32[128,1,128]{2,1,0:T(1,128)S(1)} async-done(((s32[128,1,128]{2,1,0:T(1,128)}), s32[128,1,128]{2,1,0:T(1,128)S(1)}, u32[]{:S(2)}, u32[]{:S(2)}) %all-to-all-start) | async-done | bytes 65568 | tf_op jit(solution)/shard_map/all_to_all | solution.py:591
  33.8 2.0 %send.1.after = bf16[128,48,128]{2,1,0:T(8,128)(2,1)} custom-call(s32[128,1,128]{2,1,0:T(1,128)S(1)} %all-to-all-done.req, bf16[128,768]{1,0:T(8,128)(2,1)S(1)} %lamb.1.table), custom_call_target="tpu_custom_call" | custom-call | tf_op jit(solution)/shard_map/send/pallas_call | solution.py:41
  35.9 4.7 %all-to-all-start.1 = ((bf16[128,48,128]{2,1,0:T(8,128)(2,1)}), bf16[128,48,128]{2,1,0:T(8,128)(2,1)S(1)}, u32[]{:S(2)}, u32[]{:S(2)}) async-start(bf16[128,48,128]{2,1,0:T(8,128)(2,1)} %send.1.after), calls=%async_computation.1 | async-start | bytes 3145728 | tf_op jit(solution)/shard_map/all_to_all | solution.py:621
  40.6 4.1 %flow_one.1 = (f32[5,4,128,128]{3,2,1,0:T(8,128)}, bf16[5,128,128]{2,1,0:T(8,128)(2,1)}, bf16[5,128,128]{2,1,0:T(8,128)(2,1)}, f32[128,128]{1,0:T(8,128)}, f32[128,128]{1,0:T(8,128)}) custom-call(f32[5,4,128,128]{3,2,1,0:T(8,128)S(1)} %copy-done, f32[5,128,128]{2,1,0:T(8,128)} %copy-done.7, f32[5,128,128]{2,1,0:T(8,128)} %copy-done.8, ...), custom_call_target="tpu_custom_call" | custom-call | tf_op jit(solution)/shard_map/flow_one/pallas_call | solution.py:41
  44.8 1.2 %collective-permute-start.7 = (f32[128,128]{1,0:T(8,128)}, f32[128,128]{1,0:T(8,128)S(1)}, u32[]{:S(2)}, u32[]{:S(2)}) collective-permute-start(f32[128,128]{1,0:T(8,128)} %get-tuple-element.40), channel_id=1, source_target_pairs={{0,96},{32,64},{64,32},{96,0},{1,97},{33,65},{65,33},{97,1},{2,98}... | collective-permute-start | bytes 196616 | tf_op jit(solution)/shard_map/ppermute | solution.py:577
  46.0 1.5 %collective-permute-start.4 = (bf16[5,128,128]{2,1,0:T(8,128)(2,1)}, bf16[5,128,128]{2,1,0:T(8,128)(2,1)S(1)}, u32[]{:S(2)}, u32[]{:S(2)}) collective-permute-start(bf16[5,128,128]{2,1,0:T(8,128)(2,1)} %get-tuple-element.37), channel_id=1, source_target_pairs={{0,1},{1,0},{2,3},{3,2},{4,5},{5,4},{6,7},{7,6},{8,9},{9,8},{10,11... | collective-permute-start | bytes 491528 | tf_op jit(solution)/shard_map/ppermute | solution.py:578
  47.5 7.0 %collective-permute-start.5 = (bf16[5,128,128]{2,1,0:T(8,128)(2,1)}, bf16[5,128,128]{2,1,0:T(8,128)(2,1)S(1)}, u32[]{:S(2)}, u32[]{:S(2)}) collective-permute-start(bf16[5,128,128]{2,1,0:T(8,128)(2,1)} %get-tuple-element.38), channel_id=1, source_target_pairs={{0,31},{1,2},{2,1},{3,4},{4,3},{5,6},{6,5},{7,8},{8,7},{9,10},{10,... | collective-permute-start | bytes 491528 | tf_op jit(solution)/shard_map/ppermute | solution.py:577
  54.5 3.2 %prepare.1 = (bf16[224,896]{1,0:T(8,128)(2,1)}, bf16[224,448]{1,0:T(8,128)(2,1)}, bf16[224,448]{1,0:T(8,128)(2,1)}, bf16[2,224,1024]{2,1,0:T(8,128)(2,1)}, bf16[...) custom-call(s32[6,224]{1,0:T(8,128)} %nb_far.1, s32[1,224]{1,0:T(1,128)} %bitcast.3, bf16[128,48,128]{2,1,0:T(8,128)(2,1)} %send.1.after), custom_call_target="tpu_custom_call" | custom-call | tf_op jit(solution)/shard_map/prepare/pallas_call | solution.py:41
  57.8 5.9 %sound_zero.1.part = f32[4,224,512]{2,1,0:T(8,128)} custom-call(bf16[4,224,512]{2,1,0:T(8,128)(2,1)} %q0.3, bf16[512,256]{1,0:T(8,128)(2,1)} %get-tuple-element.45.refs_1_.esrc, bf16[224,896]{1,0:T(8,128)(2,1)} %get-tuple-element.46.refs_2_.gcat, bf16[256,512]{1,0:T(8,128)(2,1)} %get-tuple-element.47.refs_3_.edst, bf16[512,512]{1,0:T(8,128)(2,1)} %dx.3, ...), custom_call_target="tpu_custom_call" | custom-call | tf_op jit(solution)/shard_map/sound_zero/pallas_call | solution.py:41
  63.7 0.8 all-to-all-done.1.got
  64.5 2.8 %sources.1 = (f32[4,224,512]{2,1,0:T(8,128)S(1)}, bf16[3,224,512]{2,1,0:T(8,128)(2,1)S(1)}, bf16[2,224,128]{2,1,0:T(8,128)(2,1)S(1)}, bf16[2,224,128]{2,1,0:T(8,128)(2,1)S(1)}, f32[8,128]{1,0:T(8,128)}) custom-call(bf16[128,48,128]{2,1,0:T(8,128)(2,1)S(1)} %all-to-all-done.1.got, bf16[2,224,1024]{2,1,0:T(8,128)(2,1)} %get-tuple-element.44.pick, ...), custom_call_target="tpu_custom_call" | custom-call | tf_op jit(solution)/shard_map/sources/pallas_call | solution.py:41
  68.0 6.2 %collective-permute-start.11 = (bf16[2,224,128]{2,1,0:T(8,128)(2,1)S(1)}, bf16[2,224,128]{2,1,0:T(8,128)(2,1)S(1)}, u32[]{:S(2)}, u32[]{:S(2)}) collective-permute-start(bf16[2,224,128]{2,1,0:T(8,128)(2,1)S(1)} %get-tuple-element.54.r_3_), channel_id=1, source_target_pairs={{0,31},{1,2},{2,1},{3,4},{4,3},{5,6},{6,5},{7,8},{8,7},{9,10},{10,... | collective-permute-start | bytes 344072 | tf_op jit(solution)/shard_map/ppermute | solution.py:577
  74.3 3.6 %flow_two.1.after = f32[5,4,128,128]{3,2,1,0:T(8,128)} custom-call(f32[5,4,128,128]{3,2,1,0:T(8,128)S(1)} %copy-done, f32[5,4,128,128]{3,2,1,0:T(8,128)S(1)} %copy-done.2, f32[5,128,128]{2,1,0:T(8,128)} %copy-done.7, f32[5,128,128]{2,1,0:T(8,128)} %copy-done.8, bf16[5,128,128]{2,1,0:T(8,128)(2,1)S(1)} %collective-permute-done.4.ce, ...), custom_call_target="tpu_custom_call" | custom-call | tf_op jit(solution)/shard_map/flow_two/pallas_call | solution.py:41
  78.0 2.6 %sound_one.1.r_6_.mid = f32[4,224,512]{2,1,0:T(8,128)S(1)} custom-call(bf16[4,224,512]{2,1,0:T(8,128)(2,1)S(1)} %copy-done.1, f32[4,224,512]{2,1,0:T(8,128)S(1)} %get-tuple-element.55.q1, bf16[3,224,512]{2,1,0:T(8,128)(2,1)S(1)} %get-tuple-element.56.src, bf16[512,512]{1,0:T(8,128)(2,1)S(1)} %copy-done.3, bf16[512,512]{1,0:T(8,128)(2,1)S(1)} %copy-done.4, ...), custom_call_target="tpu_custom_call" | custom-call | tf_op jit(solution)/shard_map/sound_one/pallas_call | solution.py:41
  81.2 4.8 %collective-permute-start.13 = (bf16[2,224,128]{2,1,0:T(8,128)(2,1)S(1)}, bf16[2,224,128]{2,1,0:T(8,128)(2,1)S(1)}, u32[]{:S(2)}, u32[]{:S(2)}) collective-permute-start(bf16[2,224,128]{2,1,0:T(8,128)(2,1)S(1)} %get-tuple-element.58.r_3_), channel_id=1, source_target_pairs={{0,31},{1,2},{2,1},{3,4},{4,3},{5,6},{6,5},{7,8},{8,7},{9,10},{10,... | collective-permute-start | bytes 344072 | tf_op jit(solution)/shard_map/ppermute | solution.py:577
  86.0 3.4 %sound_two.1 = (f32[4,224,512]{2,1,0:T(8,128)}, f32[2,4,224,128]{3,2,1,0:T(8,128)S(1)}) custom-call(bf16[4,224,512]{2,1,0:T(8,128)(2,1)S(1)} %copy-done.1, f32[4,224,512]{2,1,0:T(8,128)S(1)} %sound_one.1.r_6_.mid, f32[2,4,224,128]{3,2,1,0:T(8,128)S(1)} %get-tuple-element.59.ends, bf16[3,224,512]{2,1,0:T(8,128)(2,1)S(1)} %get-tuple-element.56.src, ...), custom_call_target="tpu_custom_call" | custom-call | tf_op jit(solution)/shard_map/sound_two/pallas_call | solution.py:41
  89.4 2.8 %collective-permute-done.13.r_5_ = bf16[2,224,128]{2,1,0:T(8,128)(2,1)S(1)} collective-permute-done((bf16[2,224,128]{2,1,0:T(8,128)(2,1)S(1)}, bf16[2,224,128]{2,1,0:T(8,128)(2,1)S(1)}, u32[]{:S(2)}, u32[]{:S(2)}) %collective-permute-start.13) | collective-permute-done | bytes 114720 | tf_op jit(solution)/shard_map/ppermute | solution.py:577
  92.1 1.4 %cross_two.1 = f32[4,224,512]{2,1,0:T(8,128)} custom-call(bf16[224,448]{1,0:T(8,128)(2,1)S(1)} %copy-done.11, bf16[224,448]{1,0:T(8,128)(2,1)S(1)} %copy-done.12, bf16[2,224,128]{2,1,0:T(8,128)(2,1)S(1)} %get-tuple-element.57.r_2_, bf16[2,224,128]{2,1,0:T(8,128)(2,1)S(1)} %get-tuple-element.58.r_3_, ...), custom_call_target="tpu_custom_call", output_to_operand_aliasing={{}: (7, {})} | custom-call | tf_op jit(solution)/shard_map/cross_two/pallas_call | solution.py:41
  (66 shorter events, 3.3 us)
Async XLA Ops:
  0.6 24.3 %copy-start = (f32[5,4,128,128]{3,2,1,0:T(8,128)S(1)}, f32[5,4,128,128]{3,2,1,0:T(8,128)}, u32[]{:S(2)}) copy-start(f32[5,4,128,128]{3,2,1,0:T(8,128)} %u.7) | copy-start | bytes 3932164
  0.6 14.1 %copy-start.21 = (s32[1,128,4]{1,2,0:T(4,128)S(1)}, s32[1,128,4]{1,2,0:T(4,128)}, u32[]{:S(2)}) copy-start(s32[1,128,4]{1,2,0:T(4,128)} %param.13) | copy-start | bytes 6148
  3.2 32.7 %copy-start.15 = (bf16[2,224,128]{2,1,0:T(8,128)(2,1)}, bf16[2,224,128]{2,1,0:T(8,128)(2,1)S(1)}, u32[]{:S(2)}) copy-start(bf16[2,224,128]{2,1,0:T(8,128)(2,1)S(1)} %get-tuple-element.41.refs_9_) | copy-start | bytes 344068
  3.2 32.7 %copy-start.16 = (bf16[2,224,128]{2,1,0:T(8,128)(2,1)}, bf16[2,224,128]{2,1,0:T(8,128)(2,1)S(1)}, u32[]{:S(2)}) copy-start(bf16[2,224,128]{2,1,0:T(8,128)(2,1)S(1)} %get-tuple-element.42.refs_10_) | copy-start | bytes 344068
  3.2 21.7 %collective-permute-start = (f32[5,128,128]{2,1,0:T(8,128)S(1)}, f32[5,128,128]{2,1,0:T(8,128)S(1)}, u32[]{:S(2)}, u32[]{:S(2)}) collective-permute-start(f32[5,128,128]{2,1,0:T(8,128)S(1)} %get-tuple-element.32), channel_id=1, source_target_pairs={{0,1},{1,0},{2,3},{3,2},{4,5},{5,4},{6,7},{7,6},{8,9},{9,8},{10,11... | collective-permute-start | bytes 983048 | tf_op jit(solution)/shard_map/ppermute | solution.py:578
  4.8 20.1 %collective-permute-start.1 = (f32[5,128,128]{2,1,0:T(8,128)S(1)}, f32[5,128,128]{2,1,0:T(8,128)S(1)}, u32[]{:S(2)}, u32[]{:S(2)}) collective-permute-start(f32[5,128,128]{2,1,0:T(8,128)S(1)} %get-tuple-element.33), channel_id=1, source_target_pairs={{0,31},{1,2},{2,1},{3,4},{4,3},{5,6},{6,5},{7,8},{8,7},{9,10},{10,... | collective-permute-start | bytes 983048 | tf_op jit(solution)/shard_map/ppermute | solution.py:577
  12.7 1.3 %collective-permute-start.2 = (f32[128,128]{1,0:T(8,128)S(1)}, f32[128,128]{1,0:T(8,128)S(1)}, u32[]{:S(2)}, u32[]{:S(2)}) collective-permute-start(f32[128,128]{1,0:T(8,128)S(1)} %get-tuple-element.34), channel_id=1, source_target_pairs={{0,32},{32,0},{64,96},{96,64},{1,33},{33,1},{65,97},{97,65},{2,34}... | collective-permute-start | bytes 196616 | tf_op jit(solution)/shard_map/ppermute | solution.py:578
  12.7 13.3 %collective-permute-start.8 = (bf16[2,224,128]{2,1,0:T(8,128)(2,1)S(1)}, bf16[2,224,128]{2,1,0:T(8,128)(2,1)S(1)}, u32[]{:S(2)}, u32[]{:S(2)}) collective-permute-start(bf16[2,224,128]{2,1,0:T(8,128)(2,1)S(1)} %get-tuple-element.41.refs_9_), channel_id=1, source_target_pairs={{0,1},{1,0},{2,3},{3,2},{4,5},{5,4},{6,7},{7,6},{8,9},{9,8},{10,11... | collective-permute-start | bytes 344072 | tf_op jit(solution)/shard_map/ppermute | solution.py:578
  12.7 13.3 %collective-permute-start.9 = (bf16[2,224,128]{2,1,0:T(8,128)(2,1)S(1)}, bf16[2,224,128]{2,1,0:T(8,128)(2,1)S(1)}, u32[]{:S(2)}, u32[]{:S(2)}) collective-permute-start(bf16[2,224,128]{2,1,0:T(8,128)(2,1)S(1)} %get-tuple-element.42.refs_10_), channel_id=1, source_target_pairs={{0,31},{1,2},{2,1},{3,4},{4,3},{5,6},{6,5},{7,8},{8,7},{9,10},{10,... | collective-permute-start | bytes 344072 | tf_op jit(solution)/shard_map/ppermute | solution.py:577
  13.9 21.9 %copy-start.13 = (f32[128,128]{1,0:T(8,128)}, f32[128,128]{1,0:T(8,128)S(1)}, u32[]{:S(2)}) copy-start(f32[128,128]{1,0:T(8,128)S(1)} %collective-permute-done.2.ze) | copy-start | bytes 196612
  13.9 11.0 %collective-permute-start.3 = (f32[128,128]{1,0:T(8,128)S(1)}, f32[128,128]{1,0:T(8,128)S(1)}, u32[]{:S(2)}, u32[]{:S(2)}) collective-permute-start(f32[128,128]{1,0:T(8,128)S(1)} %get-tuple-element.35), channel_id=1, source_target_pairs={{0,96},{32,64},{64,32},{96,0},{1,97},{33,65},{65,33},{97,1},{2,98}... | collective-permute-start | bytes 196616 | tf_op jit(solution)/shard_map/ppermute | solution.py:577
  15.5 18.3 %all-to-all-start = ((s32[128,1,128]{2,1,0:T(1,128)}), s32[128,1,128]{2,1,0:T(1,128)S(1)}, u32[]{:S(2)}, u32[]{:S(2)}) async-start(s32[128,1,128]{2,1,0:T(1,128)} %pad.4), calls=%async_computation | async-start | bytes 131072 | tf_op jit(solution)/shard_map/all_to_all | solution.py:591
  24.9 11.0 %copy-start.7 = (f32[5,128,128]{2,1,0:T(8,128)}, f32[5,128,128]{2,1,0:T(8,128)S(1)}, u32[]{:S(2)}) copy-start(f32[5,128,128]{2,1,0:T(8,128)S(1)} %collective-permute-done.ue.xe) | copy-start | bytes 983044
  35.9 28.6 %all-to-all-start.1 = ((bf16[128,48,128]{2,1,0:T(8,128)(2,1)}), bf16[128,48,128]{2,1,0:T(8,128)(2,1)S(1)}, u32[]{:S(2)}, u32[]{:S(2)}) async-start(bf16[128,48,128]{2,1,0:T(8,128)(2,1)} %send.1.after), calls=%async_computation.1 | async-start | bytes 3145728 | tf_op jit(solution)/shard_map/all_to_all | solution.py:621
  40.6 17.2 %copy-start.18 = (bf16[2,224,128]{2,1,0:T(8,128)(2,1)S(1)}, bf16[2,224,128]{2,1,0:T(8,128)(2,1)}, u32[]{:S(2)}) copy-start(bf16[2,224,128]{2,1,0:T(8,128)(2,1)} %copy-done.17) | copy-start | bytes 344068
  40.6 17.2 %copy-start.20 = (bf16[2,224,128]{2,1,0:T(8,128)(2,1)S(1)}, bf16[2,224,128]{2,1,0:T(8,128)(2,1)}, u32[]{:S(2)}) copy-start(bf16[2,224,128]{2,1,0:T(8,128)(2,1)} %copy-done.19) | copy-start | bytes 344068
  44.7 13.0 %collective-permute-start.6 = (f32[128,128]{1,0:T(8,128)}, f32[128,128]{1,0:T(8,128)S(1)}, u32[]{:S(2)}, u32[]{:S(2)}) collective-permute-start(f32[128,128]{1,0:T(8,128)} %get-tuple-element.39), channel_id=1, source_target_pairs={{0,32},{32,0},{64,96},{96,64},{1,33},{33,1},{65,97},{97,65},{2,34}... | collective-permute-start | bytes 196616 | tf_op jit(solution)/shard_map/ppermute | solution.py:578
  44.8 18.8 %collective-permute-start.7 = (f32[128,128]{1,0:T(8,128)}, f32[128,128]{1,0:T(8,128)S(1)}, u32[]{:S(2)}, u32[]{:S(2)}) collective-permute-start(f32[128,128]{1,0:T(8,128)} %get-tuple-element.40), channel_id=1, source_target_pairs={{0,96},{32,64},{64,32},{96,0},{1,97},{33,65},{65,33},{97,1},{2,98}... | collective-permute-start | bytes 196616 | tf_op jit(solution)/shard_map/ppermute | solution.py:577
  46.0 28.2 %collective-permute-start.4 = (bf16[5,128,128]{2,1,0:T(8,128)(2,1)}, bf16[5,128,128]{2,1,0:T(8,128)(2,1)S(1)}, u32[]{:S(2)}, u32[]{:S(2)}) collective-permute-start(bf16[5,128,128]{2,1,0:T(8,128)(2,1)} %get-tuple-element.37), channel_id=1, source_target_pairs={{0,1},{1,0},{2,3},{3,2},{4,5},{5,4},{6,7},{7,6},{8,9},{9,8},{10,11... | collective-permute-start | bytes 491528 | tf_op jit(solution)/shard_map/ppermute | solution.py:578
  47.5 26.7 %collective-permute-start.5 = (bf16[5,128,128]{2,1,0:T(8,128)(2,1)}, bf16[5,128,128]{2,1,0:T(8,128)(2,1)S(1)}, u32[]{:S(2)}, u32[]{:S(2)}) collective-permute-start(bf16[5,128,128]{2,1,0:T(8,128)(2,1)} %get-tuple-element.38), channel_id=1, source_target_pairs={{0,31},{1,2},{2,1},{3,4},{4,3},{5,6},{6,5},{7,8},{8,7},{9,10},{10,... | collective-permute-start | bytes 491528 | tf_op jit(solution)/shard_map/ppermute | solution.py:577
  67.3 13.2 %collective-permute-start.10 = (bf16[2,224,128]{2,1,0:T(8,128)(2,1)S(1)}, bf16[2,224,128]{2,1,0:T(8,128)(2,1)S(1)}, u32[]{:S(2)}, u32[]{:S(2)}) collective-permute-start(bf16[2,224,128]{2,1,0:T(8,128)(2,1)S(1)} %get-tuple-element.53.r_2_), channel_id=1, source_target_pairs={{0,1},{1,0},{2,3},{3,2},{4,5},{5,4},{6,7},{7,6},{8,9},{9,8},{10,11... | collective-permute-start | bytes 344072 | tf_op jit(solution)/shard_map/ppermute | solution.py:578
  68.0 12.6 %collective-permute-start.11 = (bf16[2,224,128]{2,1,0:T(8,128)(2,1)S(1)}, bf16[2,224,128]{2,1,0:T(8,128)(2,1)S(1)}, u32[]{:S(2)}, u32[]{:S(2)}) collective-permute-start(bf16[2,224,128]{2,1,0:T(8,128)(2,1)S(1)} %get-tuple-element.54.r_3_), channel_id=1, source_target_pairs={{0,31},{1,2},{2,1},{3,4},{4,3},{5,6},{6,5},{7,8},{8,7},{9,10},{10,... | collective-permute-start | bytes 344072 | tf_op jit(solution)/shard_map/ppermute | solution.py:577
  81.1 8.2 %collective-permute-start.12 = (bf16[2,224,128]{2,1,0:T(8,128)(2,1)S(1)}, bf16[2,224,128]{2,1,0:T(8,128)(2,1)S(1)}, u32[]{:S(2)}, u32[]{:S(2)}) collective-permute-start(bf16[2,224,128]{2,1,0:T(8,128)(2,1)S(1)} %get-tuple-element.57.r_2_), channel_id=1, source_target_pairs={{0,1},{1,0},{2,3},{3,2},{4,5},{5,4},{6,7},{7,6},{8,9},{9,8},{10,11... | collective-permute-start | bytes 344072 | tf_op jit(solution)/shard_map/ppermute | solution.py:578
  81.2 10.9 %collective-permute-start.13 = (bf16[2,224,128]{2,1,0:T(8,128)(2,1)S(1)}, bf16[2,224,128]{2,1,0:T(8,128)(2,1)S(1)}, u32[]{:S(2)}, u32[]{:S(2)}) collective-permute-start(bf16[2,224,128]{2,1,0:T(8,128)(2,1)S(1)} %get-tuple-element.58.r_3_), channel_id=1, source_target_pairs={{0,31},{1,2},{2,1},{3,4},{4,3},{5,6},{6,5},{7,8},{8,7},{9,10},{10,... | collective-permute-start | bytes 344072 | tf_op jit(solution)/shard_map/ppermute | solution.py:577
  (14 other events, 82.8 us)

commit v4 on v3

--- a/solution.py
+++ b/solution.py
@@ -167,7 +167,7 @@
         qe,
         qo,
     )
-    finish(copies[6:])
+    finish(copies[6:8])
 
 
 def lamb_body(u, xe, xo, ze, zo, table, vel, pooled):
@@ -286,48 +286,68 @@
     finish(copies)
 
 
-def stage_two_body(u, first, ue, uo, ce, co, ze, zo, after, inc, *scratch):
-    fa, hold, halo, sems = scratch
+def stage_two_inner_body(u, first, part, fa, hold, sems):
+    lane = iota((128, 128), 1)
+    fill_flux_a(inner_planes(first), fa)
+    copies = []
+    for x, rows in inner_planes(first):
+        v, p = primitives(rows)
+        fb = flux(rows, v, p, 1)
+        fc = flux(rows, v, p, 2)
+        for f in range(5):
+            total = diff_y(fb[f])
+            total = total + jnp.where(lane == 127, 0.0, roll_z(fc[f], -1))
+            total = total - jnp.where(lane == 0, 0.0, roll_z(fc[f], 1))
+            if x < 3:
+                total = total + fa[f, x + 2]
+            if x > 0:
+                total = total - fa[f, x]
+            hold[x, f] = 0.5 * ((rows[f] - u[f, x]) - (FLOW_STEP * 0.5) * total)
+        copies += begin(sems, x, (hold.at[x], part.at[:, x]))
+    finish(copies)
+
+
+def stage_two_body(part, ue, uo, ce, co, ze, zo, after, inc, *scratch):
+    hold, halo, sems = scratch
     lane = iota((128, 128), 1)
     even, even_z = is_even("space"), is_even("solver")
     e, o = jnp.where(even, 1, 0), jnp.where(even, 0, 1)
     fetch = begin(sems, 4, (ue, halo.at[e]), (uo, halo.at[o]))
-    fill_flux_a(inner_planes(first), fa)
-    finish(fetch)
-    outer = []
-    for i, x in enumerate((-1, 4)):
-        rows = []
-        for f in range(5):
-            by_even, by_odd = ce[f].astype(F32), co[f].astype(F32)
-            change = jnp.where(even, by_odd, by_even) if i == 0 else jnp.where(even, by_even, by_odd)
-            rows.append(halo[i, f] + change)
-        outer.append((x, rows))
-    fill_flux_a(outer, fa)
     below = jnp.where(even_z, zo[...], ze[...])
     above = jnp.where(even_z, ze[...], zo[...])
-    copies = []
-    for x in range(4):
-        rows, out = tendency_plane(
-            x,
-            lambda x: [first[f, x] for f in range(5)],
-            lambda x, f: fa[f, x + 2] - fa[f, x],
-            below,
-            above,
-            lane,
-        )
+    outer, copies = {}, []
+    for x in (1, 2, 0, 3):
+        if x in (0, 3):
+            if not outer:
+                finish(fetch)
+            i = x // 3
+            rows = []
+            for f in range(5):
+                by_even, by_odd = ce[f].astype(F32), co[f].astype(F32)
+                change = jnp.where(even, by_even, by_odd) if i else jnp.where(even, by_odd, by_even)
+                rows.append(halo[i, f] + change)
+            v, p = primitives(rows)
+            outer[x] = flux(rows, v, p, 0)
         for f in range(5):
-            hold[x, f] = 0.5 * ((rows[f] - u[f, x]) - (FLOW_STEP * 0.5) * out[f])
+            slot = f * 4 + x
+            extra = jnp.where(lane == 127, roll_z(above, 127 - slot), 0.0)
+            extra = extra - jnp.where(lane == 0, roll_z(below, -slot), 0.0)
+            if x == 0:
+                extra = extra - outer[x][f]
+            if x == 3:
+                extra = extra + outer[x][f]
+            hold[x, f] = part[f, x] - (FLOW_STEP * 0.25) * extra
         copies += begin(sems, x, (hold.at[x], inc.at[:, x]))
     finish(copies)
 
 
-def send_body(req, table, send, hold, sems):
-    wanted = req[...].reshape(128, 128).astype(F32).astype(BF16)
+def send_body(req, table, _, send, hold, sems):
+    wanted = req[...].reshape(128, 4).astype(F32).astype(BF16)
     row, col = iota((1024, 128), 0), iota((1024, 128), 1)
     spread = jnp.where(row // 8 == col, 1.0, 0.0).astype(BF16)
     rep = jnp.dot(spread, wanted, preferred_element_type=F32)
-    own = jnp.where(row % 4 == col, rep, 0.0).astype(BF16)
-    value = jnp.dot(own, jnp.ones((128, 128), BF16), preferred_element_type=F32)
+    own = jnp.where(iota((1024, 4), 0) % 4 == iota((1024, 4), 1), rep, 0.0).astype(BF16)
+    value = jnp.dot(own, jnp.ones((4, 128), BF16), preferred_element_type=F32)
     target = value + ((row % 8) // 4 * 16).astype(F32)
     pick = jnp.where(col.astype(F32) == target, 1.0, 0.0).astype(BF16)
     copies = []
@@ -356,8 +376,8 @@
     return jnp.concatenate([even[:, 0:128], odd[:, 0:128], even[:, 128:256], odd[:, 128:256]], 1)
 
 
-def prepare_body(nb_far, slot_far, after, gcat, ge, go, pick, esrc, edst, *scratch):
-    gcat_v, gx0_v, gx1_v, pick_v, esrc_v, edst_v, nb, slot, sems = scratch
+def prepare_body(nb_far, slot_far, _, gcat, ge, go, esrc, edst, spot_out, *scratch):
+    gcat_v, gx0_v, gx1_v, esrc_v, edst_v, spot_v, nb, slot, sems = scratch
     fetch = begin(sems, 0, (nb_far, nb), (slot_far, slot))
     me = lax.axis_index("solver") * lax.axis_size("space") + lax.axis_index("space")
     finish(fetch)
@@ -378,8 +398,8 @@
     column = 32.0 * coarse + fine
     lane = iota((EL, 128), 1).astype(F32)
 
-    def onehot(ref, col, width, shift=0.0):
-        number = column[col * EL : (col + 1) * EL] + shift
+    def onehot(ref, col, width):
+        number = column[col * EL : (col + 1) * EL]
         for t in range(0, width, 128):
             n = min(128, width - t)
             hit = jnp.where(lane + t == number, 1.0, 0.0).astype(BF16)
@@ -394,9 +414,8 @@
             hit = hit | (lane + t == column[(2 + f) * EL : (3 + f) * EL] + f * EL)
         gcat_v[:, t : t + 128] = jnp.where(hit, 1.0, 0.0).astype(BF16)
     copies += begin(sems, 4, (gcat_v, gcat))
-    onehot(pick_v.at[0], 6, 1024)
-    onehot(pick_v.at[1], 6, 1024, 4.0)
-    copies += begin(sems, 5, (pick_v, pick))
+    spot_v[...] = column[6 * EL : 7 * EL]
+    copies += begin(sems, 5, (spot_v, spot_out))
 
     def node(c, flip):
         face, a, b = c // 64, c % 64 // 8, c % 8
@@ -497,17 +516,22 @@
     finish(copies)
 
 
-def sources_body(got, pick, part, _, q1, src, lo, hi, token, pick_v, part_v, token_v, sems):
+def sources_body(got, spot, part, _, __, q1, src, lo, hi, token, spot_v, pick_v, part_v, token_v, sems):
     token_v[...] = jnp.zeros_like(token_v)
     copies = begin(
         sems,
         0,
-        (pick, pick_v),
+        (spot, spot_v),
         (part.at[0], q1.at[0]),
         *[(part.at[v], part_v.at[v - 1]) for v in (1, 2, 3)],
         (token_v, token),
     )
+    lane = iota((EL, 128), 1).astype(F32)
     copies[0].wait()
+    for parity in range(2):
+        number = spot_v[...] + 4.0 * parity
+        for t in range(0, 1024, 128):
+            pick_v[parity, :, t : t + 128] = jnp.where(lane + t == number, 1.0, 0.0).astype(BF16)
     for c in range(3):
         s = gather_source(got.at[:, 16 * c : 16 * c + 16, :], pick_v)
         src[c] = s.astype(BF16)
@@ -574,8 +598,7 @@
     count = lax.axis_size(axis)
     by_even = [(i, i + 1 - 2 * (i % 2)) for i in range(count)]
     by_odd = [(i, (i - 1 + 2 * (i % 2)) % count) for i in range(count)]
-    other = lax.ppermute(odd, axis, by_odd)
-    return lax.ppermute(even, axis, by_even), other
+    return lax.ppermute(even, axis, by_even), lax.ppermute(odd, axis, by_odd)
 
 
 def local(flow_state, acoustic_state, dx, dy, dz, requests, elem_slot, neighbours):
@@ -587,8 +610,6 @@
     keep = lambda *shape: pltpu.VMEM(shape, F32)
     keep_half = lambda *shape: pltpu.VMEM(shape, BF16)
 
-    wanted = jnp.pad(requests.reshape(128, 1, 4), ((0, 0), (0, 0), (0, 124)))
-    wanted = lax.all_to_all(wanted, both, split_axis=0, concat_axis=0, tiled=True)
     packs = call(
         edges_body,
         [plane, plane, column, column] + traces,
@@ -598,6 +619,8 @@
         far=(0, 1),
     )
     ue, uo, ze, zo, qe, qo = packs
+    wanted = requests.reshape(128, 1, 4)
+    wanted = lax.all_to_all(wanted, both, split_axis=0, concat_axis=0, tiled=True)
     ue, uo = swap(ue, uo, "space")
     ze, zo = swap(ze, zo, "solver")
     got_qe, got_qo = swap(qe, qo, "space")
@@ -609,27 +632,29 @@
         (flow_state, ue, uo, ze, zo),
         scratch=[keep(3, 6, 128, 128), keep(6, 128, 128)],
     )
+    shapes = [(EL, 4 * EL), (EL, 2 * EL), (EL, 2 * EL), (512, 256), (256, 512)]
+    gcat, ge, go, esrc, edst, spot = call(
+        prepare_body,
+        [half(*t) for t in shapes] + [full(EL, 128)],
+        "prepare",
+        (neighbours, elem_slot.reshape(1, EL), ue),
+        scratch=[keep_half(*t) for t in shapes]
+        + [keep(EL, 128), pltpu.VMEM((6, EL), I32), pltpu.VMEM((1, EL), I32), dma(8)],
+        far=(0, 1, 2),
+        far_out=range(6),
+    )
     table, got_qe, got_qo = lax.optimization_barrier((table, got_qe, got_qo))
     send = call(
         send_body,
         half(128, 48, 128),
         "send",
-        (wanted, table),
+        (wanted, table, gcat),
         scratch=[keep_half(3, 128, 16, 128), dma(3)],
+        far=(2,),
         far_out=(0,),
     )
     got = lax.all_to_all(send, both, split_axis=0, concat_axis=0, tiled=True)
 
-    shapes = [(EL, 4 * EL), (EL, 2 * EL), (EL, 2 * EL), (2, EL, 1024), (512, 256), (256, 512)]
-    gcat, ge, go, pick, esrc, edst = call(
-        prepare_body,
-        [half(*t) for t in shapes],
-        "prepare",
-        (neighbours, elem_slot.reshape(1, EL), send),
-        scratch=[keep_half(*t) for t in shapes] + [pltpu.VMEM((6, EL), I32), pltpu.VMEM((1, EL), I32), dma(8)],
-        far=(0, 1, 2),
-        far_out=range(6),
-    )
     first, ce, co, ye, yo = call(
         stage_one_body,
         [grid] + [half(5, 128, 128)] * 2 + [column, column],
@@ -661,13 +686,21 @@
         far_out=(0,),
     )
 
+    inner = call(
+        stage_two_inner_body,
+        grid,
+        "flow_inner",
+        (flow_state, first),
+        scratch=[keep(5, 6, 128, 128), keep(4, 5, 128, 128), dma(4)],
+        far_out=(0,),
+    )
     q1, src, qe, qo, token = call(
         sources_body,
         [state, half(3, EL, NODES)] + traces + [full(8, 128)],
         "sources",
-        (got, pick, part, yo),
-        scratch=[keep_half(2, EL, 1024), keep(3, EL, NODES), keep(8, 128), dma(6)],
-        far=(1, 2),
+        (got, spot, part, yo, inner),
+        scratch=[keep(EL, 128), keep_half(2, EL, 1024), keep(3, EL, NODES), keep(8, 128), dma(6)],
+        far=(1, 2, 4),
         far_out=(4,),
     )
     mats = (dx, dy, dz, gcat, esrc, edst)
@@ -676,9 +709,9 @@
         stage_two_body,
         grid,
         "flow_two",
-        (flow_state, first, ue, uo, ce, co, ye, yo, token),
-        scratch=[keep(5, 6, 128, 128), keep(4, 5, 128, 128), keep(2, 5, 128, 128), dma(6)],
-        far=(2, 3, 8),
+        (inner, ue, uo, ce, co, ye, yo, token),
+        scratch=[keep(4, 5, 128, 128), keep(2, 5, 128, 128), dma(6)],
+        far=(1, 2, 7),
         far_out=(0,),
     )
     part = call(

time: 94 us -> 92.4 us (0.983)
  waiting for transfers between devices: 11.7 us -> 7.96 us
  local copies, waits for them, and re-layouts: 0.89 us -> 2.16 us
    all_to_all x1, waiting for transfers between devices: 7.82 us -> 4.82 us  [local(): lax.all_to_all(wanted, both, split_axis=0, concat_axis=0, tiled=True)]
    unnamed x45 -> x47, local copies, waits for them, and re-layouts: 0.22 us -> 2.16 us
    pallas_call x12 -> x13, Pallas kernels: 33 us -> 33.2 us  [call(): pl.pallas_call(body, out_shape=outs if many else outs[0], in_specs=[space...]
  transfers between devices with their start and end apart: 16 -> 16, of which waited for: 4 -> 4; matrix products, arithmetic and copies ran while one was open for 1% -> 1% of each run, Pallas kernels for 28% -> 29%
where the time goes in v4:
time: 92.4 us; the launch traced here: 92.1 us
  starting transfers between devices  47.5 us (51%)
  Pallas kernels  33.2 us (36%)
  waiting for transfers between devices  7.96 us (9%)
  local copies, waits for them, and re-layouts  2.16 us (2%)
  between operations  1.27 us (1%)
    ppermute x14, starting transfers between devices, swap(): return (lax.ppermute(even, axis, by_even), lax.ppermute(odd, axis, by_odd))  33.7 us
    pallas_call x13, Pallas kernels, call(): pl.pallas_call(body, out_shape=outs if many else outs[0], in_specs=[space...  33.2 us
    all_to_all x1, starting transfers between devices, local(): lax.all_to_all(wanted, both, split_axis=0, concat_axis=0, tiled=True)  9.11 us
    all_to_all x1, waiting for transfers between devices, local(): lax.all_to_all(wanted, both, split_axis=0, concat_axis=0, tiled=True)  4.82 us
    all_to_all x1, starting transfers between devices, local(): got = lax.all_to_all(send, both, split_axis=0, concat_axis=0, tiled=True)  4.67 us
    ppermute x14, waiting for transfers between devices, swap(): return (lax.ppermute(even, axis, by_even), lax.ppermute(odd, axis, by_odd))  2.21 us
    unnamed x47, local copies, waits for them, and re-layouts  2.16 us
  transfers between devices with their start and end apart: 16, of which 4 were waited for; matrix products, arithmetic and copies ran while one was open for 1% of the time, Pallas kernels for 29%

profile of v4, /device:TPU:0, one launch (start us, length us, event | category | flops | bytes accessed | tf_op | source)
XLA Modules:
  0.0 92.1 jit_solution(10924212544151656369)
XLA Ops:
  0.6 2.5 %edges.1 = (f32[5,128,128]{2,1,0:T(8,128)S(1)}, f32[5,128,128]{2,1,0:T(8,128)S(1)}, f32[128,128]{1,0:T(8,128)S(1)}, f32[128,128]{1,0:T(8,128)S(1)}, bf16[2,224,1...) custom-call(f32[5,4,128,128]{3,2,1,0:T(8,128)} %u.7, bf16[4,224,512]{2,1,0:T(8,128)(2,1)} %q0.3), custom_call_target="tpu_custom_call" | custom-call | tf_op jit(solution)/shard_map/edges/pallas_call | solution.py:41
  3.2 1.7 %collective-permute-start = (f32[5,128,128]{2,1,0:T(8,128)S(1)}, f32[5,128,128]{2,1,0:T(8,128)S(1)}, u32[]{:S(2)}, u32[]{:S(2)}) collective-permute-start(f32[5,128,128]{2,1,0:T(8,128)S(1)} %get-tuple-element.32), channel_id=1, source_target_pairs={{0,1},{1,0},{2,3},{3,2},{4,5},{5,4},{6,7},{7,6},{8,9},{9,8},{10,11... | collective-permute-start | bytes 983048 | tf_op jit(solution)/shard_map/ppermute | solution.py:601
  4.8 7.9 %collective-permute-start.1 = (f32[5,128,128]{2,1,0:T(8,128)S(1)}, f32[5,128,128]{2,1,0:T(8,128)S(1)}, u32[]{:S(2)}, u32[]{:S(2)}) collective-permute-start(f32[5,128,128]{2,1,0:T(8,128)S(1)} %get-tuple-element.33), channel_id=1, source_target_pairs={{0,31},{1,2},{2,1},{3,4},{4,3},{5,6},{6,5},{7,8},{8,7},{9,10},{10,... | collective-permute-start | bytes 983048 | tf_op jit(solution)/shard_map/ppermute | solution.py:601
  12.7 1.2 %collective-permute-start.9 = (bf16[2,224,128]{2,1,0:T(8,128)(2,1)S(1)}, bf16[2,224,128]{2,1,0:T(8,128)(2,1)S(1)}, u32[]{:S(2)}, u32[]{:S(2)}) collective-permute-start(bf16[2,224,128]{2,1,0:T(8,128)(2,1)S(1)} %get-tuple-element.42.refs_10_), channel_id=1, source_target_pairs={{0,31},{1,2},{2,1},{3,4},{4,3},{5,6},{6,5},{7,8},{8,7},{9,10},{10,... | collective-permute-start | bytes 344072 | tf_op jit(solution)/shard_map/ppermute | solution.py:601
  15.5 9.1 %all-to-all-start = ((s32[128,1,4]{2,1,0:T(1,128)}), s32[128,1,4]{2,1,0:T(1,128)S(1)}, u32[]{:S(2)}, u32[]{:S(2)}) async-start(s32[128,1,4]{2,1,0:T(1,128)} %bitcast), calls=%async_computation | async-start | bytes 131072 | tf_op jit(solution)/shard_map/all_to_all | solution.py:623
  26.0 2.9 %prepare.1 = (bf16[224,896]{1,0:T(8,128)(2,1)}, bf16[224,448]{1,0:T(8,128)(2,1)}, bf16[224,448]{1,0:T(8,128)(2,1)}, bf16[512,256]{1,0:T(8,128)(2,1)}, bf16[256,512]{1,0:T(8,128)(2,1)}, /*index=5*/f32[224,128]{1,0:T(8,128)}) custom-call(s32[6,224]{1,0:T(8,128)} %nb_far.1, s32[1,224]{1,0:T(1,128)} %bitcast.2, f32[5,128,128]{2,1,0:T(8,128)} %copy-done.4), custom_call_target="tpu_custom_call" | custom-call | tf_op jit(solution)/shard_map/prepare/pallas_call | solution.py:41
  29.0 4.8 %all-to-all-done.req = s32[128,1,4]{2,1,0:T(1,128)S(1)} async-done(((s32[128,1,4]{2,1,0:T(1,128)}), s32[128,1,4]{2,1,0:T(1,128)S(1)}, u32[]{:S(2)}, u32[]{:S(2)}) %all-to-all-start) | async-done | bytes 2080 | tf_op jit(solution)/shard_map/all_to_all | solution.py:623
  33.8 1.9 %send.1 = bf16[128,48,128]{2,1,0:T(8,128)(2,1)} custom-call(s32[128,1,4]{2,1,0:T(1,128)S(1)} %all-to-all-done.req, bf16[128,768]{1,0:T(8,128)(2,1)S(1)} %lamb.1.table, bf16[224,896]{1,0:T(8,128)(2,1)} %get-tuple-element.44._.refs_2_.gcat), custom_call_target="tpu_custom_call" | custom-call | tf_op jit(solution)/shard_map/send/pallas_call | solution.py:41
  35.8 4.7 %all-to-all-start.1 = ((bf16[128,48,128]{2,1,0:T(8,128)(2,1)}), bf16[128,48,128]{2,1,0:T(8,128)(2,1)S(1)}, u32[]{:S(2)}, u32[]{:S(2)}) async-start(bf16[128,48,128]{2,1,0:T(8,128)(2,1)} %send.1), calls=%async_computation.1 | async-start | bytes 3145728 | tf_op jit(solution)/shard_map/all_to_all | solution.py:656
  40.5 4.1 %flow_one.1 = (f32[5,4,128,128]{3,2,1,0:T(8,128)}, bf16[5,128,128]{2,1,0:T(8,128)(2,1)}, bf16[5,128,128]{2,1,0:T(8,128)(2,1)}, f32[128,128]{1,0:T(8,128)}, f32[128,128]{1,0:T(8,128)}) custom-call(f32[5,4,128,128]{3,2,1,0:T(8,128)S(1)} %copy-done, f32[5,128,128]{2,1,0:T(8,128)} %copy-done.4, f32[5,128,128]{2,1,0:T(8,128)} %copy-done.9, ...), custom_call_target="tpu_custom_call" | custom-call | tf_op jit(solution)/shard_map/flow_one/pallas_call | solution.py:41
  44.6 1.2 %collective-permute-start.7 = (f32[128,128]{1,0:T(8,128)}, f32[128,128]{1,0:T(8,128)S(1)}, u32[]{:S(2)}, u32[]{:S(2)}) collective-permute-start(f32[128,128]{1,0:T(8,128)} %get-tuple-element.40), channel_id=1, source_target_pairs={{0,96},{32,64},{64,32},{96,0},{1,97},{33,65},{65,33},{97,1},{2,98}... | collective-permute-start | bytes 196616 | tf_op jit(solution)/shard_map/ppermute | solution.py:601
  45.8 1.5 %collective-permute-start.4 = (bf16[5,128,128]{2,1,0:T(8,128)(2,1)}, bf16[5,128,128]{2,1,0:T(8,128)(2,1)S(1)}, u32[]{:S(2)}, u32[]{:S(2)}) collective-permute-start(bf16[5,128,128]{2,1,0:T(8,128)(2,1)} %get-tuple-element.37), channel_id=1, source_target_pairs={{0,1},{1,0},{2,3},{3,2},{4,5},{5,4},{6,7},{7,6},{8,9},{9,8},{10,11... | collective-permute-start | bytes 491528 | tf_op jit(solution)/shard_map/ppermute | solution.py:601
  47.3 7.0 %collective-permute-start.5 = (bf16[5,128,128]{2,1,0:T(8,128)(2,1)}, bf16[5,128,128]{2,1,0:T(8,128)(2,1)S(1)}, u32[]{:S(2)}, u32[]{:S(2)}) collective-permute-start(bf16[5,128,128]{2,1,0:T(8,128)(2,1)} %get-tuple-element.38), channel_id=1, source_target_pairs={{0,31},{1,2},{2,1},{3,4},{4,3},{5,6},{6,5},{7,8},{8,7},{9,10},{10,... | collective-permute-start | bytes 491528 | tf_op jit(solution)/shard_map/ppermute | solution.py:601
  54.4 1.3 %copy-done.5 = f32[5,4,128,128]{3,2,1,0:T(8,128)S(1)} copy-done((f32[5,4,128,128]{3,2,1,0:T(8,128)S(1)}, f32[5,4,128,128]{3,2,1,0:T(8,128)}, u32[]{:S(2)}) %copy-start.5) | copy-done | bytes 1310744
  55.7 1.8 %flow_inner.1.__.part = f32[5,4,128,128]{3,2,1,0:T(8,128)} custom-call(f32[5,4,128,128]{3,2,1,0:T(8,128)S(1)} %copy-done, f32[5,4,128,128]{3,2,1,0:T(8,128)S(1)} %copy-done.5), custom_call_target="tpu_custom_call" | custom-call | tf_op jit(solution)/shard_map/flow_inner/pallas_call | solution.py:41
  57.5 5.9 %sound_zero.1.part = f32[4,224,512]{2,1,0:T(8,128)} custom-call(bf16[4,224,512]{2,1,0:T(8,128)(2,1)} %q0.3, bf16[512,256]{1,0:T(8,128)(2,1)} %get-tuple-element.46.refs_1_.esrc, bf16[224,896]{1,0:T(8,128)(2,1)} %get-tuple-element.44._.refs_2_.gcat, bf16[256,512]{1,0:T(8,128)(2,1)} %get-tuple-element.47.refs_3_.edst, bf16[512,512]{1,0:T(8,128)(2,1)} %dx.3, ...), custom_call_target="tpu_custom_call" | custom-call | tf_op jit(solution)/shard_map/sound_zero/pallas_call | solution.py:41
  64.4 2.6 %sources.1 = (f32[4,224,512]{2,1,0:T(8,128)S(1)}, bf16[3,224,512]{2,1,0:T(8,128)(2,1)S(1)}, bf16[2,224,128]{2,1,0:T(8,128)(2,1)S(1)}, bf16[2,224,128]{2,1,0:T(8,128)(2,1)S(1)}, f32[8,128]{1,0:T(8,128)}) custom-call(bf16[128,48,128]{2,1,0:T(8,128)(2,1)S(1)} %all-to-all-done.1.got, f32[224,128]{1,0:T(8,128)} %get-tuple-element.45.spot, ...), custom_call_target="tpu_custom_call" | custom-call | tf_op jit(solution)/shard_map/sources/pallas_call | solution.py:41
  67.6 6.2 %collective-permute-start.11 = (bf16[2,224,128]{2,1,0:T(8,128)(2,1)S(1)}, bf16[2,224,128]{2,1,0:T(8,128)(2,1)S(1)}, u32[]{:S(2)}, u32[]{:S(2)}) collective-permute-start(bf16[2,224,128]{2,1,0:T(8,128)(2,1)S(1)} %get-tuple-element.54.r_3_), channel_id=1, source_target_pairs={{0,31},{1,2},{2,1},{3,4},{4,3},{5,6},{6,5},{7,8},{8,7},{9,10},{10,... | collective-permute-start | bytes 344072 | tf_op jit(solution)/shard_map/ppermute | solution.py:601
  73.9 2.7 %flow_two.1.after = f32[5,4,128,128]{3,2,1,0:T(8,128)} custom-call(f32[5,4,128,128]{3,2,1,0:T(8,128)S(1)} %copy-done.2, f32[5,128,128]{2,1,0:T(8,128)} %copy-done.4, f32[5,128,128]{2,1,0:T(8,128)} %copy-done.9, bf16[5,128,128]{2,1,0:T(8,128)(2,1)S(1)} %collective-permute-done.4.ce, bf16[5,128,128]{2,1,0:T(8,128)(2,1)S(1)} %collective-permute-done.5.co, ...), custom_call_target="tpu_custom_call" | custom-call | tf_op jit(solution)/shard_map/flow_two/pallas_call | solution.py:41
  76.7 2.6 %sound_one.1.r_6_.mid = f32[4,224,512]{2,1,0:T(8,128)S(1)} custom-call(bf16[4,224,512]{2,1,0:T(8,128)(2,1)S(1)} %copy-done.1, f32[4,224,512]{2,1,0:T(8,128)S(1)} %get-tuple-element.55.q1, bf16[3,224,512]{2,1,0:T(8,128)(2,1)S(1)} %get-tuple-element.56.src, bf16[512,512]{1,0:T(8,128)(2,1)S(1)} %copy-done.6, bf16[512,512]{1,0:T(8,128)(2,1)S(1)} %copy-done.7, ...), custom_call_target="tpu_custom_call" | custom-call | tf_op jit(solution)/shard_map/sound_one/pallas_call | solution.py:41
  79.9 5.5 %collective-permute-start.13 = (bf16[2,224,128]{2,1,0:T(8,128)(2,1)S(1)}, bf16[2,224,128]{2,1,0:T(8,128)(2,1)S(1)}, u32[]{:S(2)}, u32[]{:S(2)}) collective-permute-start(bf16[2,224,128]{2,1,0:T(8,128)(2,1)S(1)} %get-tuple-element.58.r_3_), channel_id=1, source_target_pairs={{0,31},{1,2},{2,1},{3,4},{4,3},{5,6},{6,5},{7,8},{8,7},{9,10},{10,... | collective-permute-start | bytes 344072 | tf_op jit(solution)/shard_map/ppermute | solution.py:601
  85.4 3.4 %sound_two.1 = (f32[4,224,512]{2,1,0:T(8,128)}, f32[2,4,224,128]{3,2,1,0:T(8,128)S(1)}) custom-call(bf16[4,224,512]{2,1,0:T(8,128)(2,1)S(1)} %copy-done.1, f32[4,224,512]{2,1,0:T(8,128)S(1)} %sound_one.1.r_6_.mid, f32[2,4,224,128]{3,2,1,0:T(8,128)S(1)} %get-tuple-element.59.ends, bf16[3,224,512]{2,1,0:T(8,128)(2,1)S(1)} %get-tuple-element.56.src, ...), custom_call_target="tpu_custom_call" | custom-call | tf_op jit(solution)/shard_map/sound_two/pallas_call | solution.py:41
  88.8 1.8 %collective-permute-done.13.r_5_ = bf16[2,224,128]{2,1,0:T(8,128)(2,1)S(1)} collective-permute-done((bf16[2,224,128]{2,1,0:T(8,128)(2,1)S(1)}, bf16[2,224,128]{2,1,0:T(8,128)(2,1)S(1)}, u32[]{:S(2)}, u32[]{:S(2)}) %collective-permute-start.13) | collective-permute-done | bytes 114720 | tf_op jit(solution)/shard_map/ppermute | solution.py:601
  90.5 1.4 %cross_two.1 = f32[4,224,512]{2,1,0:T(8,128)} custom-call(bf16[224,448]{1,0:T(8,128)(2,1)S(1)} %copy-done.12, bf16[224,448]{1,0:T(8,128)(2,1)S(1)} %copy-done.13, bf16[2,224,128]{2,1,0:T(8,128)(2,1)S(1)} %get-tuple-element.57.r_2_, bf16[2,224,128]{2,1,0:T(8,128)(2,1)S(1)} %get-tuple-element.58.r_3_, ...), custom_call_target="tpu_custom_call", output_to_operand_aliasing={{}: (7, {})} | custom-call | tf_op jit(solution)/shard_map/cross_two/pallas_call | solution.py:41
  (68 shorter events, 5.3 us)
Async XLA Ops:
  0.6 24.3 %copy-start = (f32[5,4,128,128]{3,2,1,0:T(8,128)S(1)}, f32[5,4,128,128]{3,2,1,0:T(8,128)}, u32[]{:S(2)}) copy-start(f32[5,4,128,128]{3,2,1,0:T(8,128)} %u.7) | copy-start | bytes 3932164
  0.6 14.1 %copy-start.22 = (s32[1,128,4]{1,2,0:T(4,128)S(1)}, s32[1,128,4]{1,2,0:T(4,128)}, u32[]{:S(2)}) copy-start(s32[1,128,4]{1,2,0:T(4,128)} %param.13) | copy-start | bytes 6148
  3.2 32.6 %copy-start.16 = (bf16[2,224,128]{2,1,0:T(8,128)(2,1)}, bf16[2,224,128]{2,1,0:T(8,128)(2,1)S(1)}, u32[]{:S(2)}) copy-start(bf16[2,224,128]{2,1,0:T(8,128)(2,1)S(1)} %get-tuple-element.41.refs_9_) | copy-start | bytes 344068
  3.2 32.6 %copy-start.17 = (bf16[2,224,128]{2,1,0:T(8,128)(2,1)}, bf16[2,224,128]{2,1,0:T(8,128)(2,1)S(1)}, u32[]{:S(2)}) copy-start(bf16[2,224,128]{2,1,0:T(8,128)(2,1)S(1)} %get-tuple-element.42.refs_10_) | copy-start | bytes 344068
  3.2 21.7 %collective-permute-start = (f32[5,128,128]{2,1,0:T(8,128)S(1)}, f32[5,128,128]{2,1,0:T(8,128)S(1)}, u32[]{:S(2)}, u32[]{:S(2)}) collective-permute-start(f32[5,128,128]{2,1,0:T(8,128)S(1)} %get-tuple-element.32), channel_id=1, source_target_pairs={{0,1},{1,0},{2,3},{3,2},{4,5},{5,4},{6,7},{7,6},{8,9},{9,8},{10,11... | collective-permute-start | bytes 983048 | tf_op jit(solution)/shard_map/ppermute | solution.py:601
  4.8 20.1 %collective-permute-start.1 = (f32[5,128,128]{2,1,0:T(8,128)S(1)}, f32[5,128,128]{2,1,0:T(8,128)S(1)}, u32[]{:S(2)}, u32[]{:S(2)}) collective-permute-start(f32[5,128,128]{2,1,0:T(8,128)S(1)} %get-tuple-element.33), channel_id=1, source_target_pairs={{0,31},{1,2},{2,1},{3,4},{4,3},{5,6},{6,5},{7,8},{8,7},{9,10},{10,... | collective-permute-start | bytes 983048 | tf_op jit(solution)/shard_map/ppermute | solution.py:601
  12.7 1.3 %collective-permute-start.2 = (f32[128,128]{1,0:T(8,128)S(1)}, f32[128,128]{1,0:T(8,128)S(1)}, u32[]{:S(2)}, u32[]{:S(2)}) collective-permute-start(f32[128,128]{1,0:T(8,128)S(1)} %get-tuple-element.34), channel_id=1, source_target_pairs={{0,32},{32,0},{64,96},{96,64},{1,33},{33,1},{65,97},{97,65},{2,34}... | collective-permute-start | bytes 196616 | tf_op jit(solution)/shard_map/ppermute | solution.py:601
  12.7 13.3 %collective-permute-start.8 = (bf16[2,224,128]{2,1,0:T(8,128)(2,1)S(1)}, bf16[2,224,128]{2,1,0:T(8,128)(2,1)S(1)}, u32[]{:S(2)}, u32[]{:S(2)}) collective-permute-start(bf16[2,224,128]{2,1,0:T(8,128)(2,1)S(1)} %get-tuple-element.41.refs_9_), channel_id=1, source_target_pairs={{0,1},{1,0},{2,3},{3,2},{4,5},{5,4},{6,7},{7,6},{8,9},{9,8},{10,11... | collective-permute-start | bytes 344072 | tf_op jit(solution)/shard_map/ppermute | solution.py:601
  12.7 13.3 %collective-permute-start.9 = (bf16[2,224,128]{2,1,0:T(8,128)(2,1)S(1)}, bf16[2,224,128]{2,1,0:T(8,128)(2,1)S(1)}, u32[]{:S(2)}, u32[]{:S(2)}) collective-permute-start(bf16[2,224,128]{2,1,0:T(8,128)(2,1)S(1)} %get-tuple-element.42.refs_10_), channel_id=1, source_target_pairs={{0,31},{1,2},{2,1},{3,4},{4,3},{5,6},{6,5},{7,8},{8,7},{9,10},{10,... | collective-permute-start | bytes 344072 | tf_op jit(solution)/shard_map/ppermute | solution.py:601
  13.9 21.8 %copy-start.14 = (f32[128,128]{1,0:T(8,128)}, f32[128,128]{1,0:T(8,128)S(1)}, u32[]{:S(2)}) copy-start(f32[128,128]{1,0:T(8,128)S(1)} %collective-permute-done.2.ze) | copy-start | bytes 196612
  13.9 11.0 %collective-permute-start.3 = (f32[128,128]{1,0:T(8,128)S(1)}, f32[128,128]{1,0:T(8,128)S(1)}, u32[]{:S(2)}, u32[]{:S(2)}) collective-permute-start(f32[128,128]{1,0:T(8,128)S(1)} %get-tuple-element.35), channel_id=1, source_target_pairs={{0,96},{32,64},{64,32},{96,0},{1,97},{33,65},{65,33},{97,1},{2,98}... | collective-permute-start | bytes 196616 | tf_op jit(solution)/shard_map/ppermute | solution.py:601
  15.5 18.3 %all-to-all-start = ((s32[128,1,4]{2,1,0:T(1,128)}), s32[128,1,4]{2,1,0:T(1,128)S(1)}, u32[]{:S(2)}, u32[]{:S(2)}) async-start(s32[128,1,4]{2,1,0:T(1,128)} %bitcast), calls=%async_computation | async-start | bytes 131072 | tf_op jit(solution)/shard_map/all_to_all | solution.py:623
  24.9 10.8 %copy-start.15 = (f32[128,128]{1,0:T(8,128)}, f32[128,128]{1,0:T(8,128)S(1)}, u32[]{:S(2)}) copy-start(f32[128,128]{1,0:T(8,128)S(1)} %collective-permute-done.3.zo) | copy-start | bytes 196612
  24.9 10.8 %copy-start.9 = (f32[5,128,128]{2,1,0:T(8,128)}, f32[5,128,128]{2,1,0:T(8,128)S(1)}, u32[]{:S(2)}) copy-start(f32[5,128,128]{2,1,0:T(8,128)S(1)} %collective-permute-done.1.uo.xo) | copy-start | bytes 983044
  26.0 9.8 %copy-start.18 = (bf16[2,224,128]{2,1,0:T(8,128)(2,1)}, bf16[2,224,128]{2,1,0:T(8,128)(2,1)S(1)}, u32[]{:S(2)}) copy-start(bf16[2,224,128]{2,1,0:T(8,128)(2,1)S(1)} %collective-permute-done.8.refs_11_) | copy-start | bytes 344068
  35.8 28.6 %all-to-all-start.1 = ((bf16[128,48,128]{2,1,0:T(8,128)(2,1)}), bf16[128,48,128]{2,1,0:T(8,128)(2,1)S(1)}, u32[]{:S(2)}, u32[]{:S(2)}) async-start(bf16[128,48,128]{2,1,0:T(8,128)(2,1)} %send.1), calls=%async_computation.1 | async-start | bytes 3145728 | tf_op jit(solution)/shard_map/all_to_all | solution.py:656
  44.5 13.0 %collective-permute-start.6 = (f32[128,128]{1,0:T(8,128)}, f32[128,128]{1,0:T(8,128)S(1)}, u32[]{:S(2)}, u32[]{:S(2)}) collective-permute-start(f32[128,128]{1,0:T(8,128)} %get-tuple-element.39), channel_id=1, source_target_pairs={{0,32},{32,0},{64,96},{96,64},{1,33},{33,1},{65,97},{97,65},{2,34}... | collective-permute-start | bytes 196616 | tf_op jit(solution)/shard_map/ppermute | solution.py:601
  44.6 18.8 %collective-permute-start.7 = (f32[128,128]{1,0:T(8,128)}, f32[128,128]{1,0:T(8,128)S(1)}, u32[]{:S(2)}, u32[]{:S(2)}) collective-permute-start(f32[128,128]{1,0:T(8,128)} %get-tuple-element.40), channel_id=1, source_target_pairs={{0,96},{32,64},{64,32},{96,0},{1,97},{33,65},{65,33},{97,1},{2,98}... | collective-permute-start | bytes 196616 | tf_op jit(solution)/shard_map/ppermute | solution.py:601
  45.8 28.0 %collective-permute-start.4 = (bf16[5,128,128]{2,1,0:T(8,128)(2,1)}, bf16[5,128,128]{2,1,0:T(8,128)(2,1)S(1)}, u32[]{:S(2)}, u32[]{:S(2)}) collective-permute-start(bf16[5,128,128]{2,1,0:T(8,128)(2,1)} %get-tuple-element.37), channel_id=1, source_target_pairs={{0,1},{1,0},{2,3},{3,2},{4,5},{5,4},{6,7},{7,6},{8,9},{9,8},{10,11... | collective-permute-start | bytes 491528 | tf_op jit(solution)/shard_map/ppermute | solution.py:601
  47.3 26.5 %collective-permute-start.5 = (bf16[5,128,128]{2,1,0:T(8,128)(2,1)}, bf16[5,128,128]{2,1,0:T(8,128)(2,1)S(1)}, u32[]{:S(2)}, u32[]{:S(2)}) collective-permute-start(bf16[5,128,128]{2,1,0:T(8,128)(2,1)} %get-tuple-element.38), channel_id=1, source_target_pairs={{0,31},{1,2},{2,1},{3,4},{4,3},{5,6},{6,5},{7,8},{8,7},{9,10},{10,... | collective-permute-start | bytes 491528 | tf_op jit(solution)/shard_map/ppermute | solution.py:601
  67.0 12.3 %collective-permute-start.10 = (bf16[2,224,128]{2,1,0:T(8,128)(2,1)S(1)}, bf16[2,224,128]{2,1,0:T(8,128)(2,1)S(1)}, u32[]{:S(2)}, u32[]{:S(2)}) collective-permute-start(bf16[2,224,128]{2,1,0:T(8,128)(2,1)S(1)} %get-tuple-element.53.r_2_), channel_id=1, source_target_pairs={{0,1},{1,0},{2,3},{3,2},{4,5},{5,4},{6,7},{7,6},{8,9},{9,8},{10,11... | collective-permute-start | bytes 344072 | tf_op jit(solution)/shard_map/ppermute | solution.py:601
  67.6 11.6 %collective-permute-start.11 = (bf16[2,224,128]{2,1,0:T(8,128)(2,1)S(1)}, bf16[2,224,128]{2,1,0:T(8,128)(2,1)S(1)}, u32[]{:S(2)}, u32[]{:S(2)}) collective-permute-start(bf16[2,224,128]{2,1,0:T(8,128)(2,1)S(1)} %get-tuple-element.54.r_3_), channel_id=1, source_target_pairs={{0,31},{1,2},{2,1},{3,4},{4,3},{5,6},{6,5},{7,8},{8,7},{9,10},{10,... | collective-permute-start | bytes 344072 | tf_op jit(solution)/shard_map/ppermute | solution.py:601
  79.8 9.0 %collective-permute-start.12 = (bf16[2,224,128]{2,1,0:T(8,128)(2,1)S(1)}, bf16[2,224,128]{2,1,0:T(8,128)(2,1)S(1)}, u32[]{:S(2)}, u32[]{:S(2)}) collective-permute-start(bf16[2,224,128]{2,1,0:T(8,128)(2,1)S(1)} %get-tuple-element.57.r_2_), channel_id=1, source_target_pairs={{0,1},{1,0},{2,3},{3,2},{4,5},{5,4},{6,7},{7,6},{8,9},{9,8},{10,11... | collective-permute-start | bytes 344072 | tf_op jit(solution)/shard_map/ppermute | solution.py:601
  79.9 10.7 %collective-permute-start.13 = (bf16[2,224,128]{2,1,0:T(8,128)(2,1)S(1)}, bf16[2,224,128]{2,1,0:T(8,128)(2,1)S(1)}, u32[]{:S(2)}, u32[]{:S(2)}) collective-permute-start(bf16[2,224,128]{2,1,0:T(8,128)(2,1)S(1)} %get-tuple-element.58.r_3_), channel_id=1, source_target_pairs={{0,31},{1,2},{2,1},{3,4},{4,3},{5,6},{6,5},{7,8},{8,7},{9,10},{10,... | collective-permute-start | bytes 344072 | tf_op jit(solution)/shard_map/ppermute | solution.py:601
  (15 other events, 49.9 us)

commit v5 on v4

--- a/solution.py
+++ b/solution.py
@@ -139,8 +139,9 @@
         odd_ref[w] = jnp.where(even, lower[w], upper[w]).astype(BF16)
 
 
-def edges_body(u, q, ue, uo, ze, zo, qe, qo, planes, ends, sems):
+def edges_body(u, q, req, ue, uo, ze, zo, qe, qo, want, planes, ends, req_v, sems):
     even = is_even("space")
+    ask = begin(sems, 8, (req, req_v))
     copies = begin(
         sems,
         0,
@@ -152,6 +153,12 @@
     )
     lane = iota((128, 128), 1)
     lo = hi = jnp.zeros((128, 128), F32)
+    eye = iota((128, 128), 0) == lane
+    place = jnp.where(iota((512, 128), 0) // 128 == iota((512, 128), 1), 1.0, 0.0).astype(BF16)
+    finish(ask)
+    value = req_v[...].astype(F32)
+    spread = [jnp.where(eye, value[c : c + 1], 0.0).astype(BF16) for c in range(4)]
+    want[...] = jnp.dot(jnp.concatenate(spread, 1), place, preferred_element_type=F32)
     for x in range(4):
         copies[x].wait()
         rows = [planes[x, f] for f in range(5)]
@@ -342,12 +349,12 @@
 
 
 def send_body(req, table, _, send, hold, sems):
-    wanted = req[...].reshape(128, 4).astype(F32).astype(BF16)
+    wanted = req[...].astype(BF16)
     row, col = iota((1024, 128), 0), iota((1024, 128), 1)
     spread = jnp.where(row // 8 == col, 1.0, 0.0).astype(BF16)
     rep = jnp.dot(spread, wanted, preferred_element_type=F32)
-    own = jnp.where(iota((1024, 4), 0) % 4 == iota((1024, 4), 1), rep, 0.0).astype(BF16)
-    value = jnp.dot(own, jnp.ones((4, 128), BF16), preferred_element_type=F32)
+    own = jnp.where(row % 4 == col, rep, 0.0).astype(BF16)
+    value = jnp.dot(own, jnp.ones((128, 128), BF16), preferred_element_type=F32)
     target = value + ((row % 8) // 4 * 16).astype(F32)
     pick = jnp.where(col.astype(F32) == target, 1.0, 0.0).astype(BF16)
     copies = []
@@ -612,15 +619,16 @@
 
     packs = call(
         edges_body,
-        [plane, plane, column, column] + traces,
+        [plane, plane, column, column] + traces + [column],
         "edges",
-        (flow_state, acoustic_state),
-        scratch=[keep(4, 5, 128, 128), keep_half(2, 4, EL, 128), dma(8)],
-        far=(0, 1),
-    )
-    ue, uo, ze, zo, qe, qo = packs
-    wanted = requests.reshape(128, 1, 4)
-    wanted = lax.all_to_all(wanted, both, split_axis=0, concat_axis=0, tiled=True)
+        (flow_state, acoustic_state, requests.reshape(128, 4).T),
+        scratch=[keep(4, 5, 128, 128), keep_half(2, 4, EL, 128), pltpu.VMEM((4, 128), I32), dma(9)],
+        far=(0, 1, 2),
+    )
+    ue, uo, ze, zo, qe, qo, wanted = packs
+    wanted = lax.all_to_all(
+        wanted.reshape(128, 1, 128), both, split_axis=0, concat_axis=0, tiled=True
+    ).reshape(128, 128)
     ue, uo = swap(ue, uo, "space")
     ze, zo = swap(ze, zo, "solver")
     got_qe, got_qo = swap(qe, qo, "space")

time: 92.4 us -> 92.3 us (level)
    unnamed x47 -> x44, local copies, waits for them, and re-layouts: 2.16 us -> 1.41 us
  transfers between devices with their start and end apart: 16 -> 16, of which waited for: 4 -> 4; matrix products, arithmetic and copies ran while one was open for 1% -> 0% of each run, Pallas kernels for 29% -> 29%
where the time goes in v5:
time: 92.3 us; the launch traced here: 92 us
  starting transfers between devices  47.5 us (51%)
  Pallas kernels  33.9 us (37%)
  waiting for transfers between devices  7.96 us (9%)
  local copies, waits for them, and re-layouts  1.41 us (2%)
  between operations  1.26 us (1%)
    pallas_call x13, Pallas kernels, call(): pl.pallas_call(body, out_shape=outs if many else outs[0], in_specs=[space...  33.9 us
    ppermute x14, starting transfers between devices, swap(): return (lax.ppermute(even, axis, by_even), lax.ppermute(odd, axis, by_odd))  33.7 us
    all_to_all x1, starting transfers between devices, local(): lax.all_to_all(wanted.reshape(128, 1, 128), both, split_axis=0, concat_ax...  9.11 us
    all_to_all x1, starting transfers between devices, local(): got = lax.all_to_all(send, both, split_axis=0, concat_axis=0, tiled=True)  4.66 us
    all_to_all x1, waiting for transfers between devices, local(): lax.all_to_all(wanted.reshape(128, 1, 128), both, split_axis=0, concat_ax...  4.11 us
    ppermute x14, waiting for transfers between devices, swap(): return (lax.ppermute(even, axis, by_even), lax.ppermute(odd, axis, by_odd))  2.94 us
  transfers between devices with their start and end apart: 16, of which 4 were waited for; matrix products, arithmetic and copies ran while one was open for 0% of the time, Pallas kernels for 29%

profile of v5, /device:TPU:0, one launch (start us, length us, event | category | flops | bytes accessed | tf_op | source)
XLA Modules:
  0.0 92.0 jit_solution(4375463046371973692)
XLA Ops:
  0.6 3.1 %edges.1 = (f32[5,128,128]{2,1,0:T(8,128)S(1)}, f32[5,128,128]{2,1,0:T(8,128)S(1)}, f32[128,128]{1,0:T(8,128)S(1)}, f32[128,128]{1,0:T(8,128)S(1)}, bf16[2,224,1...) custom-call(f32[5,4,128,128]{3,2,1,0:T(8,128)} %u.7, bf16[4,224,512]{2,1,0:T(8,128)(2,1)} %q0.3, ...), custom_call_target="tpu_custom_call" | custom-call | tf_op jit(solution)/shard_map/edges/pallas_call | solution.py:41
  3.8 1.7 %collective-permute-start = (f32[5,128,128]{2,1,0:T(8,128)S(1)}, f32[5,128,128]{2,1,0:T(8,128)S(1)}, u32[]{:S(2)}, u32[]{:S(2)}) collective-permute-start(f32[5,128,128]{2,1,0:T(8,128)S(1)} %get-tuple-element.33), channel_id=1, source_target_pairs={{0,1},{1,0},{2,3},{3,2},{4,5},{5,4},{6,7},{7,6},{8,9},{9,8},{10,11... | collective-permute-start | bytes 983048 | tf_op jit(solution)/shard_map/ppermute | solution.py:608
  5.5 7.9 %collective-permute-start.1 = (f32[5,128,128]{2,1,0:T(8,128)S(1)}, f32[5,128,128]{2,1,0:T(8,128)S(1)}, u32[]{:S(2)}, u32[]{:S(2)}) collective-permute-start(f32[5,128,128]{2,1,0:T(8,128)S(1)} %get-tuple-element.34), channel_id=1, source_target_pairs={{0,31},{1,2},{2,1},{3,4},{4,3},{5,6},{6,5},{7,8},{8,7},{9,10},{10,... | collective-permute-start | bytes 983048 | tf_op jit(solution)/shard_map/ppermute | solution.py:608
  13.3 1.2 %collective-permute-start.9 = (bf16[2,224,128]{2,1,0:T(8,128)(2,1)S(1)}, bf16[2,224,128]{2,1,0:T(8,128)(2,1)S(1)}, u32[]{:S(2)}, u32[]{:S(2)}) collective-permute-start(bf16[2,224,128]{2,1,0:T(8,128)(2,1)S(1)} %get-tuple-element.44.refs_10_), channel_id=1, source_target_pairs={{0,31},{1,2},{2,1},{3,4},{4,3},{5,6},{6,5},{7,8},{8,7},{9,10},{10,... | collective-permute-start | bytes 344072 | tf_op jit(solution)/shard_map/ppermute | solution.py:608
  15.4 9.1 %all-to-all-start = ((f32[128,1,128]{2,1,0:T(1,128)}), f32[128,1,128]{2,1,0:T(1,128)S(1)}, u32[]{:S(2)}, u32[]{:S(2)}) async-start(f32[128,1,128]{2,1,0:T(1,128)} %bitcast.3), calls=%async_computation | async-start | bytes 131072 | tf_op jit(solution)/shard_map/all_to_all | solution.py:629
  26.7 2.9 %prepare.1 = (bf16[224,896]{1,0:T(8,128)(2,1)}, bf16[224,448]{1,0:T(8,128)(2,1)}, bf16[224,448]{1,0:T(8,128)(2,1)}, bf16[512,256]{1,0:T(8,128)(2,1)}, bf16[256,512]{1,0:T(8,128)(2,1)}, /*index=5*/f32[224,128]{1,0:T(8,128)}) custom-call(s32[6,224]{1,0:T(8,128)} %nb_far.1, s32[1,224]{1,0:T(1,128)} %bitcast.10, f32[5,128,128]{2,1,0:T(8,128)} %copy-done.4), custom_call_target="tpu_custom_call" | custom-call | tf_op jit(solution)/shard_map/prepare/pallas_call | solution.py:41
  29.6 4.1 %all-to-all-done = f32[128,1,128]{2,1,0:T(1,128)S(1)} async-done(((f32[128,1,128]{2,1,0:T(1,128)}), f32[128,1,128]{2,1,0:T(1,128)S(1)}, u32[]{:S(2)}, u32[]{:S(2)}) %all-to-all-start) | async-done | bytes 65568 | tf_op jit(solution)/shard_map/all_to_all | solution.py:629
  33.7 1.9 %send.1 = bf16[128,48,128]{2,1,0:T(8,128)(2,1)} custom-call(f32[128,128]{1,0:T(8,128)S(1)} %bitcast.8, bf16[128,768]{1,0:T(8,128)(2,1)S(1)} %lamb.1.table, bf16[224,896]{1,0:T(8,128)(2,1)} %get-tuple-element.46._.refs_2_.gcat), custom_call_target="tpu_custom_call" | custom-call | tf_op jit(solution)/shard_map/send/pallas_call | solution.py:41
  35.7 4.7 %all-to-all-start.1 = ((bf16[128,48,128]{2,1,0:T(8,128)(2,1)}), bf16[128,48,128]{2,1,0:T(8,128)(2,1)S(1)}, u32[]{:S(2)}, u32[]{:S(2)}) async-start(bf16[128,48,128]{2,1,0:T(8,128)(2,1)} %send.1), calls=%async_computation.1 | async-start | bytes 3145728 | tf_op jit(solution)/shard_map/all_to_all | solution.py:664
  40.4 4.1 %flow_one.1 = (f32[5,4,128,128]{3,2,1,0:T(8,128)}, bf16[5,128,128]{2,1,0:T(8,128)(2,1)}, bf16[5,128,128]{2,1,0:T(8,128)(2,1)}, f32[128,128]{1,0:T(8,128)}, f32[128,128]{1,0:T(8,128)}) custom-call(f32[5,4,128,128]{3,2,1,0:T(8,128)S(1)} %copy-done, f32[5,128,128]{2,1,0:T(8,128)} %copy-done.4, f32[5,128,128]{2,1,0:T(8,128)} %copy-done.9, ...), custom_call_target="tpu_custom_call" | custom-call | tf_op jit(solution)/shard_map/flow_one/pallas_call | solution.py:41
  44.6 1.2 %collective-permute-start.7 = (f32[128,128]{1,0:T(8,128)}, f32[128,128]{1,0:T(8,128)S(1)}, u32[]{:S(2)}, u32[]{:S(2)}) collective-permute-start(f32[128,128]{1,0:T(8,128)} %get-tuple-element.41), channel_id=1, source_target_pairs={{0,96},{32,64},{64,32},{96,0},{1,97},{33,65},{65,33},{97,1},{2,98}... | collective-permute-start | bytes 196616 | tf_op jit(solution)/shard_map/ppermute | solution.py:608
  45.7 1.5 %collective-permute-start.4 = (bf16[5,128,128]{2,1,0:T(8,128)(2,1)}, bf16[5,128,128]{2,1,0:T(8,128)(2,1)S(1)}, u32[]{:S(2)}, u32[]{:S(2)}) collective-permute-start(bf16[5,128,128]{2,1,0:T(8,128)(2,1)} %get-tuple-element.38), channel_id=1, source_target_pairs={{0,1},{1,0},{2,3},{3,2},{4,5},{5,4},{6,7},{7,6},{8,9},{9,8},{10,11... | collective-permute-start | bytes 491528 | tf_op jit(solution)/shard_map/ppermute | solution.py:608
  47.2 7.0 %collective-permute-start.5 = (bf16[5,128,128]{2,1,0:T(8,128)(2,1)}, bf16[5,128,128]{2,1,0:T(8,128)(2,1)S(1)}, u32[]{:S(2)}, u32[]{:S(2)}) collective-permute-start(bf16[5,128,128]{2,1,0:T(8,128)(2,1)} %get-tuple-element.39), channel_id=1, source_target_pairs={{0,31},{1,2},{2,1},{3,4},{4,3},{5,6},{6,5},{7,8},{8,7},{9,10},{10,... | collective-permute-start | bytes 491528 | tf_op jit(solution)/shard_map/ppermute | solution.py:608
  54.3 1.3 %copy-done.5 = f32[5,4,128,128]{3,2,1,0:T(8,128)S(1)} copy-done((f32[5,4,128,128]{3,2,1,0:T(8,128)S(1)}, f32[5,4,128,128]{3,2,1,0:T(8,128)}, u32[]{:S(2)}) %copy-start.5) | copy-done | bytes 1310744
  55.6 1.8 %flow_inner.1.__.part = f32[5,4,128,128]{3,2,1,0:T(8,128)} custom-call(f32[5,4,128,128]{3,2,1,0:T(8,128)S(1)} %copy-done, f32[5,4,128,128]{3,2,1,0:T(8,128)S(1)} %copy-done.5), custom_call_target="tpu_custom_call" | custom-call | tf_op jit(solution)/shard_map/flow_inner/pallas_call | solution.py:41
  57.5 5.9 %sound_zero.1.part = f32[4,224,512]{2,1,0:T(8,128)} custom-call(bf16[4,224,512]{2,1,0:T(8,128)(2,1)} %q0.3, bf16[512,256]{1,0:T(8,128)(2,1)} %get-tuple-element.48.refs_1_.esrc, bf16[224,896]{1,0:T(8,128)(2,1)} %get-tuple-element.46._.refs_2_.gcat, bf16[256,512]{1,0:T(8,128)(2,1)} %get-tuple-element.49.refs_3_.edst, bf16[512,512]{1,0:T(8,128)(2,1)} %dx.3, ...), custom_call_target="tpu_custom_call" | custom-call | tf_op jit(solution)/shard_map/sound_zero/pallas_call | solution.py:41
  64.3 2.6 %sources.1 = (f32[4,224,512]{2,1,0:T(8,128)S(1)}, bf16[3,224,512]{2,1,0:T(8,128)(2,1)S(1)}, bf16[2,224,128]{2,1,0:T(8,128)(2,1)S(1)}, bf16[2,224,128]{2,1,0:T(8,128)(2,1)S(1)}, f32[8,128]{1,0:T(8,128)}) custom-call(bf16[128,48,128]{2,1,0:T(8,128)(2,1)S(1)} %all-to-all-done.1.got, f32[224,128]{1,0:T(8,128)} %get-tuple-element.47.spot, ...), custom_call_target="tpu_custom_call" | custom-call | tf_op jit(solution)/shard_map/sources/pallas_call | solution.py:41
  67.5 6.2 %collective-permute-start.11 = (bf16[2,224,128]{2,1,0:T(8,128)(2,1)S(1)}, bf16[2,224,128]{2,1,0:T(8,128)(2,1)S(1)}, u32[]{:S(2)}, u32[]{:S(2)}) collective-permute-start(bf16[2,224,128]{2,1,0:T(8,128)(2,1)S(1)} %get-tuple-element.56.r_3_), channel_id=1, source_target_pairs={{0,31},{1,2},{2,1},{3,4},{4,3},{5,6},{6,5},{7,8},{8,7},{9,10},{10,... | collective-permute-start | bytes 344072 | tf_op jit(solution)/shard_map/ppermute | solution.py:608
  73.8 2.7 %flow_two.1.after = f32[5,4,128,128]{3,2,1,0:T(8,128)} custom-call(f32[5,4,128,128]{3,2,1,0:T(8,128)S(1)} %copy-done.2, f32[5,128,128]{2,1,0:T(8,128)} %copy-done.4, f32[5,128,128]{2,1,0:T(8,128)} %copy-done.9, bf16[5,128,128]{2,1,0:T(8,128)(2,1)S(1)} %collective-permute-done.4.ce, bf16[5,128,128]{2,1,0:T(8,128)(2,1)S(1)} %collective-permute-done.5.co, ...), custom_call_target="tpu_custom_call" | custom-call | tf_op jit(solution)/shard_map/flow_two/pallas_call | solution.py:41
  76.6 2.6 %sound_one.1.r_6_.mid = f32[4,224,512]{2,1,0:T(8,128)S(1)} custom-call(bf16[4,224,512]{2,1,0:T(8,128)(2,1)S(1)} %copy-done.1, f32[4,224,512]{2,1,0:T(8,128)S(1)} %get-tuple-element.57.q1, bf16[3,224,512]{2,1,0:T(8,128)(2,1)S(1)} %get-tuple-element.58.src, bf16[512,512]{1,0:T(8,128)(2,1)S(1)} %copy-done.6, bf16[512,512]{1,0:T(8,128)(2,1)S(1)} %copy-done.7, ...), custom_call_target="tpu_custom_call" | custom-call | tf_op jit(solution)/shard_map/sound_one/pallas_call | solution.py:41
  79.8 5.5 %collective-permute-start.13 = (bf16[2,224,128]{2,1,0:T(8,128)(2,1)S(1)}, bf16[2,224,128]{2,1,0:T(8,128)(2,1)S(1)}, u32[]{:S(2)}, u32[]{:S(2)}) collective-permute-start(bf16[2,224,128]{2,1,0:T(8,128)(2,1)S(1)} %get-tuple-element.60.r_3_), channel_id=1, source_target_pairs={{0,31},{1,2},{2,1},{3,4},{4,3},{5,6},{6,5},{7,8},{8,7},{9,10},{10,... | collective-permute-start | bytes 344072 | tf_op jit(solution)/shard_map/ppermute | solution.py:608
  85.3 3.4 %sound_two.1 = (f32[4,224,512]{2,1,0:T(8,128)}, f32[2,4,224,128]{3,2,1,0:T(8,128)S(1)}) custom-call(bf16[4,224,512]{2,1,0:T(8,128)(2,1)S(1)} %copy-done.1, f32[4,224,512]{2,1,0:T(8,128)S(1)} %sound_one.1.r_6_.mid, f32[2,4,224,128]{3,2,1,0:T(8,128)S(1)} %get-tuple-element.61.ends, bf16[3,224,512]{2,1,0:T(8,128)(2,1)S(1)} %get-tuple-element.58.src, ...), custom_call_target="tpu_custom_call" | custom-call | tf_op jit(solution)/shard_map/sound_two/pallas_call | solution.py:41
  88.6 1.8 %collective-permute-done.13.r_5_ = bf16[2,224,128]{2,1,0:T(8,128)(2,1)S(1)} collective-permute-done((bf16[2,224,128]{2,1,0:T(8,128)(2,1)S(1)}, bf16[2,224,128]{2,1,0:T(8,128)(2,1)S(1)}, u32[]{:S(2)}, u32[]{:S(2)}) %collective-permute-start.13) | collective-permute-done | bytes 114720 | tf_op jit(solution)/shard_map/ppermute | solution.py:608
  90.4 1.4 %cross_two.1 = f32[4,224,512]{2,1,0:T(8,128)} custom-call(bf16[224,448]{1,0:T(8,128)(2,1)S(1)} %copy-done.12, bf16[224,448]{1,0:T(8,128)(2,1)S(1)} %copy-done.13, bf16[2,224,128]{2,1,0:T(8,128)(2,1)S(1)} %get-tuple-element.59.r_2_, bf16[2,224,128]{2,1,0:T(8,128)(2,1)S(1)} %get-tuple-element.60.r_3_, ...), custom_call_target="tpu_custom_call", output_to_operand_aliasing={{}: (7, {})} | custom-call | tf_op jit(solution)/shard_map/cross_two/pallas_call | solution.py:41
  (65 shorter events, 5.3 us)
Async XLA Ops:
  0.6 24.9 %copy-start = (f32[5,4,128,128]{3,2,1,0:T(8,128)S(1)}, f32[5,4,128,128]{3,2,1,0:T(8,128)}, u32[]{:S(2)}) copy-start(f32[5,4,128,128]{3,2,1,0:T(8,128)} %u.7) | copy-start | bytes 3932164
  3.8 31.8 %copy-start.16 = (bf16[2,224,128]{2,1,0:T(8,128)(2,1)}, bf16[2,224,128]{2,1,0:T(8,128)(2,1)S(1)}, u32[]{:S(2)}) copy-start(bf16[2,224,128]{2,1,0:T(8,128)(2,1)S(1)} %get-tuple-element.43.refs_9_) | copy-start | bytes 344068
  3.8 31.8 %copy-start.17 = (bf16[2,224,128]{2,1,0:T(8,128)(2,1)}, bf16[2,224,128]{2,1,0:T(8,128)(2,1)S(1)}, u32[]{:S(2)}) copy-start(bf16[2,224,128]{2,1,0:T(8,128)(2,1)S(1)} %get-tuple-element.44.refs_10_) | copy-start | bytes 344068
  3.8 21.7 %collective-permute-start = (f32[5,128,128]{2,1,0:T(8,128)S(1)}, f32[5,128,128]{2,1,0:T(8,128)S(1)}, u32[]{:S(2)}, u32[]{:S(2)}) collective-permute-start(f32[5,128,128]{2,1,0:T(8,128)S(1)} %get-tuple-element.33), channel_id=1, source_target_pairs={{0,1},{1,0},{2,3},{3,2},{4,5},{5,4},{6,7},{7,6},{8,9},{9,8},{10,11... | collective-permute-start | bytes 983048 | tf_op jit(solution)/shard_map/ppermute | solution.py:608
  5.5 20.1 %collective-permute-start.1 = (f32[5,128,128]{2,1,0:T(8,128)S(1)}, f32[5,128,128]{2,1,0:T(8,128)S(1)}, u32[]{:S(2)}, u32[]{:S(2)}) collective-permute-start(f32[5,128,128]{2,1,0:T(8,128)S(1)} %get-tuple-element.34), channel_id=1, source_target_pairs={{0,31},{1,2},{2,1},{3,4},{4,3},{5,6},{6,5},{7,8},{8,7},{9,10},{10,... | collective-permute-start | bytes 983048 | tf_op jit(solution)/shard_map/ppermute | solution.py:608
  13.3 1.3 %collective-permute-start.2 = (f32[128,128]{1,0:T(8,128)S(1)}, f32[128,128]{1,0:T(8,128)S(1)}, u32[]{:S(2)}, u32[]{:S(2)}) collective-permute-start(f32[128,128]{1,0:T(8,128)S(1)} %get-tuple-element.35), channel_id=1, source_target_pairs={{0,32},{32,0},{64,96},{96,64},{1,33},{33,1},{65,97},{97,65},{2,34}... | collective-permute-start | bytes 196616 | tf_op jit(solution)/shard_map/ppermute | solution.py:608
  13.3 13.3 %collective-permute-start.8 = (bf16[2,224,128]{2,1,0:T(8,128)(2,1)S(1)}, bf16[2,224,128]{2,1,0:T(8,128)(2,1)S(1)}, u32[]{:S(2)}, u32[]{:S(2)}) collective-permute-start(bf16[2,224,128]{2,1,0:T(8,128)(2,1)S(1)} %get-tuple-element.43.refs_9_), channel_id=1, source_target_pairs={{0,1},{1,0},{2,3},{3,2},{4,5},{5,4},{6,7},{7,6},{8,9},{9,8},{10,11... | collective-permute-start | bytes 344072 | tf_op jit(solution)/shard_map/ppermute | solution.py:608
  13.3 13.3 %collective-permute-start.9 = (bf16[2,224,128]{2,1,0:T(8,128)(2,1)S(1)}, bf16[2,224,128]{2,1,0:T(8,128)(2,1)S(1)}, u32[]{:S(2)}, u32[]{:S(2)}) collective-permute-start(bf16[2,224,128]{2,1,0:T(8,128)(2,1)S(1)} %get-tuple-element.44.refs_10_), channel_id=1, source_target_pairs={{0,31},{1,2},{2,1},{3,4},{4,3},{5,6},{6,5},{7,8},{8,7},{9,10},{10,... | collective-permute-start | bytes 344072 | tf_op jit(solution)/shard_map/ppermute | solution.py:608
  14.6 21.1 %copy-start.14 = (f32[128,128]{1,0:T(8,128)}, f32[128,128]{1,0:T(8,128)S(1)}, u32[]{:S(2)}) copy-start(f32[128,128]{1,0:T(8,128)S(1)} %collective-permute-done.2.ze) | copy-start | bytes 196612
  14.6 11.0 %collective-permute-start.3 = (f32[128,128]{1,0:T(8,128)S(1)}, f32[128,128]{1,0:T(8,128)S(1)}, u32[]{:S(2)}, u32[]{:S(2)}) collective-permute-start(f32[128,128]{1,0:T(8,128)S(1)} %get-tuple-element.36), channel_id=1, source_target_pairs={{0,96},{32,64},{64,32},{96,0},{1,97},{33,65},{65,33},{97,1},{2,98}... | collective-permute-start | bytes 196616 | tf_op jit(solution)/shard_map/ppermute | solution.py:608
  15.4 18.3 %all-to-all-start = ((f32[128,1,128]{2,1,0:T(1,128)}), f32[128,1,128]{2,1,0:T(1,128)S(1)}, u32[]{:S(2)}, u32[]{:S(2)}) async-start(f32[128,1,128]{2,1,0:T(1,128)} %bitcast.3), calls=%async_computation | async-start | bytes 131072 | tf_op jit(solution)/shard_map/all_to_all | solution.py:629
  25.6 10.1 %copy-start.15 = (f32[128,128]{1,0:T(8,128)}, f32[128,128]{1,0:T(8,128)S(1)}, u32[]{:S(2)}) copy-start(f32[128,128]{1,0:T(8,128)S(1)} %collective-permute-done.3.zo) | copy-start | bytes 196612
  25.6 10.1 %copy-start.9 = (f32[5,128,128]{2,1,0:T(8,128)}, f32[5,128,128]{2,1,0:T(8,128)S(1)}, u32[]{:S(2)}) copy-start(f32[5,128,128]{2,1,0:T(8,128)S(1)} %collective-permute-done.1.uo.xo) | copy-start | bytes 983044
  26.6 9.1 %copy-start.18 = (bf16[2,224,128]{2,1,0:T(8,128)(2,1)}, bf16[2,224,128]{2,1,0:T(8,128)(2,1)S(1)}, u32[]{:S(2)}) copy-start(bf16[2,224,128]{2,1,0:T(8,128)(2,1)S(1)} %collective-permute-done.8.refs_11_) | copy-start | bytes 344068
  35.7 28.6 %all-to-all-start.1 = ((bf16[128,48,128]{2,1,0:T(8,128)(2,1)}), bf16[128,48,128]{2,1,0:T(8,128)(2,1)S(1)}, u32[]{:S(2)}, u32[]{:S(2)}) async-start(bf16[128,48,128]{2,1,0:T(8,128)(2,1)} %send.1), calls=%async_computation.1 | async-start | bytes 3145728 | tf_op jit(solution)/shard_map/all_to_all | solution.py:664
  44.5 13.0 %collective-permute-start.6 = (f32[128,128]{1,0:T(8,128)}, f32[128,128]{1,0:T(8,128)S(1)}, u32[]{:S(2)}, u32[]{:S(2)}) collective-permute-start(f32[128,128]{1,0:T(8,128)} %get-tuple-element.40), channel_id=1, source_target_pairs={{0,32},{32,0},{64,96},{96,64},{1,33},{33,1},{65,97},{97,65},{2,34}... | collective-permute-start | bytes 196616 | tf_op jit(solution)/shard_map/ppermute | solution.py:608
  44.6 18.8 %collective-permute-start.7 = (f32[128,128]{1,0:T(8,128)}, f32[128,128]{1,0:T(8,128)S(1)}, u32[]{:S(2)}, u32[]{:S(2)}) collective-permute-start(f32[128,128]{1,0:T(8,128)} %get-tuple-element.41), channel_id=1, source_target_pairs={{0,96},{32,64},{64,32},{96,0},{1,97},{33,65},{65,33},{97,1},{2,98}... | collective-permute-start | bytes 196616 | tf_op jit(solution)/shard_map/ppermute | solution.py:608
  45.7 28.0 %collective-permute-start.4 = (bf16[5,128,128]{2,1,0:T(8,128)(2,1)}, bf16[5,128,128]{2,1,0:T(8,128)(2,1)S(1)}, u32[]{:S(2)}, u32[]{:S(2)}) collective-permute-start(bf16[5,128,128]{2,1,0:T(8,128)(2,1)} %get-tuple-element.38), channel_id=1, source_target_pairs={{0,1},{1,0},{2,3},{3,2},{4,5},{5,4},{6,7},{7,6},{8,9},{9,8},{10,11... | collective-permute-start | bytes 491528 | tf_op jit(solution)/shard_map/ppermute | solution.py:608
  47.2 26.5 %collective-permute-start.5 = (bf16[5,128,128]{2,1,0:T(8,128)(2,1)}, bf16[5,128,128]{2,1,0:T(8,128)(2,1)S(1)}, u32[]{:S(2)}, u32[]{:S(2)}) collective-permute-start(bf16[5,128,128]{2,1,0:T(8,128)(2,1)} %get-tuple-element.39), channel_id=1, source_target_pairs={{0,31},{1,2},{2,1},{3,4},{4,3},{5,6},{6,5},{7,8},{8,7},{9,10},{10,... | collective-permute-start | bytes 491528 | tf_op jit(solution)/shard_map/ppermute | solution.py:608
  64.3 9.4 %copy-start.2 = (f32[5,4,128,128]{3,2,1,0:T(8,128)S(1)}, f32[5,4,128,128]{3,2,1,0:T(8,128)}, u32[]{:S(2)}) copy-start(f32[5,4,128,128]{3,2,1,0:T(8,128)} %flow_inner.1.__.part) | copy-start | bytes 3932164
  66.9 12.3 %collective-permute-start.10 = (bf16[2,224,128]{2,1,0:T(8,128)(2,1)S(1)}, bf16[2,224,128]{2,1,0:T(8,128)(2,1)S(1)}, u32[]{:S(2)}, u32[]{:S(2)}) collective-permute-start(bf16[2,224,128]{2,1,0:T(8,128)(2,1)S(1)} %get-tuple-element.55.r_2_), channel_id=1, source_target_pairs={{0,1},{1,0},{2,3},{3,2},{4,5},{5,4},{6,7},{7,6},{8,9},{9,8},{10,11... | collective-permute-start | bytes 344072 | tf_op jit(solution)/shard_map/ppermute | solution.py:608
  67.5 11.6 %collective-permute-start.11 = (bf16[2,224,128]{2,1,0:T(8,128)(2,1)S(1)}, bf16[2,224,128]{2,1,0:T(8,128)(2,1)S(1)}, u32[]{:S(2)}, u32[]{:S(2)}) collective-permute-start(bf16[2,224,128]{2,1,0:T(8,128)(2,1)S(1)} %get-tuple-element.56.r_3_), channel_id=1, source_target_pairs={{0,31},{1,2},{2,1},{3,4},{4,3},{5,6},{6,5},{7,8},{8,7},{9,10},{10,... | collective-permute-start | bytes 344072 | tf_op jit(solution)/shard_map/ppermute | solution.py:608
  79.7 9.0 %collective-permute-start.12 = (bf16[2,224,128]{2,1,0:T(8,128)(2,1)S(1)}, bf16[2,224,128]{2,1,0:T(8,128)(2,1)S(1)}, u32[]{:S(2)}, u32[]{:S(2)}) collective-permute-start(bf16[2,224,128]{2,1,0:T(8,128)(2,1)S(1)} %get-tuple-element.59.r_2_), channel_id=1, source_target_pairs={{0,1},{1,0},{2,3},{3,2},{4,5},{5,4},{6,7},{7,6},{8,9},{9,8},{10,11... | collective-permute-start | bytes 344072 | tf_op jit(solution)/shard_map/ppermute | solution.py:608
  79.8 10.7 %collective-permute-start.13 = (bf16[2,224,128]{2,1,0:T(8,128)(2,1)S(1)}, bf16[2,224,128]{2,1,0:T(8,128)(2,1)S(1)}, u32[]{:S(2)}, u32[]{:S(2)}) collective-permute-start(bf16[2,224,128]{2,1,0:T(8,128)(2,1)S(1)} %get-tuple-element.60.r_3_), channel_id=1, source_target_pairs={{0,31},{1,2},{2,1},{3,4},{4,3},{5,6},{6,5},{7,8},{8,7},{9,10},{10,... | collective-permute-start | bytes 344072 | tf_op jit(solution)/shard_map/ppermute | solution.py:608
  (14 other events, 39.7 us)

commit v6 on v5

--- a/solution.py
+++ b/solution.py
@@ -73,8 +73,7 @@
 
 
 def primitives(rows):
-    inv = 1.0 / rows[0]
-    v1, v2, v3 = rows[1] * inv, rows[2] * inv, rows[3] * inv
+    v1, v2, v3 = rows[1] / rows[0], rows[2] / rows[0], rows[3] / rows[0]
     p = 0.4 * (rows[4] - 0.5 * (rows[1] * v1 + rows[2] * v2 + rows[3] * v3))
     return (v1, v2, v3), p
 
@@ -180,14 +179,12 @@
 def lamb_body(u, xe, xo, ze, zo, table, vel, pooled):
     lane = iota((128, 128), 1)
     for x in range(4):
-        inv = 1.0 / u[0, x]
         for c in range(3):
-            vel[c, x + 1] = u[1 + c, x] * inv
+            vel[c, x + 1] = u[1 + c, x] / u[0, x]
     even = is_even("space")
     by_link = []
     for link in (xe, xo):
-        inv = 1.0 / link[0]
-        by_link.append([link[1 + c] * inv for c in (1, 2)])
+        by_link.append([link[1 + c] / link[0] for c in (1, 2)])
     for c in (1, 2):
         by_even, by_odd = by_link[0][c - 1], by_link[1][c - 1]
         vel[c, 0] = jnp.where(even, by_odd, by_even)
@@ -199,9 +196,9 @@
         total = None
         for x in (2 * pair, 2 * pair + 1):
             v1, v2, v3 = vel[0, x + 1], vel[1, x + 1], vel[2, x + 1]
-            w1 = diff_y(v3) - diff_z(v2, lane, below, above, 24 + x)
-            w2 = diff_z(v1, lane, below, above, 20 + x) - (vel[2, x + 2] - vel[2, x])
-            w3 = (vel[1, x + 2] - vel[1, x]) - diff_y(v1)
+            w1 = 0.5 * diff_y(v3) - 0.5 * diff_z(v2, lane, below, above, 24 + x)
+            w2 = 0.5 * diff_z(v1, lane, below, above, 20 + x) - 0.5 * (vel[2, x + 2] - vel[2, x])
+            w3 = 0.5 * (vel[1, x + 2] - vel[1, x]) - 0.5 * diff_y(v1)
             lamb = [w2 * v3 - w3 * v2, w3 * v1 - w1 * v3, w1 * v2 - w2 * v1]
             total = lamb if total is None else [a + b for a, b in zip(total, lamb)]
         for c in range(3):
@@ -213,7 +210,7 @@
         odd.append(t[pl.ds(2, 32, stride=4), :] + t[pl.ds(3, 32, stride=4), :])
     rows = jnp.concatenate([jnp.concatenate(even, 0), jnp.concatenate(odd, 0)], 1)
     z, n = iota((256, 128), 0), iota((256, 128), 1)
-    pool = jnp.where((z // 128) * 64 + (z % 128) // 2 == n, 0.0625, 0.0).astype(F32)
+    pool = jnp.where((z // 128) * 64 + (z % 128) // 2 == n, 0.125, 0.0).astype(F32)
     coarse = jnp.dot(rows, pool, preferred_element_type=F32, precision=lax.Precision.HIGHEST)
     flat = pooled.at[0]
     hold = pooled.at[1]
@@ -236,8 +233,8 @@
     fc = flux(rows, v, p, 2)
     out = []
     for f in range(5):
-        total = along_a(x, f) + diff_y(fb[f])
-        out.append(total + diff_z(fc[f], lane, below, above, f * 4 + x))
+        total = 0.5 * along_a(x, f) + 0.5 * diff_y(fb[f])
+        out.append(total + 0.5 * diff_z(fc[f], lane, below, above, f * 4 + x))
     return rows, out
 
 
@@ -276,13 +273,13 @@
             above,
             lane,
         )
-        now = [rows[f] - (FLOW_STEP * 0.5) * out[f] for f in range(5)]
+        now = [rows[f] - FLOW_STEP * out[f] for f in range(5)]
         for f in range(5):
             hold[x, f] = now[f]
         copies += begin(sems, i, (hold.at[x], first.at[:, x]))
         if x in (0, 3):
             for f in range(5):
-                edge[i, f] = ((-FLOW_STEP * 0.5) * out[f]).astype(BF16)
+                edge[i, f] = (-FLOW_STEP * out[f]).astype(BF16)
         v, p = primitives(now)
         lo, hi = add_columns(x, flux(now, v, p, 2), lane, lo, hi)
     zpack[0] = lo
@@ -302,14 +299,16 @@
         fb = flux(rows, v, p, 1)
         fc = flux(rows, v, p, 2)
         for f in range(5):
-            total = diff_y(fb[f])
-            total = total + jnp.where(lane == 127, 0.0, roll_z(fc[f], -1))
-            total = total - jnp.where(lane == 0, 0.0, roll_z(fc[f], 1))
-            if x < 3:
-                total = total + fa[f, x + 2]
-            if x > 0:
-                total = total - fa[f, x]
-            hold[x, f] = 0.5 * ((rows[f] - u[f, x]) - (FLOW_STEP * 0.5) * total)
+            along_c = jnp.where(lane == 127, 0.0, roll_z(fc[f], -1))
+            along_c = along_c - jnp.where(lane == 0, 0.0, roll_z(fc[f], 1))
+            if x == 0:
+                along_a = fa[f, x + 2]
+            elif x == 3:
+                along_a = -fa[f, x]
+            else:
+                along_a = fa[f, x + 2] - fa[f, x]
+            total = 0.5 * along_a + 0.5 * diff_y(fb[f]) + 0.5 * along_c
+            hold[x, f] = 0.5 * ((rows[f] - u[f, x]) - FLOW_STEP * total)
         copies += begin(sems, x, (hold.at[x], part.at[:, x]))
     finish(copies)
 
@@ -523,14 +522,14 @@
     finish(copies)
 
 
-def sources_body(got, spot, part, _, __, q1, src, lo, hi, token, spot_v, pick_v, part_v, token_v, sems):
+def sources_body(got, spot, part, _, __, src, even, odd, token, spot_v, pick_v, ends, token_v, sems):
     token_v[...] = jnp.zeros_like(token_v)
     copies = begin(
         sems,
         0,
         (spot, spot_v),
-        (part.at[0], q1.at[0]),
-        *[(part.at[v], part_v.at[v - 1]) for v in (1, 2, 3)],
+        (part.at[:, :, 0:128], ends.at[0]),
+        (part.at[:, :, 384:512], ends.at[1]),
         (token_v, token),
     )
     lane = iota((EL, 128), 1).astype(F32)
@@ -539,25 +538,26 @@
         number = spot_v[...] + 4.0 * parity
         for t in range(0, 1024, 128):
             pick_v[parity, :, t : t + 128] = jnp.where(lane + t == number, 1.0, 0.0).astype(BF16)
+    tiles = []
     for c in range(3):
         s = gather_source(got.at[:, 16 * c : 16 * c + 16, :], pick_v)
         src[c] = s.astype(BF16)
-        copies[2 + c].wait()
-        q1[1 + c] = part_v[c] + SOUND_STEP * s
-    copies[1].wait()
-    copies[5].wait()
+        tiles.append((SOUND_STEP * s[:, 0:128], SOUND_STEP * s[:, 384:512]))
+    finish(copies[1:])
     store_traces(
-        [q1[v, :, 0:128] for v in range(4)],
-        [q1[v, :, 384:512] for v in range(4)],
-        lo,
-        hi,
-    )
-
-
-def sound_one_body(q0, q1, src, dx, dy, dz, gcat, esrc, edst, after, part):
-    terms = local_terms([q1[v].astype(BF16) for v in range(4)], dx, dy, dz, gcat, esrc, edst)
+        [ends[0, 0]] + [ends[0, 1 + c] + tiles[c][0] for c in range(3)],
+        [ends[1, 0]] + [ends[1, 1 + c] + tiles[c][1] for c in range(3)],
+        even,
+        odd,
+    )
+
+
+def sound_one_body(q0, start, src, dx, dy, dz, gcat, esrc, edst, _, part):
+    given = [src[c].astype(F32) for c in range(3)]
+    q1 = [start[0]] + [start[1 + c] + SOUND_STEP * given[c] for c in range(3)]
+    terms = local_terms([t.astype(BF16) for t in q1], dx, dy, dz, gcat, esrc, edst)
     for v in range(4):
-        t = terms[v] if v == 0 else terms[v] + src[v - 1].astype(F32)
+        t = terms[v] if v == 0 else terms[v] + given[v - 1]
         part[v] = 0.75 * q0[v].astype(F32) + 0.25 * (q1[v] + SOUND_STEP * t)
 
 
@@ -702,14 +702,14 @@
         scratch=[keep(5, 6, 128, 128), keep(4, 5, 128, 128), dma(4)],
         far_out=(0,),
     )
-    q1, src, qe, qo, token = call(
+    src, qe, qo, token = call(
         sources_body,
-        [state, half(3, EL, NODES)] + traces + [full(8, 128)],
+        [half(3, EL, NODES)] + traces + [full(8, 128)],
         "sources",
         (got, spot, part, yo, inner),
-        scratch=[keep(EL, 128), keep_half(2, EL, 1024), keep(3, EL, NODES), keep(8, 128), dma(6)],
+        scratch=[keep(EL, 128), keep_half(2, EL, 1024), keep(2, 4, EL, 128), keep(8, 128), dma(4)],
         far=(1, 2, 4),
-        far_out=(4,),
+        far_out=(3,),
     )
     mats = (dx, dy, dz, gcat, esrc, edst)
     got_qe, got_qo = swap(qe, qo, "space")
@@ -726,7 +726,7 @@
         sound_one_body,
         state,
         "sound_one",
-        (acoustic_state, q1, src) + mats + (flow_increment,),
+        (acoustic_state, part, src) + mats + (flow_increment,),
         far=(9,),
     )
     ends, qe, qo = call(

time: 92.3 us -> 91.8 us (level)
  no operation moved by 1% of the time
where the time goes in v6:
time: 91.8 us; the launch traced here: 91.5 us
  starting transfers between devices  47.6 us (52%)
  Pallas kernels  33.5 us (36%)
  waiting for transfers between devices  7.81 us (9%)
  local copies, waits for them, and re-layouts  1.41 us (2%)
  between operations  1.26 us (1%)
    ppermute x14, starting transfers between devices, swap(): return (lax.ppermute(even, axis, by_even), lax.ppermute(odd, axis, by_odd))  33.8 us
    pallas_call x13, Pallas kernels, call(): pl.pallas_call(body, out_shape=outs if many else outs[0], in_specs=[space...  33.5 us
    all_to_all x1, starting transfers between devices, local(): lax.all_to_all(wanted.reshape(128, 1, 128), both, split_axis=0, concat_ax...  9.11 us
    all_to_all x1, starting transfers between devices, local(): got = lax.all_to_all(send, both, split_axis=0, concat_axis=0, tiled=True)  4.66 us
    all_to_all x1, waiting for transfers between devices, local(): lax.all_to_all(wanted.reshape(128, 1, 128), both, split_axis=0, concat_ax...  4.09 us
    ppermute x14, waiting for transfers between devices, swap(): return (lax.ppermute(even, axis, by_even), lax.ppermute(odd, axis, by_odd))  2.88 us
  transfers between devices with their start and end apart: 16, of which 4 were waited for; matrix products, arithmetic and copies ran while one was open for 0% of the time, Pallas kernels for 29%

profile of v6, /device:TPU:0, one launch (start us, length us, event | category | flops | bytes accessed | tf_op | source)
XLA Modules:
  0.0 91.5 jit_solution(14338568322447389003)
XLA Ops:
  0.6 3.1 %edges.1 = (f32[5,128,128]{2,1,0:T(8,128)S(1)}, f32[5,128,128]{2,1,0:T(8,128)S(1)}, f32[128,128]{1,0:T(8,128)S(1)}, f32[128,128]{1,0:T(8,128)S(1)}, bf16[2,224,1...) custom-call(f32[5,4,128,128]{3,2,1,0:T(8,128)} %u.7, bf16[4,224,512]{2,1,0:T(8,128)(2,1)} %q0.3, ...), custom_call_target="tpu_custom_call" | custom-call | tf_op jit(solution)/shard_map/edges/pallas_call | solution.py:41
  3.8 1.7 %collective-permute-start = (f32[5,128,128]{2,1,0:T(8,128)S(1)}, f32[5,128,128]{2,1,0:T(8,128)S(1)}, u32[]{:S(2)}, u32[]{:S(2)}) collective-permute-start(f32[5,128,128]{2,1,0:T(8,128)S(1)} %get-tuple-element.32), channel_id=1, source_target_pairs={{0,1},{1,0},{2,3},{3,2},{4,5},{5,4},{6,7},{7,6},{8,9},{9,8},{10,11... | collective-permute-start | bytes 983048 | tf_op jit(solution)/shard_map/ppermute | solution.py:608
  5.5 7.9 %collective-permute-start.1 = (f32[5,128,128]{2,1,0:T(8,128)S(1)}, f32[5,128,128]{2,1,0:T(8,128)S(1)}, u32[]{:S(2)}, u32[]{:S(2)}) collective-permute-start(f32[5,128,128]{2,1,0:T(8,128)S(1)} %get-tuple-element.33), channel_id=1, source_target_pairs={{0,31},{1,2},{2,1},{3,4},{4,3},{5,6},{6,5},{7,8},{8,7},{9,10},{10,... | collective-permute-start | bytes 983048 | tf_op jit(solution)/shard_map/ppermute | solution.py:608
  13.3 1.2 %collective-permute-start.9 = (bf16[2,224,128]{2,1,0:T(8,128)(2,1)S(1)}, bf16[2,224,128]{2,1,0:T(8,128)(2,1)S(1)}, u32[]{:S(2)}, u32[]{:S(2)}) collective-permute-start(bf16[2,224,128]{2,1,0:T(8,128)(2,1)S(1)} %get-tuple-element.43.refs_10_), channel_id=1, source_target_pairs={{0,31},{1,2},{2,1},{3,4},{4,3},{5,6},{6,5},{7,8},{8,7},{9,10},{10,... | collective-permute-start | bytes 344072 | tf_op jit(solution)/shard_map/ppermute | solution.py:608
  15.4 9.1 %all-to-all-start = ((f32[128,1,128]{2,1,0:T(1,128)}), f32[128,1,128]{2,1,0:T(1,128)S(1)}, u32[]{:S(2)}, u32[]{:S(2)}) async-start(f32[128,1,128]{2,1,0:T(1,128)} %bitcast.3), calls=%async_computation | async-start | bytes 131072 | tf_op jit(solution)/shard_map/all_to_all | solution.py:629
  26.7 2.9 %prepare.1 = (bf16[224,896]{1,0:T(8,128)(2,1)}, bf16[224,448]{1,0:T(8,128)(2,1)}, bf16[224,448]{1,0:T(8,128)(2,1)}, bf16[512,256]{1,0:T(8,128)(2,1)}, bf16[256,512]{1,0:T(8,128)(2,1)}, /*index=5*/f32[224,128]{1,0:T(8,128)}) custom-call(s32[6,224]{1,0:T(8,128)} %nb_far.1, s32[1,224]{1,0:T(1,128)} %bitcast.10, f32[5,128,128]{2,1,0:T(8,128)} %copy-done.5), custom_call_target="tpu_custom_call" | custom-call | tf_op jit(solution)/shard_map/prepare/pallas_call | solution.py:41
  29.6 4.1 %all-to-all-done = f32[128,1,128]{2,1,0:T(1,128)S(1)} async-done(((f32[128,1,128]{2,1,0:T(1,128)}), f32[128,1,128]{2,1,0:T(1,128)S(1)}, u32[]{:S(2)}, u32[]{:S(2)}) %all-to-all-start) | async-done | bytes 65568 | tf_op jit(solution)/shard_map/all_to_all | solution.py:629
  33.7 1.9 %send.1 = bf16[128,48,128]{2,1,0:T(8,128)(2,1)} custom-call(f32[128,128]{1,0:T(8,128)S(1)} %bitcast.8, bf16[128,768]{1,0:T(8,128)(2,1)S(1)} %lamb.1.table, bf16[224,896]{1,0:T(8,128)(2,1)} %get-tuple-element.45._.refs_2_.gcat), custom_call_target="tpu_custom_call" | custom-call | tf_op jit(solution)/shard_map/send/pallas_call | solution.py:41
  35.7 4.7 %all-to-all-start.1 = ((bf16[128,48,128]{2,1,0:T(8,128)(2,1)}), bf16[128,48,128]{2,1,0:T(8,128)(2,1)S(1)}, u32[]{:S(2)}, u32[]{:S(2)}) async-start(bf16[128,48,128]{2,1,0:T(8,128)(2,1)} %send.1), calls=%async_computation.1 | async-start | bytes 3145728 | tf_op jit(solution)/shard_map/all_to_all | solution.py:664
  40.3 4.0 %flow_one.1 = (f32[5,4,128,128]{3,2,1,0:T(8,128)}, bf16[5,128,128]{2,1,0:T(8,128)(2,1)}, bf16[5,128,128]{2,1,0:T(8,128)(2,1)}, f32[128,128]{1,0:T(8,128)}, f32[128,128]{1,0:T(8,128)}) custom-call(f32[5,4,128,128]{3,2,1,0:T(8,128)S(1)} %copy-done, f32[5,128,128]{2,1,0:T(8,128)} %copy-done.5, f32[5,128,128]{2,1,0:T(8,128)} %copy-done.10, ...), custom_call_target="tpu_custom_call" | custom-call | tf_op jit(solution)/shard_map/flow_one/pallas_call | solution.py:41
  44.5 1.2 %collective-permute-start.7 = (f32[128,128]{1,0:T(8,128)}, f32[128,128]{1,0:T(8,128)S(1)}, u32[]{:S(2)}, u32[]{:S(2)}) collective-permute-start(f32[128,128]{1,0:T(8,128)} %get-tuple-element.40), channel_id=1, source_target_pairs={{0,96},{32,64},{64,32},{96,0},{1,97},{33,65},{65,33},{97,1},{2,98}... | collective-permute-start | bytes 196616 | tf_op jit(solution)/shard_map/ppermute | solution.py:608
  45.6 1.5 %collective-permute-start.4 = (bf16[5,128,128]{2,1,0:T(8,128)(2,1)}, bf16[5,128,128]{2,1,0:T(8,128)(2,1)S(1)}, u32[]{:S(2)}, u32[]{:S(2)}) collective-permute-start(bf16[5,128,128]{2,1,0:T(8,128)(2,1)} %get-tuple-element.37), channel_id=1, source_target_pairs={{0,1},{1,0},{2,3},{3,2},{4,5},{5,4},{6,7},{7,6},{8,9},{9,8},{10,11... | collective-permute-start | bytes 491528 | tf_op jit(solution)/shard_map/ppermute | solution.py:608
  47.1 7.0 %collective-permute-start.5 = (bf16[5,128,128]{2,1,0:T(8,128)(2,1)}, bf16[5,128,128]{2,1,0:T(8,128)(2,1)S(1)}, u32[]{:S(2)}, u32[]{:S(2)}) collective-permute-start(bf16[5,128,128]{2,1,0:T(8,128)(2,1)} %get-tuple-element.38), channel_id=1, source_target_pairs={{0,31},{1,2},{2,1},{3,4},{4,3},{5,6},{6,5},{7,8},{8,7},{9,10},{10,... | collective-permute-start | bytes 491528 | tf_op jit(solution)/shard_map/ppermute | solution.py:608
  54.2 1.3 %copy-done.6 = f32[5,4,128,128]{3,2,1,0:T(8,128)S(1)} copy-done((f32[5,4,128,128]{3,2,1,0:T(8,128)S(1)}, f32[5,4,128,128]{3,2,1,0:T(8,128)}, u32[]{:S(2)}) %copy-start.6) | copy-done | bytes 1310744
  55.5 2.0 %flow_inner.1.__.part = f32[5,4,128,128]{3,2,1,0:T(8,128)} custom-call(f32[5,4,128,128]{3,2,1,0:T(8,128)S(1)} %copy-done, f32[5,4,128,128]{3,2,1,0:T(8,128)S(1)} %copy-done.6), custom_call_target="tpu_custom_call" | custom-call | tf_op jit(solution)/shard_map/flow_inner/pallas_call | solution.py:41
  57.5 5.9 %sound_zero.1.part.start = f32[4,224,512]{2,1,0:T(8,128)} custom-call(bf16[4,224,512]{2,1,0:T(8,128)(2,1)} %q0.3, bf16[512,256]{1,0:T(8,128)(2,1)} %get-tuple-element.47.refs_1_.esrc, bf16[224,896]{1,0:T(8,128)(2,1)} %get-tuple-element.45._.refs_2_.gcat, bf16[256,512]{1,0:T(8,128)(2,1)} %get-tuple-element.48.refs_3_.edst, bf16[512,512]{1,0:T(8,128)(2,1)} %dx.3, ...), custom_call_target="tpu_custom_call" | custom-call | tf_op jit(solution)/shard_map/sound_zero/pallas_call | solution.py:41
  64.3 2.1 %sources.1 = (bf16[3,224,512]{2,1,0:T(8,128)(2,1)S(1)}, bf16[2,224,128]{2,1,0:T(8,128)(2,1)S(1)}, bf16[2,224,128]{2,1,0:T(8,128)(2,1)S(1)}, f32[8,128]{1,0:T(8,128)}) custom-call(bf16[128,48,128]{2,1,0:T(8,128)(2,1)S(1)} %all-to-all-done.1.got, f32[224,128]{1,0:T(8,128)} %get-tuple-element.46.spot, f32[4,224,512]{2,1,0:T(8,128)} %sound_zero.1.part.start, ...), custom_call_target="tpu_custom_call" | custom-call | tf_op jit(solution)/shard_map/sources/pallas_call | solution.py:41
  67.1 6.2 %collective-permute-start.11 = (bf16[2,224,128]{2,1,0:T(8,128)(2,1)S(1)}, bf16[2,224,128]{2,1,0:T(8,128)(2,1)S(1)}, u32[]{:S(2)}, u32[]{:S(2)}) collective-permute-start(bf16[2,224,128]{2,1,0:T(8,128)(2,1)S(1)} %get-tuple-element.55.r_3_), channel_id=1, source_target_pairs={{0,31},{1,2},{2,1},{3,4},{4,3},{5,6},{6,5},{7,8},{8,7},{9,10},{10,... | collective-permute-start | bytes 344072 | tf_op jit(solution)/shard_map/ppermute | solution.py:608
  73.3 2.7 %flow_two.1._ = f32[5,4,128,128]{3,2,1,0:T(8,128)} custom-call(f32[5,4,128,128]{3,2,1,0:T(8,128)S(1)} %copy-done.3, f32[5,128,128]{2,1,0:T(8,128)} %copy-done.5, f32[5,128,128]{2,1,0:T(8,128)} %copy-done.10, bf16[5,128,128]{2,1,0:T(8,128)(2,1)S(1)} %collective-permute-done.4.ce, bf16[5,128,128]{2,1,0:T(8,128)(2,1)S(1)} %collective-permute-done.5.co, ...), custom_call_target="tpu_custom_call" | custom-call | tf_op jit(solution)/shard_map/flow_two/pallas_call | solution.py:41
  76.1 2.5 %sound_one.1.r_6_.mid = f32[4,224,512]{2,1,0:T(8,128)S(1)} custom-call(bf16[4,224,512]{2,1,0:T(8,128)(2,1)S(1)} %copy-done.2, f32[4,224,512]{2,1,0:T(8,128)S(1)} %copy-done.1, bf16[3,224,512]{2,1,0:T(8,128)(2,1)S(1)} %get-tuple-element.56.src, bf16[512,512]{1,0:T(8,128)(2,1)S(1)} %copy-done.7, bf16[512,512]{1,0:T(8,128)(2,1)S(1)} %copy-done.8, ...), custom_call_target="tpu_custom_call" | custom-call | tf_op jit(solution)/shard_map/sound_one/pallas_call | solution.py:41
  79.3 5.6 %collective-permute-start.13 = (bf16[2,224,128]{2,1,0:T(8,128)(2,1)S(1)}, bf16[2,224,128]{2,1,0:T(8,128)(2,1)S(1)}, u32[]{:S(2)}, u32[]{:S(2)}) collective-permute-start(bf16[2,224,128]{2,1,0:T(8,128)(2,1)S(1)} %get-tuple-element.58.r_3_), channel_id=1, source_target_pairs={{0,31},{1,2},{2,1},{3,4},{4,3},{5,6},{6,5},{7,8},{8,7},{9,10},{10,... | collective-permute-start | bytes 344072 | tf_op jit(solution)/shard_map/ppermute | solution.py:608
  84.8 3.4 %sound_two.1 = (f32[4,224,512]{2,1,0:T(8,128)}, f32[2,4,224,128]{3,2,1,0:T(8,128)S(1)}) custom-call(bf16[4,224,512]{2,1,0:T(8,128)(2,1)S(1)} %copy-done.2, f32[4,224,512]{2,1,0:T(8,128)S(1)} %sound_one.1.r_6_.mid, f32[2,4,224,128]{3,2,1,0:T(8,128)S(1)} %get-tuple-element.59.ends, bf16[3,224,512]{2,1,0:T(8,128)(2,1)S(1)} %get-tuple-element.56.src, ...), custom_call_target="tpu_custom_call" | custom-call | tf_op jit(solution)/shard_map/sound_two/pallas_call | solution.py:41
  88.2 1.7 %collective-permute-done.13.r_5_ = bf16[2,224,128]{2,1,0:T(8,128)(2,1)S(1)} collective-permute-done((bf16[2,224,128]{2,1,0:T(8,128)(2,1)S(1)}, bf16[2,224,128]{2,1,0:T(8,128)(2,1)S(1)}, u32[]{:S(2)}, u32[]{:S(2)}) %collective-permute-start.13) | collective-permute-done | bytes 114720 | tf_op jit(solution)/shard_map/ppermute | solution.py:608
  90.0 1.4 %cross_two.1 = f32[4,224,512]{2,1,0:T(8,128)} custom-call(bf16[224,448]{1,0:T(8,128)(2,1)S(1)} %copy-done.13, bf16[224,448]{1,0:T(8,128)(2,1)S(1)} %copy-done.14, bf16[2,224,128]{2,1,0:T(8,128)(2,1)S(1)} %get-tuple-element.57.r_2_, bf16[2,224,128]{2,1,0:T(8,128)(2,1)S(1)} %get-tuple-element.58.r_3_, ...), custom_call_target="tpu_custom_call", output_to_operand_aliasing={{}: (7, {})} | custom-call | tf_op jit(solution)/shard_map/cross_two/pallas_call | solution.py:41
  (67 shorter events, 5.2 us)
Async XLA Ops:
  0.6 24.9 %copy-start = (f32[5,4,128,128]{3,2,1,0:T(8,128)S(1)}, f32[5,4,128,128]{3,2,1,0:T(8,128)}, u32[]{:S(2)}) copy-start(f32[5,4,128,128]{3,2,1,0:T(8,128)} %u.7) | copy-start | bytes 3932164
  3.8 31.8 %copy-start.17 = (bf16[2,224,128]{2,1,0:T(8,128)(2,1)}, bf16[2,224,128]{2,1,0:T(8,128)(2,1)S(1)}, u32[]{:S(2)}) copy-start(bf16[2,224,128]{2,1,0:T(8,128)(2,1)S(1)} %get-tuple-element.42.refs_9_) | copy-start | bytes 344068
  3.8 31.8 %copy-start.18 = (bf16[2,224,128]{2,1,0:T(8,128)(2,1)}, bf16[2,224,128]{2,1,0:T(8,128)(2,1)S(1)}, u32[]{:S(2)}) copy-start(bf16[2,224,128]{2,1,0:T(8,128)(2,1)S(1)} %get-tuple-element.43.refs_10_) | copy-start | bytes 344068
  3.8 21.7 %collective-permute-start = (f32[5,128,128]{2,1,0:T(8,128)S(1)}, f32[5,128,128]{2,1,0:T(8,128)S(1)}, u32[]{:S(2)}, u32[]{:S(2)}) collective-permute-start(f32[5,128,128]{2,1,0:T(8,128)S(1)} %get-tuple-element.32), channel_id=1, source_target_pairs={{0,1},{1,0},{2,3},{3,2},{4,5},{5,4},{6,7},{7,6},{8,9},{9,8},{10,11... | collective-permute-start | bytes 983048 | tf_op jit(solution)/shard_map/ppermute | solution.py:608
  5.5 20.1 %collective-permute-start.1 = (f32[5,128,128]{2,1,0:T(8,128)S(1)}, f32[5,128,128]{2,1,0:T(8,128)S(1)}, u32[]{:S(2)}, u32[]{:S(2)}) collective-permute-start(f32[5,128,128]{2,1,0:T(8,128)S(1)} %get-tuple-element.33), channel_id=1, source_target_pairs={{0,31},{1,2},{2,1},{3,4},{4,3},{5,6},{6,5},{7,8},{8,7},{9,10},{10,... | collective-permute-start | bytes 983048 | tf_op jit(solution)/shard_map/ppermute | solution.py:608
  13.3 1.3 %collective-permute-start.2 = (f32[128,128]{1,0:T(8,128)S(1)}, f32[128,128]{1,0:T(8,128)S(1)}, u32[]{:S(2)}, u32[]{:S(2)}) collective-permute-start(f32[128,128]{1,0:T(8,128)S(1)} %get-tuple-element.34), channel_id=1, source_target_pairs={{0,32},{32,0},{64,96},{96,64},{1,33},{33,1},{65,97},{97,65},{2,34}... | collective-permute-start | bytes 196616 | tf_op jit(solution)/shard_map/ppermute | solution.py:608
  13.3 13.3 %collective-permute-start.8 = (bf16[2,224,128]{2,1,0:T(8,128)(2,1)S(1)}, bf16[2,224,128]{2,1,0:T(8,128)(2,1)S(1)}, u32[]{:S(2)}, u32[]{:S(2)}) collective-permute-start(bf16[2,224,128]{2,1,0:T(8,128)(2,1)S(1)} %get-tuple-element.42.refs_9_), channel_id=1, source_target_pairs={{0,1},{1,0},{2,3},{3,2},{4,5},{5,4},{6,7},{7,6},{8,9},{9,8},{10,11... | collective-permute-start | bytes 344072 | tf_op jit(solution)/shard_map/ppermute | solution.py:608
  13.3 13.3 %collective-permute-start.9 = (bf16[2,224,128]{2,1,0:T(8,128)(2,1)S(1)}, bf16[2,224,128]{2,1,0:T(8,128)(2,1)S(1)}, u32[]{:S(2)}, u32[]{:S(2)}) collective-permute-start(bf16[2,224,128]{2,1,0:T(8,128)(2,1)S(1)} %get-tuple-element.43.refs_10_), channel_id=1, source_target_pairs={{0,31},{1,2},{2,1},{3,4},{4,3},{5,6},{6,5},{7,8},{8,7},{9,10},{10,... | collective-permute-start | bytes 344072 | tf_op jit(solution)/shard_map/ppermute | solution.py:608
  14.6 21.0 %copy-start.15 = (f32[128,128]{1,0:T(8,128)}, f32[128,128]{1,0:T(8,128)S(1)}, u32[]{:S(2)}) copy-start(f32[128,128]{1,0:T(8,128)S(1)} %collective-permute-done.2.ze) | copy-start | bytes 196612
  14.6 11.0 %collective-permute-start.3 = (f32[128,128]{1,0:T(8,128)S(1)}, f32[128,128]{1,0:T(8,128)S(1)}, u32[]{:S(2)}, u32[]{:S(2)}) collective-permute-start(f32[128,128]{1,0:T(8,128)S(1)} %get-tuple-element.35), channel_id=1, source_target_pairs={{0,96},{32,64},{64,32},{96,0},{1,97},{33,65},{65,33},{97,1},{2,98}... | collective-permute-start | bytes 196616 | tf_op jit(solution)/shard_map/ppermute | solution.py:608
  15.4 18.3 %all-to-all-start = ((f32[128,1,128]{2,1,0:T(1,128)}), f32[128,1,128]{2,1,0:T(1,128)S(1)}, u32[]{:S(2)}, u32[]{:S(2)}) async-start(f32[128,1,128]{2,1,0:T(1,128)} %bitcast.3), calls=%async_computation | async-start | bytes 131072 | tf_op jit(solution)/shard_map/all_to_all | solution.py:629
  35.7 28.6 %all-to-all-start.1 = ((bf16[128,48,128]{2,1,0:T(8,128)(2,1)}), bf16[128,48,128]{2,1,0:T(8,128)(2,1)S(1)}, u32[]{:S(2)}, u32[]{:S(2)}) async-start(bf16[128,48,128]{2,1,0:T(8,128)(2,1)} %send.1), calls=%async_computation.1 | async-start | bytes 3145728 | tf_op jit(solution)/shard_map/all_to_all | solution.py:664
  44.4 13.1 %collective-permute-start.6 = (f32[128,128]{1,0:T(8,128)}, f32[128,128]{1,0:T(8,128)S(1)}, u32[]{:S(2)}, u32[]{:S(2)}) collective-permute-start(f32[128,128]{1,0:T(8,128)} %get-tuple-element.39), channel_id=1, source_target_pairs={{0,32},{32,0},{64,96},{96,64},{1,33},{33,1},{65,97},{97,65},{2,34}... | collective-permute-start | bytes 196616 | tf_op jit(solution)/shard_map/ppermute | solution.py:608
  44.5 18.9 %collective-permute-start.7 = (f32[128,128]{1,0:T(8,128)}, f32[128,128]{1,0:T(8,128)S(1)}, u32[]{:S(2)}, u32[]{:S(2)}) collective-permute-start(f32[128,128]{1,0:T(8,128)} %get-tuple-element.40), channel_id=1, source_target_pairs={{0,96},{32,64},{64,32},{96,0},{1,97},{33,65},{65,33},{97,1},{2,98}... | collective-permute-start | bytes 196616 | tf_op jit(solution)/shard_map/ppermute | solution.py:608
  45.6 27.6 %collective-permute-start.4 = (bf16[5,128,128]{2,1,0:T(8,128)(2,1)}, bf16[5,128,128]{2,1,0:T(8,128)(2,1)S(1)}, u32[]{:S(2)}, u32[]{:S(2)}) collective-permute-start(bf16[5,128,128]{2,1,0:T(8,128)(2,1)} %get-tuple-element.37), channel_id=1, source_target_pairs={{0,1},{1,0},{2,3},{3,2},{4,5},{5,4},{6,7},{7,6},{8,9},{9,8},{10,11... | collective-permute-start | bytes 491528 | tf_op jit(solution)/shard_map/ppermute | solution.py:608
  47.1 26.2 %collective-permute-start.5 = (bf16[5,128,128]{2,1,0:T(8,128)(2,1)}, bf16[5,128,128]{2,1,0:T(8,128)(2,1)S(1)}, u32[]{:S(2)}, u32[]{:S(2)}) collective-permute-start(bf16[5,128,128]{2,1,0:T(8,128)(2,1)} %get-tuple-element.38), channel_id=1, source_target_pairs={{0,31},{1,2},{2,1},{3,4},{4,3},{5,6},{6,5},{7,8},{8,7},{9,10},{10,... | collective-permute-start | bytes 491528 | tf_op jit(solution)/shard_map/ppermute | solution.py:608
  64.2 11.8 %copy-start.8 = (bf16[512,512]{1,0:T(8,128)(2,1)S(1)}, bf16[512,512]{1,0:T(8,128)(2,1)}, u32[]{:S(2)}) copy-start(bf16[512,512]{1,0:T(8,128)(2,1)} %dy.3) | copy-start | bytes 1572868
  64.3 11.8 %copy-start.9 = (bf16[512,512]{1,0:T(8,128)(2,1)S(1)}, bf16[512,512]{1,0:T(8,128)(2,1)}, u32[]{:S(2)}) copy-start(bf16[512,512]{1,0:T(8,128)(2,1)} %dz.3) | copy-start | bytes 1572868
  64.3 11.8 %copy-start.11 = (bf16[512,256]{1,0:T(8,128)(2,1)S(1)}, bf16[512,256]{1,0:T(8,128)(2,1)}, u32[]{:S(2)}) copy-start(bf16[512,256]{1,0:T(8,128)(2,1)} %get-tuple-element.47.refs_1_.esrc) | copy-start | bytes 786436
  64.3 11.8 %copy-start.12 = (bf16[256,512]{1,0:T(8,128)(2,1)S(1)}, bf16[256,512]{1,0:T(8,128)(2,1)}, u32[]{:S(2)}) copy-start(bf16[256,512]{1,0:T(8,128)(2,1)} %get-tuple-element.48.refs_3_.edst) | copy-start | bytes 786436
  66.4 12.2 %collective-permute-start.10 = (bf16[2,224,128]{2,1,0:T(8,128)(2,1)S(1)}, bf16[2,224,128]{2,1,0:T(8,128)(2,1)S(1)}, u32[]{:S(2)}, u32[]{:S(2)}) collective-permute-start(bf16[2,224,128]{2,1,0:T(8,128)(2,1)S(1)} %get-tuple-element.54.r_2_), channel_id=1, source_target_pairs={{0,1},{1,0},{2,3},{3,2},{4,5},{5,4},{6,7},{7,6},{8,9},{9,8},{10,11... | collective-permute-start | bytes 344072 | tf_op jit(solution)/shard_map/ppermute | solution.py:608
  67.1 11.6 %collective-permute-start.11 = (bf16[2,224,128]{2,1,0:T(8,128)(2,1)S(1)}, bf16[2,224,128]{2,1,0:T(8,128)(2,1)S(1)}, u32[]{:S(2)}, u32[]{:S(2)}) collective-permute-start(bf16[2,224,128]{2,1,0:T(8,128)(2,1)S(1)} %get-tuple-element.55.r_3_), channel_id=1, source_target_pairs={{0,31},{1,2},{2,1},{3,4},{4,3},{5,6},{6,5},{7,8},{8,7},{9,10},{10,... | collective-permute-start | bytes 344072 | tf_op jit(solution)/shard_map/ppermute | solution.py:608
  79.2 9.0 %collective-permute-start.12 = (bf16[2,224,128]{2,1,0:T(8,128)(2,1)S(1)}, bf16[2,224,128]{2,1,0:T(8,128)(2,1)S(1)}, u32[]{:S(2)}, u32[]{:S(2)}) collective-permute-start(bf16[2,224,128]{2,1,0:T(8,128)(2,1)S(1)} %get-tuple-element.57.r_2_), channel_id=1, source_target_pairs={{0,1},{1,0},{2,3},{3,2},{4,5},{5,4},{6,7},{7,6},{8,9},{9,8},{10,11... | collective-permute-start | bytes 344072 | tf_op jit(solution)/shard_map/ppermute | solution.py:608
  79.3 10.7 %collective-permute-start.13 = (bf16[2,224,128]{2,1,0:T(8,128)(2,1)S(1)}, bf16[2,224,128]{2,1,0:T(8,128)(2,1)S(1)}, u32[]{:S(2)}, u32[]{:S(2)}) collective-permute-start(bf16[2,224,128]{2,1,0:T(8,128)(2,1)S(1)} %get-tuple-element.58.r_3_), channel_id=1, source_target_pairs={{0,31},{1,2},{2,1},{3,4},{4,3},{5,6},{6,5},{7,8},{8,7},{9,10},{10,... | collective-permute-start | bytes 344072 | tf_op jit(solution)/shard_map/ppermute | solution.py:608
  (15 other events, 69.9 us)

commit v7 on v6

--- a/solution.py
+++ b/solution.py
@@ -96,26 +96,21 @@
     return pltpu.roll(f, step % f.shape[1], 1)
 
 
-def put_lane(acc, lane, f, source, target):
-    return jnp.where(lane == target, roll_z(f, target - source), acc)
-
-
 def diff_y(f):
     return roll_y(f, -1) - roll_y(f, 1)
 
 
 def diff_z(f, lane, below, above, slot):
-    up = jnp.where(lane == 127, roll_z(above, 127 - slot), roll_z(f, -1))
-    down = jnp.where(lane == 0, roll_z(below, -slot), roll_z(f, 1))
+    up = jnp.where(lane == 127, roll_z(above, 126 - 2 * slot), roll_z(f, -1))
+    down = jnp.where(lane == 0, roll_z(below, -2 * slot), roll_z(f, 1))
     return up - down
 
 
-def add_columns(x, fields, lane, lo, hi):
+def add_columns(x, fields, lane, pack):
     for f, field in enumerate(fields):
         slot = f * 4 + x
-        lo = put_lane(lo, lane, field, 0, slot)
-        hi = put_lane(hi, lane, field, 127, slot)
-    return lo, hi
+        pack = jnp.where(lane // 2 == slot, roll_z(field, 2 * slot + 1), pack)
+    return pack
 
 
 def pair_lanes(tiles, upper):
@@ -151,7 +146,7 @@
         (u.at[:, jnp.where(even, 0, 3)], uo),
     )
     lane = iota((128, 128), 1)
-    lo = hi = jnp.zeros((128, 128), F32)
+    pack = jnp.zeros((128, 128), F32)
     eye = iota((128, 128), 0) == lane
     place = jnp.where(iota((512, 128), 0) // 128 == iota((512, 128), 1), 1.0, 0.0).astype(BF16)
     finish(ask)
@@ -162,10 +157,9 @@
         copies[x].wait()
         rows = [planes[x, f] for f in range(5)]
         v, p = primitives(rows)
-        lo, hi = add_columns(x, flux(rows, v, p, 2) + [v[0], v[1]], lane, lo, hi)
-    even = is_even("solver")
-    ze[...] = jnp.where(even, hi, lo)
-    zo[...] = jnp.where(even, lo, hi)
+        pack = add_columns(x, flux(rows, v, p, 2) + [v[0], v[1]], lane, pack)
+    ze[...] = pack
+    zo[...] = pack
     finish(copies[4:6])
     store_traces(
         [ends[0, v].astype(F32) for v in range(4)],
@@ -262,7 +256,7 @@
     finish(fetch)
     fill_flux_a([(x, [halo[i, f] for f in range(5)]) for i, x in enumerate((-1, 4))], fa)
     below, above = zhalo[0], zhalo[1]
-    lo = hi = jnp.zeros((128, 128), F32)
+    pack = jnp.zeros((128, 128), F32)
     copies = []
     for i, x in enumerate((0, 3, 1, 2)):
         rows, out = tendency_plane(
@@ -281,11 +275,10 @@
             for f in range(5):
                 edge[i, f] = (-FLOW_STEP * out[f]).astype(BF16)
         v, p = primitives(now)
-        lo, hi = add_columns(x, flux(now, v, p, 2), lane, lo, hi)
-    zpack[0] = lo
-    zpack[1] = hi
+        pack = add_columns(x, flux(now, v, p, 2), lane, pack)
+    zpack[...] = pack
     copies += begin(
-        sems, 4, (edge.at[e], ce), (edge.at[o], co), (zpack.at[ez], ye), (zpack.at[oz], yo)
+        sems, 4, (edge.at[e], ce), (edge.at[o], co), (zpack, ye), (zpack, yo)
     )
     finish(copies)
 
@@ -336,8 +329,8 @@
             outer[x] = flux(rows, v, p, 0)
         for f in range(5):
             slot = f * 4 + x
-            extra = jnp.where(lane == 127, roll_z(above, 127 - slot), 0.0)
-            extra = extra - jnp.where(lane == 0, roll_z(below, -slot), 0.0)
+            extra = jnp.where(lane == 127, roll_z(above, 126 - 2 * slot), 0.0)
+            extra = extra - jnp.where(lane == 0, roll_z(below, -2 * slot), 0.0)
             if x == 0:
                 extra = extra - outer[x][f]
             if x == 3:
@@ -672,7 +665,7 @@
             keep(5, 6, 128, 128),
             keep(4, 5, 128, 128),
             keep_half(2, 5, 128, 128),
-            keep(2, 128, 128),
+            keep(128, 128),
             keep(2, 5, 128, 128),
             keep(2, 128, 128),
             dma(12),

time: 91.8 us -> 91.4 us (level)
  no operation moved by 1% of the time
where the time goes in v7:
time: 91.4 us; the launch traced here: 91.1 us
  starting transfers between devices  47.6 us (52%)
  Pallas kernels  32.9 us (36%)
  waiting for transfers between devices  7.98 us (9%)
  local copies, waits for them, and re-layouts  1.41 us (2%)
  between operations  1.26 us (1%)
    ppermute x14, starting transfers between devices, swap(): return (lax.ppermute(even, axis, by_even), lax.ppermute(odd, axis, by_odd))  33.8 us
    pallas_call x13, Pallas kernels, call(): pl.pallas_call(body, out_shape=outs if many else outs[0], in_specs=[space...  32.9 us
    all_to_all x1, starting transfers between devices, local(): lax.all_to_all(wanted.reshape(128, 1, 128), both, split_axis=0, concat_ax...  9.11 us
    all_to_all x1, starting transfers between devices, local(): got = lax.all_to_all(send, both, split_axis=0, concat_axis=0, tiled=True)  4.67 us
    all_to_all x1, waiting for transfers between devices, local(): lax.all_to_all(wanted.reshape(128, 1, 128), both, split_axis=0, concat_ax...  4.09 us
    ppermute x14, waiting for transfers between devices, swap(): return (lax.ppermute(even, axis, by_even), lax.ppermute(odd, axis, by_odd))  2.89 us
  transfers between devices with their start and end apart: 16, of which 4 were waited for; matrix products, arithmetic and copies ran while one was open for 0% of the time, Pallas kernels for 29%

profile of v7, /device:TPU:0, one launch (start us, length us, event | category | flops | bytes accessed | tf_op | source)
XLA Modules:
  0.0 91.1 jit_solution(3197482725452784821)
XLA Ops:
  0.6 2.7 %edges.1 = (f32[5,128,128]{2,1,0:T(8,128)S(1)}, f32[5,128,128]{2,1,0:T(8,128)S(1)}, f32[128,128]{1,0:T(8,128)S(1)}, f32[128,128]{1,0:T(8,128)S(1)}, bf16[2,224,1...) custom-call(f32[5,4,128,128]{3,2,1,0:T(8,128)} %u.7, bf16[4,224,512]{2,1,0:T(8,128)(2,1)} %q0.3, ...), custom_call_target="tpu_custom_call" | custom-call | tf_op jit(solution)/shard_map/edges/pallas_call | solution.py:41
  3.4 1.7 %collective-permute-start = (f32[5,128,128]{2,1,0:T(8,128)S(1)}, f32[5,128,128]{2,1,0:T(8,128)S(1)}, u32[]{:S(2)}, u32[]{:S(2)}) collective-permute-start(f32[5,128,128]{2,1,0:T(8,128)S(1)} %get-tuple-element.32), channel_id=1, source_target_pairs={{0,1},{1,0},{2,3},{3,2},{4,5},{5,4},{6,7},{7,6},{8,9},{9,8},{10,11... | collective-permute-start | bytes 983048 | tf_op jit(solution)/shard_map/ppermute | solution.py:601
  5.0 7.9 %collective-permute-start.1 = (f32[5,128,128]{2,1,0:T(8,128)S(1)}, f32[5,128,128]{2,1,0:T(8,128)S(1)}, u32[]{:S(2)}, u32[]{:S(2)}) collective-permute-start(f32[5,128,128]{2,1,0:T(8,128)S(1)} %get-tuple-element.33), channel_id=1, source_target_pairs={{0,31},{1,2},{2,1},{3,4},{4,3},{5,6},{6,5},{7,8},{8,7},{9,10},{10,... | collective-permute-start | bytes 983048 | tf_op jit(solution)/shard_map/ppermute | solution.py:601
  12.9 1.2 %collective-permute-start.9 = (bf16[2,224,128]{2,1,0:T(8,128)(2,1)S(1)}, bf16[2,224,128]{2,1,0:T(8,128)(2,1)S(1)}, u32[]{:S(2)}, u32[]{:S(2)}) collective-permute-start(bf16[2,224,128]{2,1,0:T(8,128)(2,1)S(1)} %get-tuple-element.43.refs_10_), channel_id=1, source_target_pairs={{0,31},{1,2},{2,1},{3,4},{4,3},{5,6},{6,5},{7,8},{8,7},{9,10},{10,... | collective-permute-start | bytes 344072 | tf_op jit(solution)/shard_map/ppermute | solution.py:601
  14.9 9.1 %all-to-all-start = ((f32[128,1,128]{2,1,0:T(1,128)}), f32[128,1,128]{2,1,0:T(1,128)S(1)}, u32[]{:S(2)}, u32[]{:S(2)}) async-start(f32[128,1,128]{2,1,0:T(1,128)} %bitcast.3), calls=%async_computation | async-start | bytes 131072 | tf_op jit(solution)/shard_map/all_to_all | solution.py:622
  26.2 2.9 %prepare.1 = (bf16[224,896]{1,0:T(8,128)(2,1)}, bf16[224,448]{1,0:T(8,128)(2,1)}, bf16[224,448]{1,0:T(8,128)(2,1)}, bf16[512,256]{1,0:T(8,128)(2,1)}, bf16[256,512]{1,0:T(8,128)(2,1)}, /*index=5*/f32[224,128]{1,0:T(8,128)}) custom-call(s32[6,224]{1,0:T(8,128)} %nb_far.1, s32[1,224]{1,0:T(1,128)} %bitcast.10, f32[5,128,128]{2,1,0:T(8,128)} %copy-done.5), custom_call_target="tpu_custom_call" | custom-call | tf_op jit(solution)/shard_map/prepare/pallas_call | solution.py:41
  29.1 4.1 %all-to-all-done = f32[128,1,128]{2,1,0:T(1,128)S(1)} async-done(((f32[128,1,128]{2,1,0:T(1,128)}), f32[128,1,128]{2,1,0:T(1,128)S(1)}, u32[]{:S(2)}, u32[]{:S(2)}) %all-to-all-start) | async-done | bytes 65568 | tf_op jit(solution)/shard_map/all_to_all | solution.py:622
  33.2 1.9 %send.1 = bf16[128,48,128]{2,1,0:T(8,128)(2,1)} custom-call(f32[128,128]{1,0:T(8,128)S(1)} %bitcast.8, bf16[128,768]{1,0:T(8,128)(2,1)S(1)} %lamb.1.table, bf16[224,896]{1,0:T(8,128)(2,1)} %get-tuple-element.45._.refs_2_.gcat), custom_call_target="tpu_custom_call" | custom-call | tf_op jit(solution)/shard_map/send/pallas_call | solution.py:41
  35.2 4.7 %all-to-all-start.1 = ((bf16[128,48,128]{2,1,0:T(8,128)(2,1)}), bf16[128,48,128]{2,1,0:T(8,128)(2,1)S(1)}, u32[]{:S(2)}, u32[]{:S(2)}) async-start(bf16[128,48,128]{2,1,0:T(8,128)(2,1)} %send.1), calls=%async_computation.1 | async-start | bytes 3145728 | tf_op jit(solution)/shard_map/all_to_all | solution.py:657
  39.9 3.9 %flow_one.1 = (f32[5,4,128,128]{3,2,1,0:T(8,128)}, bf16[5,128,128]{2,1,0:T(8,128)(2,1)}, bf16[5,128,128]{2,1,0:T(8,128)(2,1)}, f32[128,128]{1,0:T(8,128)}, f32[128,128]{1,0:T(8,128)}) custom-call(f32[5,4,128,128]{3,2,1,0:T(8,128)S(1)} %copy-done, f32[5,128,128]{2,1,0:T(8,128)} %copy-done.5, f32[5,128,128]{2,1,0:T(8,128)} %copy-done.10, ...), custom_call_target="tpu_custom_call" | custom-call | tf_op jit(solution)/shard_map/flow_one/pallas_call | solution.py:41
  43.8 1.2 %collective-permute-start.7 = (f32[128,128]{1,0:T(8,128)}, f32[128,128]{1,0:T(8,128)S(1)}, u32[]{:S(2)}, u32[]{:S(2)}) collective-permute-start(f32[128,128]{1,0:T(8,128)} %get-tuple-element.40), channel_id=1, source_target_pairs={{0,96},{32,64},{64,32},{96,0},{1,97},{33,65},{65,33},{97,1},{2,98}... | collective-permute-start | bytes 196616 | tf_op jit(solution)/shard_map/ppermute | solution.py:601
  45.0 1.5 %collective-permute-start.4 = (bf16[5,128,128]{2,1,0:T(8,128)(2,1)}, bf16[5,128,128]{2,1,0:T(8,128)(2,1)S(1)}, u32[]{:S(2)}, u32[]{:S(2)}) collective-permute-start(bf16[5,128,128]{2,1,0:T(8,128)(2,1)} %get-tuple-element.37), channel_id=1, source_target_pairs={{0,1},{1,0},{2,3},{3,2},{4,5},{5,4},{6,7},{7,6},{8,9},{9,8},{10,11... | collective-permute-start | bytes 491528 | tf_op jit(solution)/shard_map/ppermute | solution.py:601
  46.5 7.0 %collective-permute-start.5 = (bf16[5,128,128]{2,1,0:T(8,128)(2,1)}, bf16[5,128,128]{2,1,0:T(8,128)(2,1)S(1)}, u32[]{:S(2)}, u32[]{:S(2)}) collective-permute-start(bf16[5,128,128]{2,1,0:T(8,128)(2,1)} %get-tuple-element.38), channel_id=1, source_target_pairs={{0,31},{1,2},{2,1},{3,4},{4,3},{5,6},{6,5},{7,8},{8,7},{9,10},{10,... | collective-permute-start | bytes 491528 | tf_op jit(solution)/shard_map/ppermute | solution.py:601
  53.6 1.3 %copy-done.6 = f32[5,4,128,128]{3,2,1,0:T(8,128)S(1)} copy-done((f32[5,4,128,128]{3,2,1,0:T(8,128)S(1)}, f32[5,4,128,128]{3,2,1,0:T(8,128)}, u32[]{:S(2)}) %copy-start.6) | copy-done | bytes 1310744
  54.9 2.0 %flow_inner.1.__.part = f32[5,4,128,128]{3,2,1,0:T(8,128)} custom-call(f32[5,4,128,128]{3,2,1,0:T(8,128)S(1)} %copy-done, f32[5,4,128,128]{3,2,1,0:T(8,128)S(1)} %copy-done.6), custom_call_target="tpu_custom_call" | custom-call | tf_op jit(solution)/shard_map/flow_inner/pallas_call | solution.py:41
  56.9 5.9 %sound_zero.1.part.start = f32[4,224,512]{2,1,0:T(8,128)} custom-call(bf16[4,224,512]{2,1,0:T(8,128)(2,1)} %q0.3, bf16[512,256]{1,0:T(8,128)(2,1)} %get-tuple-element.47.refs_1_.esrc, bf16[224,896]{1,0:T(8,128)(2,1)} %get-tuple-element.45._.refs_2_.gcat, bf16[256,512]{1,0:T(8,128)(2,1)} %get-tuple-element.48.refs_3_.edst, bf16[512,512]{1,0:T(8,128)(2,1)} %dx.3, ...), custom_call_target="tpu_custom_call" | custom-call | tf_op jit(solution)/shard_map/sound_zero/pallas_call | solution.py:41
  63.8 2.1 %sources.1 = (bf16[3,224,512]{2,1,0:T(8,128)(2,1)S(1)}, bf16[2,224,128]{2,1,0:T(8,128)(2,1)S(1)}, bf16[2,224,128]{2,1,0:T(8,128)(2,1)S(1)}, f32[8,128]{1,0:T(8,128)}) custom-call(bf16[128,48,128]{2,1,0:T(8,128)(2,1)S(1)} %all-to-all-done.1.got, f32[224,128]{1,0:T(8,128)} %get-tuple-element.46.spot, f32[4,224,512]{2,1,0:T(8,128)} %sound_zero.1.part.start, ...), custom_call_target="tpu_custom_call" | custom-call | tf_op jit(solution)/shard_map/sources/pallas_call | solution.py:41
  66.6 6.2 %collective-permute-start.11 = (bf16[2,224,128]{2,1,0:T(8,128)(2,1)S(1)}, bf16[2,224,128]{2,1,0:T(8,128)(2,1)S(1)}, u32[]{:S(2)}, u32[]{:S(2)}) collective-permute-start(bf16[2,224,128]{2,1,0:T(8,128)(2,1)S(1)} %get-tuple-element.55.r_3_), channel_id=1, source_target_pairs={{0,31},{1,2},{2,1},{3,4},{4,3},{5,6},{6,5},{7,8},{8,7},{9,10},{10,... | collective-permute-start | bytes 344072 | tf_op jit(solution)/shard_map/ppermute | solution.py:601
  72.9 2.7 %flow_two.1._ = f32[5,4,128,128]{3,2,1,0:T(8,128)} custom-call(f32[5,4,128,128]{3,2,1,0:T(8,128)S(1)} %copy-done.3, f32[5,128,128]{2,1,0:T(8,128)} %copy-done.5, f32[5,128,128]{2,1,0:T(8,128)} %copy-done.10, bf16[5,128,128]{2,1,0:T(8,128)(2,1)S(1)} %collective-permute-done.4.ce, bf16[5,128,128]{2,1,0:T(8,128)(2,1)S(1)} %collective-permute-done.5.co, ...), custom_call_target="tpu_custom_call" | custom-call | tf_op jit(solution)/shard_map/flow_two/pallas_call | solution.py:41
  75.7 2.5 %sound_one.1.r_6_.mid = f32[4,224,512]{2,1,0:T(8,128)S(1)} custom-call(bf16[4,224,512]{2,1,0:T(8,128)(2,1)S(1)} %copy-done.2, f32[4,224,512]{2,1,0:T(8,128)S(1)} %copy-done.1, bf16[3,224,512]{2,1,0:T(8,128)(2,1)S(1)} %get-tuple-element.56.src, bf16[512,512]{1,0:T(8,128)(2,1)S(1)} %copy-done.7, bf16[512,512]{1,0:T(8,128)(2,1)S(1)} %copy-done.8, ...), custom_call_target="tpu_custom_call" | custom-call | tf_op jit(solution)/shard_map/sound_one/pallas_call | solution.py:41
  78.8 5.6 %collective-permute-start.13 = (bf16[2,224,128]{2,1,0:T(8,128)(2,1)S(1)}, bf16[2,224,128]{2,1,0:T(8,128)(2,1)S(1)}, u32[]{:S(2)}, u32[]{:S(2)}) collective-permute-start(bf16[2,224,128]{2,1,0:T(8,128)(2,1)S(1)} %get-tuple-element.58.r_3_), channel_id=1, source_target_pairs={{0,31},{1,2},{2,1},{3,4},{4,3},{5,6},{6,5},{7,8},{8,7},{9,10},{10,... | collective-permute-start | bytes 344072 | tf_op jit(solution)/shard_map/ppermute | solution.py:601
  84.4 3.4 %sound_two.1 = (f32[4,224,512]{2,1,0:T(8,128)}, f32[2,4,224,128]{3,2,1,0:T(8,128)S(1)}) custom-call(bf16[4,224,512]{2,1,0:T(8,128)(2,1)S(1)} %copy-done.2, f32[4,224,512]{2,1,0:T(8,128)S(1)} %sound_one.1.r_6_.mid, f32[2,4,224,128]{3,2,1,0:T(8,128)S(1)} %get-tuple-element.59.ends, bf16[3,224,512]{2,1,0:T(8,128)(2,1)S(1)} %get-tuple-element.56.src, ...), custom_call_target="tpu_custom_call" | custom-call | tf_op jit(solution)/shard_map/sound_two/pallas_call | solution.py:41
  87.8 1.7 %collective-permute-done.13.r_5_ = bf16[2,224,128]{2,1,0:T(8,128)(2,1)S(1)} collective-permute-done((bf16[2,224,128]{2,1,0:T(8,128)(2,1)S(1)}, bf16[2,224,128]{2,1,0:T(8,128)(2,1)S(1)}, u32[]{:S(2)}, u32[]{:S(2)}) %collective-permute-start.13) | collective-permute-done | bytes 114720 | tf_op jit(solution)/shard_map/ppermute | solution.py:601
  89.5 1.4 %cross_two.1 = f32[4,224,512]{2,1,0:T(8,128)} custom-call(bf16[224,448]{1,0:T(8,128)(2,1)S(1)} %copy-done.13, bf16[224,448]{1,0:T(8,128)(2,1)S(1)} %copy-done.14, bf16[2,224,128]{2,1,0:T(8,128)(2,1)S(1)} %get-tuple-element.57.r_2_, bf16[2,224,128]{2,1,0:T(8,128)(2,1)S(1)} %get-tuple-element.58.r_3_, ...), custom_call_target="tpu_custom_call", output_to_operand_aliasing={{}: (7, {})} | custom-call | tf_op jit(solution)/shard_map/cross_two/pallas_call | solution.py:41
  (67 shorter events, 5.4 us)
Async XLA Ops:
  0.6 24.5 %copy-start = (f32[5,4,128,128]{3,2,1,0:T(8,128)S(1)}, f32[5,4,128,128]{3,2,1,0:T(8,128)}, u32[]{:S(2)}) copy-start(f32[5,4,128,128]{3,2,1,0:T(8,128)} %u.7) | copy-start | bytes 3932164
  3.3 31.8 %copy-start.17 = (bf16[2,224,128]{2,1,0:T(8,128)(2,1)}, bf16[2,224,128]{2,1,0:T(8,128)(2,1)S(1)}, u32[]{:S(2)}) copy-start(bf16[2,224,128]{2,1,0:T(8,128)(2,1)S(1)} %get-tuple-element.42.refs_9_) | copy-start | bytes 344068
  3.4 31.8 %copy-start.18 = (bf16[2,224,128]{2,1,0:T(8,128)(2,1)}, bf16[2,224,128]{2,1,0:T(8,128)(2,1)S(1)}, u32[]{:S(2)}) copy-start(bf16[2,224,128]{2,1,0:T(8,128)(2,1)S(1)} %get-tuple-element.43.refs_10_) | copy-start | bytes 344068
  3.4 21.7 %collective-permute-start = (f32[5,128,128]{2,1,0:T(8,128)S(1)}, f32[5,128,128]{2,1,0:T(8,128)S(1)}, u32[]{:S(2)}, u32[]{:S(2)}) collective-permute-start(f32[5,128,128]{2,1,0:T(8,128)S(1)} %get-tuple-element.32), channel_id=1, source_target_pairs={{0,1},{1,0},{2,3},{3,2},{4,5},{5,4},{6,7},{7,6},{8,9},{9,8},{10,11... | collective-permute-start | bytes 983048 | tf_op jit(solution)/shard_map/ppermute | solution.py:601
  5.0 20.1 %collective-permute-start.1 = (f32[5,128,128]{2,1,0:T(8,128)S(1)}, f32[5,128,128]{2,1,0:T(8,128)S(1)}, u32[]{:S(2)}, u32[]{:S(2)}) collective-permute-start(f32[5,128,128]{2,1,0:T(8,128)S(1)} %get-tuple-element.33), channel_id=1, source_target_pairs={{0,31},{1,2},{2,1},{3,4},{4,3},{5,6},{6,5},{7,8},{8,7},{9,10},{10,... | collective-permute-start | bytes 983048 | tf_op jit(solution)/shard_map/ppermute | solution.py:601
  12.9 1.3 %collective-permute-start.2 = (f32[128,128]{1,0:T(8,128)S(1)}, f32[128,128]{1,0:T(8,128)S(1)}, u32[]{:S(2)}, u32[]{:S(2)}) collective-permute-start(f32[128,128]{1,0:T(8,128)S(1)} %get-tuple-element.34), channel_id=1, source_target_pairs={{0,32},{32,0},{64,96},{96,64},{1,33},{33,1},{65,97},{97,65},{2,34}... | collective-permute-start | bytes 196616 | tf_op jit(solution)/shard_map/ppermute | solution.py:601
  12.9 13.3 %collective-permute-start.8 = (bf16[2,224,128]{2,1,0:T(8,128)(2,1)S(1)}, bf16[2,224,128]{2,1,0:T(8,128)(2,1)S(1)}, u32[]{:S(2)}, u32[]{:S(2)}) collective-permute-start(bf16[2,224,128]{2,1,0:T(8,128)(2,1)S(1)} %get-tuple-element.42.refs_9_), channel_id=1, source_target_pairs={{0,1},{1,0},{2,3},{3,2},{4,5},{5,4},{6,7},{7,6},{8,9},{9,8},{10,11... | collective-permute-start | bytes 344072 | tf_op jit(solution)/shard_map/ppermute | solution.py:601
  12.9 13.3 %collective-permute-start.9 = (bf16[2,224,128]{2,1,0:T(8,128)(2,1)S(1)}, bf16[2,224,128]{2,1,0:T(8,128)(2,1)S(1)}, u32[]{:S(2)}, u32[]{:S(2)}) collective-permute-start(bf16[2,224,128]{2,1,0:T(8,128)(2,1)S(1)} %get-tuple-element.43.refs_10_), channel_id=1, source_target_pairs={{0,31},{1,2},{2,1},{3,4},{4,3},{5,6},{6,5},{7,8},{8,7},{9,10},{10,... | collective-permute-start | bytes 344072 | tf_op jit(solution)/shard_map/ppermute | solution.py:601
  14.1 21.0 %copy-start.15 = (f32[128,128]{1,0:T(8,128)}, f32[128,128]{1,0:T(8,128)S(1)}, u32[]{:S(2)}) copy-start(f32[128,128]{1,0:T(8,128)S(1)} %collective-permute-done.2.ze) | copy-start | bytes 196612
  14.1 11.0 %collective-permute-start.3 = (f32[128,128]{1,0:T(8,128)S(1)}, f32[128,128]{1,0:T(8,128)S(1)}, u32[]{:S(2)}, u32[]{:S(2)}) collective-permute-start(f32[128,128]{1,0:T(8,128)S(1)} %get-tuple-element.35), channel_id=1, source_target_pairs={{0,96},{32,64},{64,32},{96,0},{1,97},{33,65},{65,33},{97,1},{2,98}... | collective-permute-start | bytes 196616 | tf_op jit(solution)/shard_map/ppermute | solution.py:601
  14.9 18.3 %all-to-all-start = ((f32[128,1,128]{2,1,0:T(1,128)}), f32[128,1,128]{2,1,0:T(1,128)S(1)}, u32[]{:S(2)}, u32[]{:S(2)}) async-start(f32[128,1,128]{2,1,0:T(1,128)} %bitcast.3), calls=%async_computation | async-start | bytes 131072 | tf_op jit(solution)/shard_map/all_to_all | solution.py:622
  35.2 28.6 %all-to-all-start.1 = ((bf16[128,48,128]{2,1,0:T(8,128)(2,1)}), bf16[128,48,128]{2,1,0:T(8,128)(2,1)S(1)}, u32[]{:S(2)}, u32[]{:S(2)}) async-start(bf16[128,48,128]{2,1,0:T(8,128)(2,1)} %send.1), calls=%async_computation.1 | async-start | bytes 3145728 | tf_op jit(solution)/shard_map/all_to_all | solution.py:657
  43.7 13.1 %collective-permute-start.6 = (f32[128,128]{1,0:T(8,128)}, f32[128,128]{1,0:T(8,128)S(1)}, u32[]{:S(2)}, u32[]{:S(2)}) collective-permute-start(f32[128,128]{1,0:T(8,128)} %get-tuple-element.39), channel_id=1, source_target_pairs={{0,32},{32,0},{64,96},{96,64},{1,33},{33,1},{65,97},{97,65},{2,34}... | collective-permute-start | bytes 196616 | tf_op jit(solution)/shard_map/ppermute | solution.py:601
  43.8 18.9 %collective-permute-start.7 = (f32[128,128]{1,0:T(8,128)}, f32[128,128]{1,0:T(8,128)S(1)}, u32[]{:S(2)}, u32[]{:S(2)}) collective-permute-start(f32[128,128]{1,0:T(8,128)} %get-tuple-element.40), channel_id=1, source_target_pairs={{0,96},{32,64},{64,32},{96,0},{1,97},{33,65},{65,33},{97,1},{2,98}... | collective-permute-start | bytes 196616 | tf_op jit(solution)/shard_map/ppermute | solution.py:601
  45.0 27.8 %collective-permute-start.4 = (bf16[5,128,128]{2,1,0:T(8,128)(2,1)}, bf16[5,128,128]{2,1,0:T(8,128)(2,1)S(1)}, u32[]{:S(2)}, u32[]{:S(2)}) collective-permute-start(bf16[5,128,128]{2,1,0:T(8,128)(2,1)} %get-tuple-element.37), channel_id=1, source_target_pairs={{0,1},{1,0},{2,3},{3,2},{4,5},{5,4},{6,7},{7,6},{8,9},{9,8},{10,11... | collective-permute-start | bytes 491528 | tf_op jit(solution)/shard_map/ppermute | solution.py:601
  46.5 26.3 %collective-permute-start.5 = (bf16[5,128,128]{2,1,0:T(8,128)(2,1)}, bf16[5,128,128]{2,1,0:T(8,128)(2,1)S(1)}, u32[]{:S(2)}, u32[]{:S(2)}) collective-permute-start(bf16[5,128,128]{2,1,0:T(8,128)(2,1)} %get-tuple-element.38), channel_id=1, source_target_pairs={{0,31},{1,2},{2,1},{3,4},{4,3},{5,6},{6,5},{7,8},{8,7},{9,10},{10,... | collective-permute-start | bytes 491528 | tf_op jit(solution)/shard_map/ppermute | solution.py:601
  63.8 11.8 %copy-start.8 = (bf16[512,512]{1,0:T(8,128)(2,1)S(1)}, bf16[512,512]{1,0:T(8,128)(2,1)}, u32[]{:S(2)}) copy-start(bf16[512,512]{1,0:T(8,128)(2,1)} %dy.3) | copy-start | bytes 1572868
  63.8 11.8 %copy-start.9 = (bf16[512,512]{1,0:T(8,128)(2,1)S(1)}, bf16[512,512]{1,0:T(8,128)(2,1)}, u32[]{:S(2)}) copy-start(bf16[512,512]{1,0:T(8,128)(2,1)} %dz.3) | copy-start | bytes 1572868
  63.8 11.8 %copy-start.11 = (bf16[512,256]{1,0:T(8,128)(2,1)S(1)}, bf16[512,256]{1,0:T(8,128)(2,1)}, u32[]{:S(2)}) copy-start(bf16[512,256]{1,0:T(8,128)(2,1)} %get-tuple-element.47.refs_1_.esrc) | copy-start | bytes 786436
  63.8 11.8 %copy-start.12 = (bf16[256,512]{1,0:T(8,128)(2,1)S(1)}, bf16[256,512]{1,0:T(8,128)(2,1)}, u32[]{:S(2)}) copy-start(bf16[256,512]{1,0:T(8,128)(2,1)} %get-tuple-element.48.refs_3_.edst) | copy-start | bytes 786436
  66.0 12.2 %collective-permute-start.10 = (bf16[2,224,128]{2,1,0:T(8,128)(2,1)S(1)}, bf16[2,224,128]{2,1,0:T(8,128)(2,1)S(1)}, u32[]{:S(2)}, u32[]{:S(2)}) collective-permute-start(bf16[2,224,128]{2,1,0:T(8,128)(2,1)S(1)} %get-tuple-element.54.r_2_), channel_id=1, source_target_pairs={{0,1},{1,0},{2,3},{3,2},{4,5},{5,4},{6,7},{7,6},{8,9},{9,8},{10,11... | collective-permute-start | bytes 344072 | tf_op jit(solution)/shard_map/ppermute | solution.py:601
  66.6 11.6 %collective-permute-start.11 = (bf16[2,224,128]{2,1,0:T(8,128)(2,1)S(1)}, bf16[2,224,128]{2,1,0:T(8,128)(2,1)S(1)}, u32[]{:S(2)}, u32[]{:S(2)}) collective-permute-start(bf16[2,224,128]{2,1,0:T(8,128)(2,1)S(1)} %get-tuple-element.55.r_3_), channel_id=1, source_target_pairs={{0,31},{1,2},{2,1},{3,4},{4,3},{5,6},{6,5},{7,8},{8,7},{9,10},{10,... | collective-permute-start | bytes 344072 | tf_op jit(solution)/shard_map/ppermute | solution.py:601
  78.7 9.0 %collective-permute-start.12 = (bf16[2,224,128]{2,1,0:T(8,128)(2,1)S(1)}, bf16[2,224,128]{2,1,0:T(8,128)(2,1)S(1)}, u32[]{:S(2)}, u32[]{:S(2)}) collective-permute-start(bf16[2,224,128]{2,1,0:T(8,128)(2,1)S(1)} %get-tuple-element.57.r_2_), channel_id=1, source_target_pairs={{0,1},{1,0},{2,3},{3,2},{4,5},{5,4},{6,7},{7,6},{8,9},{9,8},{10,11... | collective-permute-start | bytes 344072 | tf_op jit(solution)/shard_map/ppermute | solution.py:601
  78.8 10.7 %collective-permute-start.13 = (bf16[2,224,128]{2,1,0:T(8,128)(2,1)S(1)}, bf16[2,224,128]{2,1,0:T(8,128)(2,1)S(1)}, u32[]{:S(2)}, u32[]{:S(2)}) collective-permute-start(bf16[2,224,128]{2,1,0:T(8,128)(2,1)S(1)} %get-tuple-element.58.r_3_), channel_id=1, source_target_pairs={{0,31},{1,2},{2,1},{3,4},{4,3},{5,6},{6,5},{7,8},{8,7},{9,10},{10,... | collective-permute-start | bytes 344072 | tf_op jit(solution)/shard_map/ppermute | solution.py:601
  (15 other events, 69.9 us)
